TPU v7x, 32 devices: a whole 2x2x4 slice. The times are simulated.
32 devices in a mesh: lag: 4 (over y, core), row: 8 (over z, x).
Axes of the slice: x: 2, y: 2, z: 4, core: 2. Of those that a mesh axis runs over, the one named last changes fastest.
Arguments:
- lag_ops: float32 [8, 3072, 3072], P('lag', 'row'), may hold values from -0.109375 to 0.109375
- inverse: float32 [3072, 3072], P('row'), may hold values from -0.109375 to 0.109375
- history: float32 [8, 3072, 128], P('lag', 'row'), may hold values from -6 to 6
- loads: float32 [3, 3072, 128], P(None, 'row'), may hold values from -6 to 6
Outputs:
- current: float32 [3072, 128], P('row')
- future: float32 [8, 3072, 128], P('lag', 'row')
All inputs are finite; a program needn't handle non-finite values.
Results may differ from a plain program's by a relative error of at most 0.00011.
Values sent between devices are 32-bit elements; how exact they have to be, the bound alone decides.
No kernel may reach another device: no remote copies, remote signals or barrier semaphores. Data moves between devices by JAX's collectives and lax.ppermute only.
A program may use at most 64 MiB of HBM per device.

v0:
```python
import functools

import jax
import jax.numpy as jnp
from jax import lax
from jax.experimental import pallas as pl
from jax.experimental.pallas import tpu as pltpu
from jax.sharding import PartitionSpec as P


STEPS = 3
AXES = ("lag", "row")


def broadcast(array, axis, root):
    mine = lax.axis_index(axis) == root
    return lax.psum(jnp.where(mine, array, jnp.zeros_like(array)), axis)


def from_behind(array, axis, by):
    length = lax.axis_size(axis)
    pairs = [(i, i + by) for i in range(length) if 0 <= i + by < length]
    return lax.ppermute(array, axis, pairs)


def plain_body(lag_ops, inverse, history, loads):
    acc = history
    local_lags = lag_ops.shape[0]
    local_rows = lag_ops.shape[1]
    total_cols = lag_ops.shape[2]
    loads_width = history.shape[2]
    flat_ops = lag_ops.reshape(local_lags * local_rows, total_cols)
    current = jnp.zeros((local_rows, loads_width), jnp.float32)
    for step in range(STEPS):
        rhs = broadcast(loads[step] - acc[0], "lag", 0)
        width = loads_width // lax.axis_size("lag")
        offset = lax.axis_index("lag") * width
        rhs_part = lax.dynamic_slice_in_dim(rhs, offset, width, 1)
        partial_value = jnp.dot(
            inverse,
            lax.all_gather(rhs_part, "row", axis=0, tiled=True),
            precision=lax.Precision.HIGHEST,
            preferred_element_type=jnp.float32,
        )
        current = lax.all_gather(partial_value, "lag", axis=1, tiled=True)
        product = jnp.dot(
            flat_ops,
            lax.all_gather(current, "row", axis=0, tiled=True),
            precision=lax.Precision.HIGHEST,
            preferred_element_type=jnp.float32,
        )
        product = product.reshape(local_lags, local_rows, loads_width)
        incoming = from_behind(acc[0], "lag", -1)
        shifted = jnp.concatenate([acc[1:], incoming[None]], axis=0)
        acc = shifted + product
    return (current, acc)


def swap(array, lag_bits, row_bits):
    lags, rows = lax.axis_size("lag"), lax.axis_size("row")
    pairs = [
        (g * rows + r, (g ^ lag_bits) * rows + (r ^ row_bits))
        for g in range(lags)
        for r in range(rows)
    ]
    return lax.ppermute(array, AXES, pairs)


def split(array):
    high = lax.reduce_precision(array, 8, 7)
    return high.astype(jnp.bfloat16), (array - high).astype(jnp.bfloat16)


def split_here(array):
    high = array.astype(jnp.bfloat16)
    return high, (array - high.astype(jnp.float32)).astype(jnp.bfloat16)


def contract(a, b):
    return lax.dot_general(
        a, b, (((1,), (1,)), ((), ())), preferred_element_type=jnp.float32
    )


def product(vector, matrix):
    vh, vl = vector
    mh, ml = matrix
    n = vh.shape[0]
    both = contract(jnp.concatenate([vh, vl], 0), mh)
    return both[:n] + both[n:] + contract(vh, ml)


def turn_first_kernel(history_ref, loads_ref, past_ref, rhs_ref):
    past_ref[...] = history_ref[0].T
    rhs_ref[...] = loads_ref[0].T - past_ref[...]


def turn_first(history, loads):
    _, rows, n = history.shape
    spec = pl.BlockSpec((1, rows, n), lambda i: (0, 0, 0))
    shape = jax.ShapeDtypeStruct((n, rows), history.dtype)
    out = pl.BlockSpec((n, rows), lambda i: (0, 0))
    return pl.pallas_call(
        turn_first_kernel,
        out_shape=(shape, shape),
        grid=(1,),
        in_specs=[spec, spec],
        out_specs=(out, out),
        compiler_params=pltpu.CompilerParams(vmem_limit_bytes=8 << 20),
        name="turn_first",
    )(history, loads)


def turn_kernel(history_ref, loads_ref, past_ref, given_ref):
    past_ref[...] = history_ref[1].T
    for i in range(given_ref.shape[0]):
        given_ref[i] = loads_ref[i + 1].T


def turn(history, loads):
    _, rows, n = history.shape
    return pl.pallas_call(
        turn_kernel,
        out_shape=(
            jax.ShapeDtypeStruct((n, rows), history.dtype),
            jax.ShapeDtypeStruct((loads.shape[0] - 1, n, rows), loads.dtype),
        ),
        compiler_params=pltpu.CompilerParams(vmem_limit_bytes=8 << 20),
        name="turn",
    )(history, loads)


def split_kernel(order_ref, m_ref, high_ref, low_ref):
    high_ref[...], low_ref[...] = split_here(m_ref[...])


def split_blocks(matrix, order, size, lag=None):
    rows, cols = matrix.shape[-2:]
    out = jax.ShapeDtypeStruct((rows, cols), jnp.bfloat16)
    spec = pl.BlockSpec((rows, size), lambda i, o: (0, i))
    if lag is None:
        source = pl.BlockSpec((rows, size), lambda i, o: (0, o[i]))
    else:
        source = pl.BlockSpec((None, rows, size), lambda i, o: (lag, 0, o[i]))
    return pl.pallas_call(
        split_kernel,
        out_shape=(out, out),
        grid_spec=pltpu.PrefetchScalarGridSpec(
            num_scalar_prefetch=1,
            grid=(cols // size,),
            in_specs=[source],
            out_specs=(spec, spec),
        ),
        compiler_params=pltpu.CompilerParams(vmem_limit_bytes=8 << 20),
        cost_estimate=pl.CostEstimate(
            flops=0, bytes_accessed=8 * rows * cols, transcendentals=0
        ),
        name="split_blocks",
    )(order, matrix)


VMEM = pl.BlockSpec(memory_space=pltpu.VMEM)


def times(vh, vl, high_ref, low_ref):
    n = vh.shape[0]
    both = contract(high_ref[...], jnp.concatenate([vh, vl], 0))
    return both[:, :n] + both[:, n:] + contract(low_ref[...], vh)


def field_kernel(step, high_ref, low_ref, v_ref, base_ref, *refs):
    total = base_ref[...] + times(*split_here(v_ref[...]), high_ref, low_ref).T
    if len(refs) == 1:
        refs[0][...] = total
    else:
        given_ref, out_ref, rhs_ref = refs
        out_ref[...] = total
        rhs_ref[...] = given_ref[step] - total


def costs(rows, cols, n):
    return pl.CostEstimate(
        flops=6 * rows * cols * n, bytes_accessed=4 * rows * cols, transcendentals=0
    )


def field(op, current, base, loads=None, step=0):
    high, low = op
    n = current.shape[0]
    shape = jax.ShapeDtypeStruct((n, high.shape[0]), jnp.float32)
    inputs = [high, low, current, base] + ([] if loads is None else [loads])
    return pl.pallas_call(
        functools.partial(field_kernel, step),
        out_shape=shape if loads is None else (shape, shape),
        in_specs=[VMEM] * len(inputs),
        out_specs=VMEM if loads is None else (VMEM, VMEM),
        compiler_params=pltpu.CompilerParams(vmem_limit_bytes=8 << 20),
        cost_estimate=costs(*high.shape, n),
        name="field",
    )(*inputs)


def last_kernel(h0_ref, l0_ref, h1_ref, l1_ref, v_ref, b0_ref, b1_ref, current_ref, out_ref):
    rows = current_ref.shape[0]
    vh, vl = split_here(v_ref[...])
    current_ref[...] = v_ref[:, :rows].T
    out_ref[0] = b0_ref[...].T + times(vh, vl, h0_ref, l0_ref)
    out_ref[1] = b1_ref[...].T + times(vh, vl, h1_ref, l1_ref)


def last(op0, op1, current, base0, base1):
    rows, cols = op0[0].shape
    n = current.shape[0]
    return pl.pallas_call(
        last_kernel,
        out_shape=(
            jax.ShapeDtypeStruct((rows, n), jnp.float32),
            jax.ShapeDtypeStruct((2, rows, n), jnp.float32),
        ),
        in_specs=[VMEM] * 7,
        out_specs=(VMEM, VMEM),
        compiler_params=pltpu.CompilerParams(vmem_limit_bytes=8 << 20),
        cost_estimate=costs(2 * rows, cols, n),
        name="last",
    )(*op0, *op1, current, base0, base1)


def quad_body(lag_ops, inverse, history, loads):
    rows_n = lax.axis_size("row")
    height = lag_ops.shape[1]
    width = loads.shape[2] // 4
    g = lax.axis_index("lag")
    r = lax.axis_index("row")
    plane, core = g // 2, g % 2
    near = [k for k in range(0, rows_n, 2)]
    steps = near + [k + 1 for k in near]
    cut = len(near) * height
    order = r ^ jnp.array(steps, jnp.int32)

    def line(v):
        return jnp.concatenate([v] + [swap(v, 0, k) for k in near[1:]], 1)

    def scatter(rhs):
        parts = [rhs[j * width : (j + 1) * width] for j in range(4)]
        got = [parts[0]] + [swap(parts[j], j, 0) for j in (3, 2, 1)][::-1]
        return lax.select_n(g, *got)

    def full(a):
        near_y, far_y, far = swap(a, 2, 0), swap(a, 2, 1), swap(a, 0, 1)
        near_ = jnp.concatenate([a, near_y], 0)
        far_ = jnp.concatenate([far, far_y], 0)
        v = jnp.concatenate([near_, far_], 1)
        w = jnp.concatenate([swap(near_, 1, 0), swap(far_, 1, 0)], 1)
        chunks = [v[:width], w[:width], v[width:], w[width:]]
        even = [jnp.where(core == 0, chunks[j], chunks[j ^ 1]) for j in range(4)]
        return jnp.concatenate(
            [jnp.where(plane == 0, even[j], even[j ^ 2]) for j in range(4)], 0
        )

    def behind(array):
        near_, far = swap(array, 1, 0), swap(array, 3, 0)
        return jnp.where(core == 0, near_, jnp.where(plane == 0, far, 0.0))

    tie = lax.optimization_barrier
    keep = functools.partial(pltpu.with_memory_space_constraint, memory_space=pltpu.HBM)
    acc0, rhs = turn_first(keep(history), keep(loads))
    for step in range(STEPS):
        rhs = scatter(rhs)
        if step == 0:
            rhs, inverse = tie((rhs, inverse))
            high, low = split_blocks(inverse, order, height)
            inv = [(high[:, :cut], low[:, :cut]), (high[:, cut:], low[:, cut:])]
            a = line(rhs)
            a, inv = tie((a, inv))
            a, acc0, ops0, history, loads = tie((a, acc0, lag_ops, history, loads))
            acc1, given = turn(history, loads)
            op0 = split_blocks(ops0, order, height, 0)
            b = swap(a, 0, 1)
            b, acc1, given, op0 = tie((b, acc1, given, op0))
        else:
            a = line(rhs)
            a, acc0, current = tie((a, acc0, current))
            acc1 = field(op1, current, below)
            b = swap(a, 0, 1)
            b, acc1 = tie((b, acc1))
        ahead = behind(acc0)
        solved = product(split(a), inv[0]) + product(split(b), inv[1])
        if step == 0:
            solved, ops1 = tie((solved, lag_ops))
            op1 = split_blocks(ops1, order, height, 1)
        a = line(solved)
        a, op1 = tie((a, op1))
        current = full(a)
        below = ahead
        if step < STEPS - 1:
            acc0, rhs = field(op0, current, acc1, given, step)
    return last(op0, op1, current, acc1, below)


def solution(mesh):
    placed = (P("lag", "row", None), P("row", None), P("lag", "row", None), P(None, "row", None))

    def body(lag_ops, inverse, history, loads):
        lags, rows = lax.axis_size("lag"), lax.axis_size("row")
        fits = (
            lags == 4
            and lag_ops.shape[0] == STEPS - 1
            and rows & (rows - 1) == 0
            and lag_ops.shape[1] * rows == lag_ops.shape[2]
            and loads.shape[0] == STEPS
        )
        return (quad_body if fits else plain_body)(lag_ops, inverse, history, loads)

    return jax.shard_map(
        body,
        mesh=mesh,
        in_specs=placed,
        out_specs=(P("row", None), P("lag", "row", None)),
        check_vma=False,
    )
```

profile of v0, /device:TPU:0, one launch (start us, length us, event | category | flops | bytes accessed | tf_op | source)
XLA Modules:
  0.0 146.5 jit_solution(18222433504414915432)
XLA Ops:
  2.4 2.6 %collective-permute-start.2 = (f32[32,384]{1,0:T(8,128)S(1)}, f32[32,384]{1,0:T(8,128)S(1)}, u32[]{:S(2)}, u32[]{:S(2)}) collective-permute-start(f32[32,384]{1,0:T(8,128)S(1)} %get-tuple-element.147), channel_id=1, source_target_pairs={{0,24},{1,25},{2,26},{3,27},{4,28},{5,29},{6,30},{7,31},{8,16},{9,... | collective-permute-start | bytes 147464 | tf_op jit(solution)/shard_map/ppermute | solution.py:66
  5.1 2.0 %collective-permute-done.2 = f32[32,384]{1,0:T(8,128)S(1)} collective-permute-done((f32[32,384]{1,0:T(8,128)S(1)}, f32[32,384]{1,0:T(8,128)S(1)}, u32[]{:S(2)}, u32[]{:S(2)}) %collective-permute-start.2) | collective-permute-done | bytes 49184 | tf_op jit(solution)/shard_map/ppermute | solution.py:66
  7.1 2.0 %collective-permute-done.1 = f32[32,384]{1,0:T(8,128)S(1)} collective-permute-done((f32[32,384]{1,0:T(8,128)S(1)}, f32[32,384]{1,0:T(8,128)S(1)}, u32[]{:S(2)}, u32[]{:S(2)}) %collective-permute-start.1) | collective-permute-done | bytes 49184 | tf_op jit(solution)/shard_map/ppermute | solution.py:66
  9.1 3.7 %collective-permute-start.5 = (f32[32,384]{1,0:T(8,128)S(1)}, f32[32,384]{1,0:T(8,128)S(1)}, u32[]{:S(2)}, u32[]{:S(2)}) collective-permute-start(f32[32,384]{1,0:T(8,128)S(1)} %select_select_fusion.5), channel_id=1, source_target_pairs={{0,6},{1,7},{2,4},{3,5},{4,2},{5,3},{6,0},{7,1},{8,14},{9,15},{10,... | collective-permute-start | bytes 147464 | tf_op jit(solution)/shard_map/ppermute | solution.py:66
  13.6 2.3 %copy-done.7 = f32[384,3072]{1,0:T(8,128)S(1)} copy-done((f32[384,3072]{1,0:T(8,128)S(1)}, f32[384,3072]{1,0:T(8,128)}, u32[]{:S(2)}) %copy-start.7) | copy-done | bytes 4718616
  15.9 2.7 %split_blocks.3 = (bf16[384,3072]{1,0:T(8,128)(2,1)S(1)}, bf16[384,3072]{1,0:T(8,128)(2,1)S(1)}) custom-call(s32[8]{0:T(128)S(1)} %broadcast_xor_fusion.order_ref, f32[384,3072]{1,0:T(8,128)S(1)} %copy-done.7), custom_call_target="tpu_custom_call" | custom-call | bytes 9437184 | tf_op jit(solution)/shard_map/split_blocks/pallas_call | solution.py:145
  19.2 1.6 %collective-permute-start.6 = (f32[32,1536]{1,0:T(8,128)S(1)}, f32[32,1536]{1,0:T(8,128)S(1)}, u32[]{:S(2)}, u32[]{:S(2)}) collective-permute-start(f32[32,1536]{1,0:T(8,128)S(1)} %pad_maximum_fusion.6), channel_id=1, source_target_pairs={{0,1},{1,0},{2,3},{3,2},{4,5},{5,4},{6,7},{7,6},{8,9},{9,8},{10,11... | collective-permute-start | bytes 589832 | tf_op jit(solution)/shard_map/ppermute | solution.py:66
  20.8 3.2 %copy-done = f32[2,384,3072]{2,1,0:T(8,128)S(1)} copy-done((f32[2,384,3072]{2,1,0:T(8,128)S(1)}, f32[2,384,3072]{2,1,0:T(8,128)}, u32[]{:S(2)}) %copy-start) | copy-done | bytes 9437208
  24.0 2.7 %split_blocks.4 = (bf16[384,3072]{1,0:T(8,128)(2,1)S(1)}, bf16[384,3072]{1,0:T(8,128)(2,1)S(1)}) custom-call(s32[8]{0:T(128)S(1)} %broadcast_xor_fusion.order_ref, f32[2,384,3072]{2,1,0:T(8,128)S(1)} %copy-done), custom_call_target="tpu_custom_call" | custom-call | bytes 9437184 | tf_op jit(solution)/shard_map/split_blocks/pallas_call | solution.py:145
  31.1 3.7 %collective-permute-start.9 = (f32[32,384]{1,0:T(8,128)S(1)}, f32[32,384]{1,0:T(8,128)S(1)}, u32[]{:S(2)}, u32[]{:S(2)}) collective-permute-start(f32[32,384]{1,0:T(8,128)S(1)} %fusion.2), channel_id=1, source_target_pairs={{0,6},{1,7},{2,4},{3,5},{4,2},{5,3},{6,0},{7,1},{8,14},{9,15},{10,... | collective-permute-start | bytes 147464 | tf_op jit(solution)/shard_map/ppermute | solution.py:66
  35.5 2.9 %split_blocks.5 = (bf16[384,3072]{1,0:T(8,128)(2,1)S(1)}, bf16[384,3072]{1,0:T(8,128)(2,1)S(1)}) custom-call(s32[8]{0:T(128)S(1)} %broadcast_xor_fusion.order_ref, f32[2,384,3072]{2,1,0:T(8,128)S(1)} %copy-done), custom_call_target="tpu_custom_call" | custom-call | bytes 9437184 | tf_op jit(solution)/shard_map/split_blocks/pallas_call | solution.py:145
  39.8 2.0 %collective-permute-start.12 = (f32[32,1536]{1,0:T(8,128)S(1)}, f32[32,1536]{1,0:T(8,128)S(1)}, u32[]{:S(2)}, u32[]{:S(2)}) collective-permute-start(f32[32,1536]{1,0:T(8,128)S(1)} %pad_maximum_fusion.7), channel_id=1, source_target_pairs={{0,17},{1,16},{2,19},{3,18},{4,21},{5,20},{6,23},{7,22},{8,25},{9,... | collective-permute-start | bytes 589832 | tf_op jit(solution)/shard_map/ppermute | solution.py:66
  44.1 5.1 %collective-permute-done.10 = f32[32,1536]{1,0:T(8,128)S(1)} collective-permute-done((f32[32,1536]{1,0:T(8,128)S(1)}, f32[32,1536]{1,0:T(8,128)S(1)}, u32[]{:S(2)}, u32[]{:S(2)}) %collective-permute-start.10) | collective-permute-done | bytes 196640 | tf_op jit(solution)/shard_map/ppermute | solution.py:66
  62.8 2.3 %collective-permute-done.16 = f32[32,384]{1,0:T(8,128)S(1)} collective-permute-done((f32[32,384]{1,0:T(8,128)S(1)}, f32[32,384]{1,0:T(8,128)S(1)}, u32[]{:S(2)}, u32[]{:S(2)}) %collective-permute-start.16) | collective-permute-done | bytes 49184 | tf_op jit(solution)/shard_map/ppermute | solution.py:66
  65.2 3.5 %collective-permute-start.20 = (f32[32,384]{1,0:T(8,128)S(1)}, f32[32,384]{1,0:T(8,128)S(1)}, u32[]{:S(2)}, u32[]{:S(2)}) collective-permute-start(f32[32,384]{1,0:T(8,128)S(1)} %select_select_fusion.4), channel_id=1, source_target_pairs={{0,6},{1,7},{2,4},{3,5},{4,2},{5,3},{6,0},{7,1},{8,14},{9,15},{10,... | collective-permute-start | bytes 147464 | tf_op jit(solution)/shard_map/ppermute | solution.py:66
  69.6 1.6 %collective-permute-done.20 = f32[32,384]{1,0:T(8,128)S(1)} collective-permute-done((f32[32,384]{1,0:T(8,128)S(1)}, f32[32,384]{1,0:T(8,128)S(1)}, u32[]{:S(2)}, u32[]{:S(2)}) %collective-permute-start.20) | collective-permute-done | bytes 49184 | tf_op jit(solution)/shard_map/ppermute | solution.py:66
  71.2 2.5 %collective-permute-done.19 = f32[32,384]{1,0:T(8,128)S(1)} collective-permute-done((f32[32,384]{1,0:T(8,128)S(1)}, f32[32,384]{1,0:T(8,128)S(1)}, u32[]{:S(2)}, u32[]{:S(2)}) %collective-permute-start.19) | collective-permute-done | bytes 49184 | tf_op jit(solution)/shard_map/ppermute | solution.py:66
  77.9 1.6 %collective-permute-done.21 = f32[32,1536]{1,0:T(8,128)S(1)} collective-permute-done((f32[32,1536]{1,0:T(8,128)S(1)}, f32[32,1536]{1,0:T(8,128)S(1)}, u32[]{:S(2)}, u32[]{:S(2)}) %collective-permute-start.21) | collective-permute-done | bytes 196640 | tf_op jit(solution)/shard_map/ppermute | solution.py:66
  82.7 2.3 %collective-permute-start.24 = (f32[32,384]{1,0:T(8,128)S(1)}, f32[32,384]{1,0:T(8,128)S(1)}, u32[]{:S(2)}, u32[]{:S(2)}) collective-permute-start(f32[32,384]{1,0:T(8,128)S(1)} %fusion.1), channel_id=1, source_target_pairs={{0,2},{1,3},{2,0},{3,1},{4,6},{5,7},{6,4},{7,5},{8,10},{9,11},{10,... | collective-permute-start | bytes 147464 | tf_op jit(solution)/shard_map/ppermute | solution.py:66
  87.6 1.7 %collective-permute-start.29 = (f32[32,1536]{1,0:T(8,128)S(1)}, f32[32,1536]{1,0:T(8,128)S(1)}, u32[]{:S(2)}, u32[]{:S(2)}) collective-permute-start(f32[32,1536]{1,0:T(8,128)S(1)} %pad_maximum_fusion.9), channel_id=1, source_target_pairs={{0,17},{1,16},{2,19},{3,18},{4,21},{5,20},{6,23},{7,22},{8,25},{9,... | collective-permute-start | bytes 589832 | tf_op jit(solution)/shard_map/ppermute | solution.py:66
  91.2 5.2 %collective-permute-done.27 = f32[32,1536]{1,0:T(8,128)S(1)} collective-permute-done((f32[32,1536]{1,0:T(8,128)S(1)}, f32[32,1536]{1,0:T(8,128)S(1)}, u32[]{:S(2)}, u32[]{:S(2)}) %collective-permute-start.27) | collective-permute-done | bytes 196640 | tf_op jit(solution)/shard_map/ppermute | solution.py:66
  104.4 1.7 %collective-permute-done.33 = f32[32,384]{1,0:T(8,128)S(1)} collective-permute-done((f32[32,384]{1,0:T(8,128)S(1)}, f32[32,384]{1,0:T(8,128)S(1)}, u32[]{:S(2)}, u32[]{:S(2)}) %collective-permute-start.33) | collective-permute-done | bytes 49184 | tf_op jit(solution)/shard_map/ppermute | solution.py:66
  106.1 2.4 %collective-permute-start.37 = (f32[32,384]{1,0:T(8,128)S(1)}, f32[32,384]{1,0:T(8,128)S(1)}, u32[]{:S(2)}, u32[]{:S(2)}) collective-permute-start(f32[32,384]{1,0:T(8,128)S(1)} %select_select_fusion.3), channel_id=1, source_target_pairs={{0,6},{1,7},{2,4},{3,5},{4,2},{5,3},{6,0},{7,1},{8,14},{9,15},{10,... | collective-permute-start | bytes 147464 | tf_op jit(solution)/shard_map/ppermute | solution.py:66
  110.6 1.6 %collective-permute-done.37 = f32[32,384]{1,0:T(8,128)S(1)} collective-permute-done((f32[32,384]{1,0:T(8,128)S(1)}, f32[32,384]{1,0:T(8,128)S(1)}, u32[]{:S(2)}, u32[]{:S(2)}) %collective-permute-start.37) | collective-permute-done | bytes 49184 | tf_op jit(solution)/shard_map/ppermute | solution.py:66
  112.1 1.6 %collective-permute-done.36 = f32[32,384]{1,0:T(8,128)S(1)} collective-permute-done((f32[32,384]{1,0:T(8,128)S(1)}, f32[32,384]{1,0:T(8,128)S(1)}, u32[]{:S(2)}, u32[]{:S(2)}) %collective-permute-start.36) | collective-permute-done | bytes 49184 | tf_op jit(solution)/shard_map/ppermute | solution.py:66
  117.8 1.7 %collective-permute-done.38 = f32[32,1536]{1,0:T(8,128)S(1)} collective-permute-done((f32[32,1536]{1,0:T(8,128)S(1)}, f32[32,1536]{1,0:T(8,128)S(1)}, u32[]{:S(2)}, u32[]{:S(2)}) %collective-permute-start.38) | collective-permute-done | bytes 196640 | tf_op jit(solution)/shard_map/ppermute | solution.py:66
  120.6 2.9 %collective-permute-start.43 = (f32[32,384]{1,0:T(8,128)S(1)}, f32[32,384]{1,0:T(8,128)S(1)}, u32[]{:S(2)}, u32[]{:S(2)}) collective-permute-start(f32[32,384]{1,0:T(8,128)S(1)} %fusion), channel_id=1, source_target_pairs={{0,6},{1,7},{2,4},{3,5},{4,2},{5,3},{6,0},{7,1},{8,14},{9,15},{10,... | collective-permute-start | bytes 147464 | tf_op jit(solution)/shard_map/ppermute | solution.py:66
  123.4 1.6 %collective-permute-start.41 = (f32[32,384]{1,0:T(8,128)S(1)}, f32[32,384]{1,0:T(8,128)S(1)}, u32[]{:S(2)}, u32[]{:S(2)}) collective-permute-start(f32[32,384]{1,0:T(8,128)S(1)} %fusion), channel_id=1, source_target_pairs={{0,2},{1,3},{2,0},{3,1},{4,6},{5,7},{6,4},{7,5},{8,10},{9,11},{10,... | collective-permute-start | bytes 147464 | tf_op jit(solution)/shard_map/ppermute | solution.py:66
  126.5 1.9 %collective-permute-done.42 = f32[32,384]{1,0:T(8,128)S(1)} collective-permute-done((f32[32,384]{1,0:T(8,128)S(1)}, f32[32,384]{1,0:T(8,128)S(1)}, u32[]{:S(2)}, u32[]{:S(2)}) %collective-permute-start.42) | collective-permute-done | bytes 49184 | tf_op jit(solution)/shard_map/ppermute | solution.py:66
  128.4 1.8 %collective-permute-start.46 = (f32[32,1536]{1,0:T(8,128)S(1)}, f32[32,1536]{1,0:T(8,128)S(1)}, u32[]{:S(2)}, u32[]{:S(2)}) collective-permute-start(f32[32,1536]{1,0:T(8,128)S(1)} %pad_maximum_fusion.11), channel_id=1, source_target_pairs={{0,17},{1,16},{2,19},{3,18},{4,21},{5,20},{6,23},{7,22},{8,25},{9,... | collective-permute-start | bytes 589832 | tf_op jit(solution)/shard_map/ppermute | solution.py:66
  132.0 8.3 %collective-permute-done.44 = f32[32,1536]{1,0:T(8,128)S(1)} collective-permute-done((f32[32,1536]{1,0:T(8,128)S(1)}, f32[32,1536]{1,0:T(8,128)S(1)}, u32[]{:S(2)}, u32[]{:S(2)}) %collective-permute-start.44) | collective-permute-done | bytes 196640 | tf_op jit(solution)/shard_map/ppermute | solution.py:66
  143.1 3.4 %last.1 = (f32[384,128]{1,0:T(8,128)}, f32[2,384,128]{2,1,0:T(8,128)}) custom-call(bf16[384,3072]{1,0:T(8,128)(2,1)S(1)} %copy-done.4, bf16[384,3072]{1,0:T(8,128)(2,1)S(1)} %copy-done.6, bf16[384,3072]{1,0:T(8,128)(2,1)S(1)} %get-tuple-element.101.high_ref.h1_ref, bf16[384,3072]{1,0:T(8,128)(2,1)S(1)} %copy-done.2, ...), custom_call_target="tpu_custom_call" | custom-call | flops 1811939328 | bytes 9437184 | tf_op jit(solution)/shard_map/last/pallas_call | solution.py:214
  (180 shorter events, 59.5 us)
Async XLA Ops:
  9.1 10.0 %collective-permute-start.5 = (f32[32,384]{1,0:T(8,128)S(1)}, f32[32,384]{1,0:T(8,128)S(1)}, u32[]{:S(2)}, u32[]{:S(2)}) collective-permute-start(f32[32,384]{1,0:T(8,128)S(1)} %select_select_fusion.5), channel_id=1, source_target_pairs={{0,6},{1,7},{2,4},{3,5},{4,2},{5,3},{6,0},{7,1},{8,14},{9,15},{10,... | collective-permute-start | bytes 147464 | tf_op jit(solution)/shard_map/ppermute | solution.py:66
  12.8 6.3 %collective-permute-start.4 = (f32[32,384]{1,0:T(8,128)S(1)}, f32[32,384]{1,0:T(8,128)S(1)}, u32[]{:S(2)}, u32[]{:S(2)}) collective-permute-start(f32[32,384]{1,0:T(8,128)S(1)} %select_select_fusion.5), channel_id=1, source_target_pairs={{0,4},{1,5},{2,6},{3,7},{4,0},{5,1},{6,2},{7,3},{8,12},{9,13},{10,... | collective-permute-start | bytes 147464 | tf_op jit(solution)/shard_map/ppermute | solution.py:66
  12.8 6.3 %collective-permute-start.3 = (f32[32,384]{1,0:T(8,128)S(1)}, f32[32,384]{1,0:T(8,128)S(1)}, u32[]{:S(2)}, u32[]{:S(2)}) collective-permute-start(f32[32,384]{1,0:T(8,128)S(1)} %select_select_fusion.5), channel_id=1, source_target_pairs={{0,2},{1,3},{2,0},{3,1},{4,6},{5,7},{6,4},{7,5},{8,10},{9,11},{10,... | collective-permute-start | bytes 147464 | tf_op jit(solution)/shard_map/ppermute | solution.py:66
  19.2 10.8 %collective-permute-start.6 = (f32[32,1536]{1,0:T(8,128)S(1)}, f32[32,1536]{1,0:T(8,128)S(1)}, u32[]{:S(2)}, u32[]{:S(2)}) collective-permute-start(f32[32,1536]{1,0:T(8,128)S(1)} %pad_maximum_fusion.6), channel_id=1, source_target_pairs={{0,1},{1,0},{2,3},{3,2},{4,5},{5,4},{6,7},{7,6},{8,9},{9,8},{10,11... | collective-permute-start | bytes 589832 | tf_op jit(solution)/shard_map/ppermute | solution.py:66
  31.1 8.7 %collective-permute-start.9 = (f32[32,384]{1,0:T(8,128)S(1)}, f32[32,384]{1,0:T(8,128)S(1)}, u32[]{:S(2)}, u32[]{:S(2)}) collective-permute-start(f32[32,384]{1,0:T(8,128)S(1)} %fusion.2), channel_id=1, source_target_pairs={{0,6},{1,7},{2,4},{3,5},{4,2},{5,3},{6,0},{7,1},{8,14},{9,15},{10,... | collective-permute-start | bytes 147464 | tf_op jit(solution)/shard_map/ppermute | solution.py:66
  34.8 5.0 %collective-permute-start.8 = (f32[32,384]{1,0:T(8,128)S(1)}, f32[32,384]{1,0:T(8,128)S(1)}, u32[]{:S(2)}, u32[]{:S(2)}) collective-permute-start(f32[32,384]{1,0:T(8,128)S(1)} %fusion.2), channel_id=1, source_target_pairs={{0,4},{1,5},{2,6},{3,7},{4,0},{5,1},{6,2},{7,3},{8,12},{9,13},{10,... | collective-permute-start | bytes 147464 | tf_op jit(solution)/shard_map/ppermute | solution.py:66
  34.8 5.0 %collective-permute-start.7 = (f32[32,384]{1,0:T(8,128)S(1)}, f32[32,384]{1,0:T(8,128)S(1)}, u32[]{:S(2)}, u32[]{:S(2)}) collective-permute-start(f32[32,384]{1,0:T(8,128)S(1)} %fusion.2), channel_id=1, source_target_pairs={{0,2},{1,3},{2,0},{3,1},{4,6},{5,7},{6,4},{7,5},{8,10},{9,11},{10,... | collective-permute-start | bytes 147464 | tf_op jit(solution)/shard_map/ppermute | solution.py:66
  39.8 10.1 %collective-permute-start.12 = (f32[32,1536]{1,0:T(8,128)S(1)}, f32[32,1536]{1,0:T(8,128)S(1)}, u32[]{:S(2)}, u32[]{:S(2)}) collective-permute-start(f32[32,1536]{1,0:T(8,128)S(1)} %pad_maximum_fusion.7), channel_id=1, source_target_pairs={{0,17},{1,16},{2,19},{3,18},{4,21},{5,20},{6,23},{7,22},{8,25},{9,... | collective-permute-start | bytes 589832 | tf_op jit(solution)/shard_map/ppermute | solution.py:66
  41.8 8.1 %collective-permute-start.11 = (f32[32,1536]{1,0:T(8,128)S(1)}, f32[32,1536]{1,0:T(8,128)S(1)}, u32[]{:S(2)}, u32[]{:S(2)}) collective-permute-start(f32[32,1536]{1,0:T(8,128)S(1)} %pad_maximum_fusion.7), channel_id=1, source_target_pairs={{0,1},{1,0},{2,3},{3,2},{4,5},{5,4},{6,7},{7,6},{8,9},{9,8},{10,11... | collective-permute-start | bytes 589832 | tf_op jit(solution)/shard_map/ppermute | solution.py:66
  42.3 6.9 %collective-permute-start.10 = (f32[32,1536]{1,0:T(8,128)S(1)}, f32[32,1536]{1,0:T(8,128)S(1)}, u32[]{:S(2)}, u32[]{:S(2)}) collective-permute-start(f32[32,1536]{1,0:T(8,128)S(1)} %pad_maximum_fusion.7), channel_id=1, source_target_pairs={{0,16},{1,17},{2,18},{3,19},{4,20},{5,21},{6,22},{7,23},{8,24},{9,... | collective-permute-start | bytes 589832 | tf_op jit(solution)/shard_map/ppermute | solution.py:66
  61.3 8.3 %collective-permute-start.23 = (f32[128,384]{1,0:T(8,128)S(1)}, f32[128,384]{1,0:T(8,128)S(1)}, u32[]{:S(2)}, u32[]{:S(2)}) collective-permute-start(f32[128,384]{1,0:T(8,128)S(1)} %get-tuple-element.89), channel_id=1, source_target_pairs={{0,24},{1,25},{2,26},{3,27},{4,28},{5,29},{6,30},{7,31},{8,16},{9,... | collective-permute-start | bytes 589832 | tf_op jit(solution)/shard_map/ppermute | solution.py:66
  62.1 7.5 %collective-permute-start.22 = (f32[128,384]{1,0:T(8,128)S(1)}, f32[128,384]{1,0:T(8,128)S(1)}, u32[]{:S(2)}, u32[]{:S(2)}) collective-permute-start(f32[128,384]{1,0:T(8,128)S(1)} %get-tuple-element.89), channel_id=1, source_target_pairs={{0,8},{1,9},{2,10},{3,11},{4,12},{5,13},{6,14},{7,15},{8,0},{9,1},... | collective-permute-start | bytes 589832 | tf_op jit(solution)/shard_map/ppermute | solution.py:66
  65.2 6.1 %collective-permute-start.20 = (f32[32,384]{1,0:T(8,128)S(1)}, f32[32,384]{1,0:T(8,128)S(1)}, u32[]{:S(2)}, u32[]{:S(2)}) collective-permute-start(f32[32,384]{1,0:T(8,128)S(1)} %select_select_fusion.4), channel_id=1, source_target_pairs={{0,6},{1,7},{2,4},{3,5},{4,2},{5,3},{6,0},{7,1},{8,14},{9,15},{10,... | collective-permute-start | bytes 147464 | tf_op jit(solution)/shard_map/ppermute | solution.py:66
  68.7 5.0 %collective-permute-start.19 = (f32[32,384]{1,0:T(8,128)S(1)}, f32[32,384]{1,0:T(8,128)S(1)}, u32[]{:S(2)}, u32[]{:S(2)}) collective-permute-start(f32[32,384]{1,0:T(8,128)S(1)} %select_select_fusion.4), channel_id=1, source_target_pairs={{0,4},{1,5},{2,6},{3,7},{4,0},{5,1},{6,2},{7,3},{8,12},{9,13},{10,... | collective-permute-start | bytes 147464 | tf_op jit(solution)/shard_map/ppermute | solution.py:66
  68.7 5.0 %collective-permute-start.18 = (f32[32,384]{1,0:T(8,128)S(1)}, f32[32,384]{1,0:T(8,128)S(1)}, u32[]{:S(2)}, u32[]{:S(2)}) collective-permute-start(f32[32,384]{1,0:T(8,128)S(1)} %select_select_fusion.4), channel_id=1, source_target_pairs={{0,2},{1,3},{2,0},{3,1},{4,6},{5,7},{6,4},{7,5},{8,10},{9,11},{10,... | collective-permute-start | bytes 147464 | tf_op jit(solution)/shard_map/ppermute | solution.py:66
  73.7 5.7 %collective-permute-start.21 = (f32[32,1536]{1,0:T(8,128)S(1)}, f32[32,1536]{1,0:T(8,128)S(1)}, u32[]{:S(2)}, u32[]{:S(2)}) collective-permute-start(f32[32,1536]{1,0:T(8,128)S(1)} %pad_maximum_fusion.8), channel_id=1, source_target_pairs={{0,1},{1,0},{2,3},{3,2},{4,5},{5,4},{6,7},{7,6},{8,9},{9,8},{10,11... | collective-permute-start | bytes 589832 | tf_op jit(solution)/shard_map/ppermute | solution.py:66
  80.5 6.0 %collective-permute-start.26 = (f32[32,384]{1,0:T(8,128)S(1)}, f32[32,384]{1,0:T(8,128)S(1)}, u32[]{:S(2)}, u32[]{:S(2)}) collective-permute-start(f32[32,384]{1,0:T(8,128)S(1)} %fusion.1), channel_id=1, source_target_pairs={{0,6},{1,7},{2,4},{3,5},{4,2},{5,3},{6,0},{7,1},{8,14},{9,15},{10,... | collective-permute-start | bytes 147464 | tf_op jit(solution)/shard_map/ppermute | solution.py:66
  82.1 5.0 %collective-permute-start.25 = (f32[32,384]{1,0:T(8,128)S(1)}, f32[32,384]{1,0:T(8,128)S(1)}, u32[]{:S(2)}, u32[]{:S(2)}) collective-permute-start(f32[32,384]{1,0:T(8,128)S(1)} %fusion.1), channel_id=1, source_target_pairs={{0,4},{1,5},{2,6},{3,7},{4,0},{5,1},{6,2},{7,3},{8,12},{9,13},{10,... | collective-permute-start | bytes 147464 | tf_op jit(solution)/shard_map/ppermute | solution.py:66
  87.6 8.9 %collective-permute-start.29 = (f32[32,1536]{1,0:T(8,128)S(1)}, f32[32,1536]{1,0:T(8,128)S(1)}, u32[]{:S(2)}, u32[]{:S(2)}) collective-permute-start(f32[32,1536]{1,0:T(8,128)S(1)} %pad_maximum_fusion.9), channel_id=1, source_target_pairs={{0,17},{1,16},{2,19},{3,18},{4,21},{5,20},{6,23},{7,22},{8,25},{9,... | collective-permute-start | bytes 589832 | tf_op jit(solution)/shard_map/ppermute | solution.py:66
  89.3 7.1 %collective-permute-start.28 = (f32[32,1536]{1,0:T(8,128)S(1)}, f32[32,1536]{1,0:T(8,128)S(1)}, u32[]{:S(2)}, u32[]{:S(2)}) collective-permute-start(f32[32,1536]{1,0:T(8,128)S(1)} %pad_maximum_fusion.9), channel_id=1, source_target_pairs={{0,1},{1,0},{2,3},{3,2},{4,5},{5,4},{6,7},{7,6},{8,9},{9,8},{10,11... | collective-permute-start | bytes 589832 | tf_op jit(solution)/shard_map/ppermute | solution.py:66
  89.8 6.5 %collective-permute-start.27 = (f32[32,1536]{1,0:T(8,128)S(1)}, f32[32,1536]{1,0:T(8,128)S(1)}, u32[]{:S(2)}, u32[]{:S(2)}) collective-permute-start(f32[32,1536]{1,0:T(8,128)S(1)} %pad_maximum_fusion.9), channel_id=1, source_target_pairs={{0,16},{1,17},{2,18},{3,19},{4,20},{5,21},{6,22},{7,23},{8,24},{9,... | collective-permute-start | bytes 589832 | tf_op jit(solution)/shard_map/ppermute | solution.py:66
  102.9 7.7 %collective-permute-start.40 = (f32[128,384]{1,0:T(8,128)S(1)}, f32[128,384]{1,0:T(8,128)S(1)}, u32[]{:S(2)}, u32[]{:S(2)}) collective-permute-start(f32[128,384]{1,0:T(8,128)S(1)} %get-tuple-element.99), channel_id=1, source_target_pairs={{0,24},{1,25},{2,26},{3,27},{4,28},{5,29},{6,30},{7,31},{8,16},{9,... | collective-permute-start | bytes 589832 | tf_op jit(solution)/shard_map/ppermute | solution.py:66
  103.1 7.5 %collective-permute-start.39 = (f32[128,384]{1,0:T(8,128)S(1)}, f32[128,384]{1,0:T(8,128)S(1)}, u32[]{:S(2)}, u32[]{:S(2)}) collective-permute-start(f32[128,384]{1,0:T(8,128)S(1)} %get-tuple-element.99), channel_id=1, source_target_pairs={{0,8},{1,9},{2,10},{3,11},{4,12},{5,13},{6,14},{7,15},{8,0},{9,1},... | collective-permute-start | bytes 589832 | tf_op jit(solution)/shard_map/ppermute | solution.py:66
  106.1 6.1 %collective-permute-start.37 = (f32[32,384]{1,0:T(8,128)S(1)}, f32[32,384]{1,0:T(8,128)S(1)}, u32[]{:S(2)}, u32[]{:S(2)}) collective-permute-start(f32[32,384]{1,0:T(8,128)S(1)} %select_select_fusion.3), channel_id=1, source_target_pairs={{0,6},{1,7},{2,4},{3,5},{4,2},{5,3},{6,0},{7,1},{8,14},{9,15},{10,... | collective-permute-start | bytes 147464 | tf_op jit(solution)/shard_map/ppermute | solution.py:66
  108.5 5.2 %collective-permute-start.36 = (f32[32,384]{1,0:T(8,128)S(1)}, f32[32,384]{1,0:T(8,128)S(1)}, u32[]{:S(2)}, u32[]{:S(2)}) collective-permute-start(f32[32,384]{1,0:T(8,128)S(1)} %select_select_fusion.3), channel_id=1, source_target_pairs={{0,4},{1,5},{2,6},{3,7},{4,0},{5,1},{6,2},{7,3},{8,12},{9,13},{10,... | collective-permute-start | bytes 147464 | tf_op jit(solution)/shard_map/ppermute | solution.py:66
  113.8 5.7 %collective-permute-start.38 = (f32[32,1536]{1,0:T(8,128)S(1)}, f32[32,1536]{1,0:T(8,128)S(1)}, u32[]{:S(2)}, u32[]{:S(2)}) collective-permute-start(f32[32,1536]{1,0:T(8,128)S(1)} %pad_maximum_fusion.10), channel_id=1, source_target_pairs={{0,1},{1,0},{2,3},{3,2},{4,5},{5,4},{6,7},{7,6},{8,9},{9,8},{10,11... | collective-permute-start | bytes 589832 | tf_op jit(solution)/shard_map/ppermute | solution.py:66
  120.6 6.0 %collective-permute-start.43 = (f32[32,384]{1,0:T(8,128)S(1)}, f32[32,384]{1,0:T(8,128)S(1)}, u32[]{:S(2)}, u32[]{:S(2)}) collective-permute-start(f32[32,384]{1,0:T(8,128)S(1)} %fusion), channel_id=1, source_target_pairs={{0,6},{1,7},{2,4},{3,5},{4,2},{5,3},{6,0},{7,1},{8,14},{9,15},{10,... | collective-permute-start | bytes 147464 | tf_op jit(solution)/shard_map/ppermute | solution.py:66
  125.0 16.0 %collective-permute-start.50 = (f32[128,384]{1,0:T(8,128)S(1)}, f32[128,384]{1,0:T(8,128)S(1)}, u32[]{:S(2)}, u32[]{:S(2)}) collective-permute-start(f32[128,384]{1,0:T(8,128)S(1)} %get-tuple-element.105), channel_id=1, source_target_pairs={{0,24},{1,25},{2,26},{3,27},{4,28},{5,29},{6,30},{7,31},{8,16},{9,... | collective-permute-start | bytes 589832 | tf_op jit(solution)/shard_map/ppermute | solution.py:66
  125.0 16.0 %collective-permute-start.49 = (f32[128,384]{1,0:T(8,128)S(1)}, f32[128,384]{1,0:T(8,128)S(1)}, u32[]{:S(2)}, u32[]{:S(2)}) collective-permute-start(f32[128,384]{1,0:T(8,128)S(1)} %get-tuple-element.105), channel_id=1, source_target_pairs={{0,8},{1,9},{2,10},{3,11},{4,12},{5,13},{6,14},{7,15},{8,0},{9,1},... | collective-permute-start | bytes 589832 | tf_op jit(solution)/shard_map/ppermute | solution.py:66
  128.4 12.1 %collective-permute-start.46 = (f32[32,1536]{1,0:T(8,128)S(1)}, f32[32,1536]{1,0:T(8,128)S(1)}, u32[]{:S(2)}, u32[]{:S(2)}) collective-permute-start(f32[32,1536]{1,0:T(8,128)S(1)} %pad_maximum_fusion.11), channel_id=1, source_target_pairs={{0,17},{1,16},{2,19},{3,18},{4,21},{5,20},{6,23},{7,22},{8,25},{9,... | collective-permute-start | bytes 589832 | tf_op jit(solution)/shard_map/ppermute | solution.py:66
  130.2 10.3 %collective-permute-start.45 = (f32[32,1536]{1,0:T(8,128)S(1)}, f32[32,1536]{1,0:T(8,128)S(1)}, u32[]{:S(2)}, u32[]{:S(2)}) collective-permute-start(f32[32,1536]{1,0:T(8,128)S(1)} %pad_maximum_fusion.11), channel_id=1, source_target_pairs={{0,1},{1,0},{2,3},{3,2},{4,5},{5,4},{6,7},{7,6},{8,9},{9,8},{10,11... | collective-permute-start | bytes 589832 | tf_op jit(solution)/shard_map/ppermute | solution.py:66
  130.7 9.6 %collective-permute-start.44 = (f32[32,1536]{1,0:T(8,128)S(1)}, f32[32,1536]{1,0:T(8,128)S(1)}, u32[]{:S(2)}, u32[]{:S(2)}) collective-permute-start(f32[32,1536]{1,0:T(8,128)S(1)} %pad_maximum_fusion.11), channel_id=1, source_target_pairs={{0,16},{1,17},{2,18},{3,19},{4,20},{5,21},{6,22},{7,23},{8,24},{9,... | collective-permute-start | bytes 589832 | tf_op jit(solution)/shard_map/ppermute | solution.py:66
  (38 other events, 176.5 us)
where the time goes:
time: 147 us
  starting transfers between devices  55.2 us (38%)
  waiting for transfers between devices  47.1 us (32%)
  Pallas kernels  19.1 us (13%)
  local copies, waits for them, and re-layouts  15.3 us (10%)
  matrix products  5.97 us (4%)
  other arithmetic  2.55 us (2%)
    ppermute x51, starting transfers between devices, swap(): return lax.ppermute(array, AXES, pairs)  55.2 us
    ppermute x51, waiting for transfers between devices, swap(): return lax.ppermute(array, AXES, pairs)  47.1 us
    unnamed x47, local copies, waits for them, and re-layouts  13 us
    pallas_call x3, Pallas kernels, split_blocks(): pl.pallas_call(split_kernel, out_shape=(out, out), grid_spec=pltpu.Prefet...  8.2 us
    pallas_call x4, Pallas kernels, field(): pl.pallas_call(functools.partial(field_kernel, step), out_shape=shape if...  6.05 us
    dot_general x12, matrix products, contract(): lax.dot_general(a, b, (((1,), (1,)), ((), ())), preferred_element_type=jn...  5.97 us
    pallas_call x1, Pallas kernels, last(): pl.pallas_call(last_kernel, out_shape=(jax.ShapeDtypeStruct((rows, n), jn...  3.43 us
  transfers between devices with their start and end apart: 51, of which 25 were waited for; matrix products, arithmetic and copies ran while one was open for 4% of the time, Pallas kernels for 8%

commit v1 on v0

--- a/solution.py
+++ b/solution.py
@@ -231,7 +231,7 @@
     width = loads.shape[2] // 4
     g = lax.axis_index("lag")
     r = lax.axis_index("row")
-    plane, core = g // 2, g % 2
+    first_plane, first_core = g < 2, (g & 1) == 0
     near = [k for k in range(0, rows_n, 2)]
     steps = near + [k + 1 for k in near]
     cut = len(near) * height
@@ -252,29 +252,30 @@
         v = jnp.concatenate([near_, far_], 1)
         w = jnp.concatenate([swap(near_, 1, 0), swap(far_, 1, 0)], 1)
         chunks = [v[:width], w[:width], v[width:], w[width:]]
-        even = [jnp.where(core == 0, chunks[j], chunks[j ^ 1]) for j in range(4)]
+        even = [jnp.where(first_core, chunks[j], chunks[j ^ 1]) for j in range(4)]
         return jnp.concatenate(
-            [jnp.where(plane == 0, even[j], even[j ^ 2]) for j in range(4)], 0
+            [jnp.where(first_plane, even[j], even[j ^ 2]) for j in range(4)], 0
         )
 
     def behind(array):
         near_, far = swap(array, 1, 0), swap(array, 3, 0)
-        return jnp.where(core == 0, near_, jnp.where(plane == 0, far, 0.0))
+        return jnp.where(first_core, near_, jnp.where(first_plane, far, 0.0))
 
     tie = lax.optimization_barrier
     keep = functools.partial(pltpu.with_memory_space_constraint, memory_space=pltpu.HBM)
     acc0, rhs = turn_first(keep(history), keep(loads))
+    rhs, first_plane, first_core, g, order = tie((rhs, first_plane, first_core, g, order))
     for step in range(STEPS):
         rhs = scatter(rhs)
         if step == 0:
-            rhs, inverse = tie((rhs, inverse))
+            rhs, order = tie((rhs, order))
             high, low = split_blocks(inverse, order, height)
             inv = [(high[:, :cut], low[:, :cut]), (high[:, cut:], low[:, cut:])]
             a = line(rhs)
             a, inv = tie((a, inv))
-            a, acc0, ops0, history, loads = tie((a, acc0, lag_ops, history, loads))
+            a, acc0, order = tie((a, acc0, order))
             acc1, given = turn(history, loads)
-            op0 = split_blocks(ops0, order, height, 0)
+            op0 = split_blocks(lag_ops, order, height, 0)
             b = swap(a, 0, 1)
             b, acc1, given, op0 = tie((b, acc1, given, op0))
         else:
@@ -286,8 +287,8 @@
         ahead = behind(acc0)
         solved = product(split(a), inv[0]) + product(split(b), inv[1])
         if step == 0:
-            solved, ops1 = tie((solved, lag_ops))
-            op1 = split_blocks(ops1, order, height, 1)
+            solved, order = tie((solved, order))
+            op1 = split_blocks(lag_ops, order, height, 1)
         a = line(solved)
         a, op1 = tie((a, op1))
         current = full(a)

time: 147 us -> 137 us (0.932)
  local copies, waits for them, and re-layouts: 15.3 us -> 4.74 us
    unnamed x47 -> x17, local copies, waits for them, and re-layouts: 13 us -> 4.1 us
  transfers between devices with their start and end apart: 51 -> 51, of which waited for: 25 -> 26; matrix products, arithmetic and copies ran while one was open for 4% -> 3% of each run, Pallas kernels for 8% -> 8%
where the time goes in v1:
time: 137 us; the launch traced here: 136 us
  starting transfers between devices  55.3 us (40%)
  waiting for transfers between devices  47.7 us (35%)
  Pallas kernels  19.3 us (14%)
  matrix products  6 us (4%)
  local copies, waits for them, and re-layouts  4.74 us (3%)
  other arithmetic  2.31 us (2%)
    ppermute x51, starting transfers between devices, swap(): return lax.ppermute(array, AXES, pairs)  55.3 us
    ppermute x51, waiting for transfers between devices, swap(): return lax.ppermute(array, AXES, pairs)  47.7 us
    pallas_call x3, Pallas kernels, split_blocks(): pl.pallas_call(split_kernel, out_shape=(out, out), grid_spec=pltpu.Prefet...  8.2 us
    pallas_call x4, Pallas kernels, field(): pl.pallas_call(functools.partial(field_kernel, step), out_shape=shape if...  6.18 us
    dot_general x12, matrix products, contract(): lax.dot_general(a, b, (((1,), (1,)), ((), ())), preferred_element_type=jn...  6 us
    unnamed x17, local copies, waits for them, and re-layouts  4.1 us
    pallas_call x1, Pallas kernels, last(): pl.pallas_call(last_kernel, out_shape=(jax.ShapeDtypeStruct((rows, n), jn...  3.45 us
  transfers between devices with their start and end apart: 51, of which 26 were waited for; matrix products, arithmetic and copies ran while one was open for 3% of the time, Pallas kernels for 8%

profile of v1, /device:TPU:0, one launch (start us, length us, event | category | flops | bytes accessed | tf_op | source)
XLA Modules:
  0.0 136.4 jit_solution(10670187496880041971)
XLA Ops:
  3.2 2.6 %collective-permute-start.2 = (f32[32,384]{1,0:T(8,128)S(1)}, f32[32,384]{1,0:T(8,128)S(1)}, u32[]{:S(2)}, u32[]{:S(2)}) collective-permute-start(f32[32,384]{1,0:T(8,128)S(1)} %get-tuple-element.153), channel_id=1, source_target_pairs={{0,24},{1,25},{2,26},{3,27},{4,28},{5,29},{6,30},{7,31},{8,16},{9,... | collective-permute-start | bytes 147464 | tf_op jit(solution)/shard_map/ppermute | solution.py:66
  6.1 1.8 %collective-permute-done.2 = f32[32,384]{1,0:T(8,128)S(1)} collective-permute-done((f32[32,384]{1,0:T(8,128)S(1)}, f32[32,384]{1,0:T(8,128)S(1)}, u32[]{:S(2)}, u32[]{:S(2)}) %collective-permute-start.2) | collective-permute-done | bytes 49184 | tf_op jit(solution)/shard_map/ppermute | solution.py:66
  7.8 2.0 %collective-permute-done.1 = f32[32,384]{1,0:T(8,128)S(1)} collective-permute-done((f32[32,384]{1,0:T(8,128)S(1)}, f32[32,384]{1,0:T(8,128)S(1)}, u32[]{:S(2)}, u32[]{:S(2)}) %collective-permute-start.1) | collective-permute-done | bytes 49184 | tf_op jit(solution)/shard_map/ppermute | solution.py:66
  9.9 3.7 %collective-permute-start.5 = (f32[32,384]{1,0:T(8,128)S(1)}, f32[32,384]{1,0:T(8,128)S(1)}, u32[]{:S(2)}, u32[]{:S(2)}) collective-permute-start(f32[32,384]{1,0:T(8,128)S(1)} %select_select_fusion.5), channel_id=1, source_target_pairs={{0,6},{1,7},{2,4},{3,5},{4,2},{5,3},{6,0},{7,1},{8,14},{9,15},{10,... | collective-permute-start | bytes 147464 | tf_op jit(solution)/shard_map/ppermute | solution.py:66
  14.4 2.3 %copy-done.1 = f32[384,3072]{1,0:T(8,128)S(1)} copy-done((f32[384,3072]{1,0:T(8,128)S(1)}, f32[384,3072]{1,0:T(8,128)}, u32[]{:S(2)}) %copy-start.1) | copy-done | bytes 4718616
  16.7 2.7 %split_blocks.3 = (bf16[384,3072]{1,0:T(8,128)(2,1)S(1)}, bf16[384,3072]{1,0:T(8,128)(2,1)S(1)}) custom-call(s32[8]{0:T(128)S(1)} %broadcast_xor_fusion.order_ref, f32[384,3072]{1,0:T(8,128)S(1)} %copy-done.1), custom_call_target="tpu_custom_call" | custom-call | bytes 9437184 | tf_op jit(solution)/shard_map/split_blocks/pallas_call | solution.py:145
  21.5 1.6 %copy-done = f32[2,384,3072]{2,1,0:T(8,128)S(1)} copy-done((f32[2,384,3072]{2,1,0:T(8,128)S(1)}, f32[2,384,3072]{2,1,0:T(8,128)}, u32[]{:S(2)}) %copy-start) | copy-done | bytes 9437208
  23.1 2.7 %split_blocks.4 = (bf16[384,3072]{1,0:T(8,128)(2,1)S(1)}, bf16[384,3072]{1,0:T(8,128)(2,1)S(1)}) custom-call(s32[8]{0:T(128)S(1)} %broadcast_xor_fusion.order_ref, f32[2,384,3072]{2,1,0:T(8,128)S(1)} %copy-done), custom_call_target="tpu_custom_call" | custom-call | bytes 9437184 | tf_op jit(solution)/shard_map/split_blocks/pallas_call | solution.py:145
  27.8 3.7 %collective-permute-start.9 = (f32[32,384]{1,0:T(8,128)S(1)}, f32[32,384]{1,0:T(8,128)S(1)}, u32[]{:S(2)}, u32[]{:S(2)}) collective-permute-start(f32[32,384]{1,0:T(8,128)S(1)} %fusion.2), channel_id=1, source_target_pairs={{0,6},{1,7},{2,4},{3,5},{4,2},{5,3},{6,0},{7,1},{8,14},{9,15},{10,... | collective-permute-start | bytes 147464 | tf_op jit(solution)/shard_map/ppermute | solution.py:66
  32.3 2.9 %split_blocks.5 = (bf16[384,3072]{1,0:T(8,128)(2,1)S(1)}, bf16[384,3072]{1,0:T(8,128)(2,1)S(1)}) custom-call(s32[8]{0:T(128)S(1)} %broadcast_xor_fusion.order_ref, f32[2,384,3072]{2,1,0:T(8,128)S(1)} %copy-done), custom_call_target="tpu_custom_call" | custom-call | bytes 9437184 | tf_op jit(solution)/shard_map/split_blocks/pallas_call | solution.py:145
  36.5 2.0 %collective-permute-start.12 = (f32[32,1536]{1,0:T(8,128)S(1)}, f32[32,1536]{1,0:T(8,128)S(1)}, u32[]{:S(2)}, u32[]{:S(2)}) collective-permute-start(f32[32,1536]{1,0:T(8,128)S(1)} %pad_maximum_fusion.7), channel_id=1, source_target_pairs={{0,17},{1,16},{2,19},{3,18},{4,21},{5,20},{6,23},{7,22},{8,25},{9,... | collective-permute-start | bytes 589832 | tf_op jit(solution)/shard_map/ppermute | solution.py:66
  40.1 5.4 %collective-permute-done.10 = f32[32,1536]{1,0:T(8,128)S(1)} collective-permute-done((f32[32,1536]{1,0:T(8,128)S(1)}, f32[32,1536]{1,0:T(8,128)S(1)}, u32[]{:S(2)}, u32[]{:S(2)}) %collective-permute-start.10) | collective-permute-done | bytes 196640 | tf_op jit(solution)/shard_map/ppermute | solution.py:66
  53.7 2.5 %collective-permute-done.16 = f32[32,384]{1,0:T(8,128)S(1)} collective-permute-done((f32[32,384]{1,0:T(8,128)S(1)}, f32[32,384]{1,0:T(8,128)S(1)}, u32[]{:S(2)}, u32[]{:S(2)}) %collective-permute-start.16) | collective-permute-done | bytes 49184 | tf_op jit(solution)/shard_map/ppermute | solution.py:66
  56.1 2.3 %collective-permute-start.20 = (f32[32,384]{1,0:T(8,128)S(1)}, f32[32,384]{1,0:T(8,128)S(1)}, u32[]{:S(2)}, u32[]{:S(2)}) collective-permute-start(f32[32,384]{1,0:T(8,128)S(1)} %select_select_fusion.4), channel_id=1, source_target_pairs={{0,6},{1,7},{2,4},{3,5},{4,2},{5,3},{6,0},{7,1},{8,14},{9,15},{10,... | collective-permute-start | bytes 147464 | tf_op jit(solution)/shard_map/ppermute | solution.py:66
  58.5 2.1 %collective-permute-start.18 = (f32[32,384]{1,0:T(8,128)S(1)}, f32[32,384]{1,0:T(8,128)S(1)}, u32[]{:S(2)}, u32[]{:S(2)}) collective-permute-start(f32[32,384]{1,0:T(8,128)S(1)} %select_select_fusion.4), channel_id=1, source_target_pairs={{0,2},{1,3},{2,0},{3,1},{4,6},{5,7},{6,4},{7,5},{8,10},{9,11},{10,... | collective-permute-start | bytes 147464 | tf_op jit(solution)/shard_map/ppermute | solution.py:66
  60.6 1.9 %collective-permute-done.20 = f32[32,384]{1,0:T(8,128)S(1)} collective-permute-done((f32[32,384]{1,0:T(8,128)S(1)}, f32[32,384]{1,0:T(8,128)S(1)}, u32[]{:S(2)}, u32[]{:S(2)}) %collective-permute-start.20) | collective-permute-done | bytes 49184 | tf_op jit(solution)/shard_map/ppermute | solution.py:66
  63.6 1.6 %collective-permute-start.21 = (f32[32,1536]{1,0:T(8,128)S(1)}, f32[32,1536]{1,0:T(8,128)S(1)}, u32[]{:S(2)}, u32[]{:S(2)}) collective-permute-start(f32[32,1536]{1,0:T(8,128)S(1)} %pad_maximum_fusion.8), channel_id=1, source_target_pairs={{0,1},{1,0},{2,3},{3,2},{4,5},{5,4},{6,7},{7,6},{8,9},{9,8},{10,11... | collective-permute-start | bytes 589832 | tf_op jit(solution)/shard_map/ppermute | solution.py:66
  67.7 1.6 %collective-permute-done.21 = f32[32,1536]{1,0:T(8,128)S(1)} collective-permute-done((f32[32,1536]{1,0:T(8,128)S(1)}, f32[32,1536]{1,0:T(8,128)S(1)}, u32[]{:S(2)}, u32[]{:S(2)}) %collective-permute-start.21) | collective-permute-done | bytes 196640 | tf_op jit(solution)/shard_map/ppermute | solution.py:66
  70.4 2.0 %collective-permute-start.26 = (f32[32,384]{1,0:T(8,128)S(1)}, f32[32,384]{1,0:T(8,128)S(1)}, u32[]{:S(2)}, u32[]{:S(2)}) collective-permute-start(f32[32,384]{1,0:T(8,128)S(1)} %fusion.1), channel_id=1, source_target_pairs={{0,6},{1,7},{2,4},{3,5},{4,2},{5,3},{6,0},{7,1},{8,14},{9,15},{10,... | collective-permute-start | bytes 147464 | tf_op jit(solution)/shard_map/ppermute | solution.py:66
  73.0 1.8 %collective-permute-start.24 = (f32[32,384]{1,0:T(8,128)S(1)}, f32[32,384]{1,0:T(8,128)S(1)}, u32[]{:S(2)}, u32[]{:S(2)}) collective-permute-start(f32[32,384]{1,0:T(8,128)S(1)} %fusion.1), channel_id=1, source_target_pairs={{0,2},{1,3},{2,0},{3,1},{4,6},{5,7},{6,4},{7,5},{8,10},{9,11},{10,... | collective-permute-start | bytes 147464 | tf_op jit(solution)/shard_map/ppermute | solution.py:66
  77.9 1.7 %collective-permute-start.29 = (f32[32,1536]{1,0:T(8,128)S(1)}, f32[32,1536]{1,0:T(8,128)S(1)}, u32[]{:S(2)}, u32[]{:S(2)}) collective-permute-start(f32[32,1536]{1,0:T(8,128)S(1)} %pad_maximum_fusion.9), channel_id=1, source_target_pairs={{0,17},{1,16},{2,19},{3,18},{4,21},{5,20},{6,23},{7,22},{8,25},{9,... | collective-permute-start | bytes 589832 | tf_op jit(solution)/shard_map/ppermute | solution.py:66
  81.4 5.2 %collective-permute-done.27 = f32[32,1536]{1,0:T(8,128)S(1)} collective-permute-done((f32[32,1536]{1,0:T(8,128)S(1)}, f32[32,1536]{1,0:T(8,128)S(1)}, u32[]{:S(2)}, u32[]{:S(2)}) %collective-permute-start.27) | collective-permute-done | bytes 196640 | tf_op jit(solution)/shard_map/ppermute | solution.py:66
  94.6 1.7 %collective-permute-done.33 = f32[32,384]{1,0:T(8,128)S(1)} collective-permute-done((f32[32,384]{1,0:T(8,128)S(1)}, f32[32,384]{1,0:T(8,128)S(1)}, u32[]{:S(2)}, u32[]{:S(2)}) %collective-permute-start.33) | collective-permute-done | bytes 49184 | tf_op jit(solution)/shard_map/ppermute | solution.py:66
  96.3 2.1 %collective-permute-start.37 = (f32[32,384]{1,0:T(8,128)S(1)}, f32[32,384]{1,0:T(8,128)S(1)}, u32[]{:S(2)}, u32[]{:S(2)}) collective-permute-start(f32[32,384]{1,0:T(8,128)S(1)} %select_select_fusion.3), channel_id=1, source_target_pairs={{0,6},{1,7},{2,4},{3,5},{4,2},{5,3},{6,0},{7,1},{8,14},{9,15},{10,... | collective-permute-start | bytes 147464 | tf_op jit(solution)/shard_map/ppermute | solution.py:66
  98.9 1.9 %collective-permute-start.35 = (f32[32,384]{1,0:T(8,128)S(1)}, f32[32,384]{1,0:T(8,128)S(1)}, u32[]{:S(2)}, u32[]{:S(2)}) collective-permute-start(f32[32,384]{1,0:T(8,128)S(1)} %select_select_fusion.3), channel_id=1, source_target_pairs={{0,2},{1,3},{2,0},{3,1},{4,6},{5,7},{6,4},{7,5},{8,10},{9,11},{10,... | collective-permute-start | bytes 147464 | tf_op jit(solution)/shard_map/ppermute | solution.py:66
  100.8 1.7 %collective-permute-done.37 = f32[32,384]{1,0:T(8,128)S(1)} collective-permute-done((f32[32,384]{1,0:T(8,128)S(1)}, f32[32,384]{1,0:T(8,128)S(1)}, u32[]{:S(2)}, u32[]{:S(2)}) %collective-permute-start.37) | collective-permute-done | bytes 49184 | tf_op jit(solution)/shard_map/ppermute | solution.py:66
  107.9 1.6 %collective-permute-done.38 = f32[32,1536]{1,0:T(8,128)S(1)} collective-permute-done((f32[32,1536]{1,0:T(8,128)S(1)}, f32[32,1536]{1,0:T(8,128)S(1)}, u32[]{:S(2)}, u32[]{:S(2)}) %collective-permute-start.38) | collective-permute-done | bytes 196640 | tf_op jit(solution)/shard_map/ppermute | solution.py:66
  110.6 2.1 %collective-permute-start.43 = (f32[32,384]{1,0:T(8,128)S(1)}, f32[32,384]{1,0:T(8,128)S(1)}, u32[]{:S(2)}, u32[]{:S(2)}) collective-permute-start(f32[32,384]{1,0:T(8,128)S(1)} %fusion), channel_id=1, source_target_pairs={{0,6},{1,7},{2,4},{3,5},{4,2},{5,3},{6,0},{7,1},{8,14},{9,15},{10,... | collective-permute-start | bytes 147464 | tf_op jit(solution)/shard_map/ppermute | solution.py:66
  113.2 1.8 %collective-permute-start.41 = (f32[32,384]{1,0:T(8,128)S(1)}, f32[32,384]{1,0:T(8,128)S(1)}, u32[]{:S(2)}, u32[]{:S(2)}) collective-permute-start(f32[32,384]{1,0:T(8,128)S(1)} %fusion), channel_id=1, source_target_pairs={{0,2},{1,3},{2,0},{3,1},{4,6},{5,7},{6,4},{7,5},{8,10},{9,11},{10,... | collective-permute-start | bytes 147464 | tf_op jit(solution)/shard_map/ppermute | solution.py:66
  117.9 2.2 %collective-permute-start.46 = (f32[32,1536]{1,0:T(8,128)S(1)}, f32[32,1536]{1,0:T(8,128)S(1)}, u32[]{:S(2)}, u32[]{:S(2)}) collective-permute-start(f32[32,1536]{1,0:T(8,128)S(1)} %pad_maximum_fusion.11), channel_id=1, source_target_pairs={{0,17},{1,16},{2,19},{3,18},{4,21},{5,20},{6,23},{7,22},{8,25},{9,... | collective-permute-start | bytes 589832 | tf_op jit(solution)/shard_map/ppermute | solution.py:66
  121.5 8.5 %collective-permute-done.44 = f32[32,1536]{1,0:T(8,128)S(1)} collective-permute-done((f32[32,1536]{1,0:T(8,128)S(1)}, f32[32,1536]{1,0:T(8,128)S(1)}, u32[]{:S(2)}, u32[]{:S(2)}) %collective-permute-start.44) | collective-permute-done | bytes 196640 | tf_op jit(solution)/shard_map/ppermute | solution.py:66
  133.0 3.5 %last.1 = (f32[384,128]{1,0:T(8,128)}, f32[2,384,128]{2,1,0:T(8,128)}) custom-call(bf16[384,3072]{1,0:T(8,128)(2,1)S(1)} %get-tuple-element.73.high_ref.h0_ref, bf16[384,3072]{1,0:T(8,128)(2,1)S(1)} %get-tuple-element.74.low_ref.l0_ref, bf16[384,3072]{1,0:T(8,128)(2,1)S(1)} %get-tuple-element.107.high_ref.h1_ref, ...), custom_call_target="tpu_custom_call" | custom-call | flops 1811939328 | bytes 9437184 | tf_op jit(solution)/shard_map/last/pallas_call | solution.py:214
  (150 shorter events, 52.2 us)
Async XLA Ops:
  9.9 9.9 %collective-permute-start.5 = (f32[32,384]{1,0:T(8,128)S(1)}, f32[32,384]{1,0:T(8,128)S(1)}, u32[]{:S(2)}, u32[]{:S(2)}) collective-permute-start(f32[32,384]{1,0:T(8,128)S(1)} %select_select_fusion.5), channel_id=1, source_target_pairs={{0,6},{1,7},{2,4},{3,5},{4,2},{5,3},{6,0},{7,1},{8,14},{9,15},{10,... | collective-permute-start | bytes 147464 | tf_op jit(solution)/shard_map/ppermute | solution.py:66
  13.6 6.3 %collective-permute-start.4 = (f32[32,384]{1,0:T(8,128)S(1)}, f32[32,384]{1,0:T(8,128)S(1)}, u32[]{:S(2)}, u32[]{:S(2)}) collective-permute-start(f32[32,384]{1,0:T(8,128)S(1)} %select_select_fusion.5), channel_id=1, source_target_pairs={{0,4},{1,5},{2,6},{3,7},{4,0},{5,1},{6,2},{7,3},{8,12},{9,13},{10,... | collective-permute-start | bytes 147464 | tf_op jit(solution)/shard_map/ppermute | solution.py:66
  13.6 6.3 %collective-permute-start.3 = (f32[32,384]{1,0:T(8,128)S(1)}, f32[32,384]{1,0:T(8,128)S(1)}, u32[]{:S(2)}, u32[]{:S(2)}) collective-permute-start(f32[32,384]{1,0:T(8,128)S(1)} %select_select_fusion.5), channel_id=1, source_target_pairs={{0,2},{1,3},{2,0},{3,1},{4,6},{5,7},{6,4},{7,5},{8,10},{9,11},{10,... | collective-permute-start | bytes 147464 | tf_op jit(solution)/shard_map/ppermute | solution.py:66
  19.9 6.8 %collective-permute-start.6 = (f32[32,1536]{1,0:T(8,128)S(1)}, f32[32,1536]{1,0:T(8,128)S(1)}, u32[]{:S(2)}, u32[]{:S(2)}) collective-permute-start(f32[32,1536]{1,0:T(8,128)S(1)} %pad_maximum_fusion.6), channel_id=1, source_target_pairs={{0,1},{1,0},{2,3},{3,2},{4,5},{5,4},{6,7},{7,6},{8,9},{9,8},{10,11... | collective-permute-start | bytes 589832 | tf_op jit(solution)/shard_map/ppermute | solution.py:66
  27.8 7.3 %collective-permute-start.9 = (f32[32,384]{1,0:T(8,128)S(1)}, f32[32,384]{1,0:T(8,128)S(1)}, u32[]{:S(2)}, u32[]{:S(2)}) collective-permute-start(f32[32,384]{1,0:T(8,128)S(1)} %fusion.2), channel_id=1, source_target_pairs={{0,6},{1,7},{2,4},{3,5},{4,2},{5,3},{6,0},{7,1},{8,14},{9,15},{10,... | collective-permute-start | bytes 147464 | tf_op jit(solution)/shard_map/ppermute | solution.py:66
  31.5 5.0 %collective-permute-start.8 = (f32[32,384]{1,0:T(8,128)S(1)}, f32[32,384]{1,0:T(8,128)S(1)}, u32[]{:S(2)}, u32[]{:S(2)}) collective-permute-start(f32[32,384]{1,0:T(8,128)S(1)} %fusion.2), channel_id=1, source_target_pairs={{0,4},{1,5},{2,6},{3,7},{4,0},{5,1},{6,2},{7,3},{8,12},{9,13},{10,... | collective-permute-start | bytes 147464 | tf_op jit(solution)/shard_map/ppermute | solution.py:66
  36.5 9.1 %collective-permute-start.12 = (f32[32,1536]{1,0:T(8,128)S(1)}, f32[32,1536]{1,0:T(8,128)S(1)}, u32[]{:S(2)}, u32[]{:S(2)}) collective-permute-start(f32[32,1536]{1,0:T(8,128)S(1)} %pad_maximum_fusion.7), channel_id=1, source_target_pairs={{0,17},{1,16},{2,19},{3,18},{4,21},{5,20},{6,23},{7,22},{8,25},{9,... | collective-permute-start | bytes 589832 | tf_op jit(solution)/shard_map/ppermute | solution.py:66
  38.5 7.2 %collective-permute-start.11 = (f32[32,1536]{1,0:T(8,128)S(1)}, f32[32,1536]{1,0:T(8,128)S(1)}, u32[]{:S(2)}, u32[]{:S(2)}) collective-permute-start(f32[32,1536]{1,0:T(8,128)S(1)} %pad_maximum_fusion.7), channel_id=1, source_target_pairs={{0,1},{1,0},{2,3},{3,2},{4,5},{5,4},{6,7},{7,6},{8,9},{9,8},{10,11... | collective-permute-start | bytes 589832 | tf_op jit(solution)/shard_map/ppermute | solution.py:66
  39.0 6.4 %collective-permute-start.10 = (f32[32,1536]{1,0:T(8,128)S(1)}, f32[32,1536]{1,0:T(8,128)S(1)}, u32[]{:S(2)}, u32[]{:S(2)}) collective-permute-start(f32[32,1536]{1,0:T(8,128)S(1)} %pad_maximum_fusion.7), channel_id=1, source_target_pairs={{0,16},{1,17},{2,18},{3,19},{4,20},{5,21},{6,22},{7,23},{8,24},{9,... | collective-permute-start | bytes 589832 | tf_op jit(solution)/shard_map/ppermute | solution.py:66
  52.0 8.6 %collective-permute-start.23 = (f32[128,384]{1,0:T(8,128)S(1)}, f32[128,384]{1,0:T(8,128)S(1)}, u32[]{:S(2)}, u32[]{:S(2)}) collective-permute-start(f32[128,384]{1,0:T(8,128)S(1)} %get-tuple-element.95), channel_id=1, source_target_pairs={{0,24},{1,25},{2,26},{3,27},{4,28},{5,29},{6,30},{7,31},{8,16},{9,... | collective-permute-start | bytes 589832 | tf_op jit(solution)/shard_map/ppermute | solution.py:66
  53.0 7.6 %collective-permute-start.22 = (f32[128,384]{1,0:T(8,128)S(1)}, f32[128,384]{1,0:T(8,128)S(1)}, u32[]{:S(2)}, u32[]{:S(2)}) collective-permute-start(f32[128,384]{1,0:T(8,128)S(1)} %get-tuple-element.95), channel_id=1, source_target_pairs={{0,8},{1,9},{2,10},{3,11},{4,12},{5,13},{6,14},{7,15},{8,0},{9,1},... | collective-permute-start | bytes 589832 | tf_op jit(solution)/shard_map/ppermute | solution.py:66
  56.1 6.4 %collective-permute-start.20 = (f32[32,384]{1,0:T(8,128)S(1)}, f32[32,384]{1,0:T(8,128)S(1)}, u32[]{:S(2)}, u32[]{:S(2)}) collective-permute-start(f32[32,384]{1,0:T(8,128)S(1)} %select_select_fusion.4), channel_id=1, source_target_pairs={{0,6},{1,7},{2,4},{3,5},{4,2},{5,3},{6,0},{7,1},{8,14},{9,15},{10,... | collective-permute-start | bytes 147464 | tf_op jit(solution)/shard_map/ppermute | solution.py:66
  58.5 5.1 %collective-permute-start.19 = (f32[32,384]{1,0:T(8,128)S(1)}, f32[32,384]{1,0:T(8,128)S(1)}, u32[]{:S(2)}, u32[]{:S(2)}) collective-permute-start(f32[32,384]{1,0:T(8,128)S(1)} %select_select_fusion.4), channel_id=1, source_target_pairs={{0,4},{1,5},{2,6},{3,7},{4,0},{5,1},{6,2},{7,3},{8,12},{9,13},{10,... | collective-permute-start | bytes 147464 | tf_op jit(solution)/shard_map/ppermute | solution.py:66
  58.5 5.1 %collective-permute-start.18 = (f32[32,384]{1,0:T(8,128)S(1)}, f32[32,384]{1,0:T(8,128)S(1)}, u32[]{:S(2)}, u32[]{:S(2)}) collective-permute-start(f32[32,384]{1,0:T(8,128)S(1)} %select_select_fusion.4), channel_id=1, source_target_pairs={{0,2},{1,3},{2,0},{3,1},{4,6},{5,7},{6,4},{7,5},{8,10},{9,11},{10,... | collective-permute-start | bytes 147464 | tf_op jit(solution)/shard_map/ppermute | solution.py:66
  63.6 5.7 %collective-permute-start.21 = (f32[32,1536]{1,0:T(8,128)S(1)}, f32[32,1536]{1,0:T(8,128)S(1)}, u32[]{:S(2)}, u32[]{:S(2)}) collective-permute-start(f32[32,1536]{1,0:T(8,128)S(1)} %pad_maximum_fusion.8), channel_id=1, source_target_pairs={{0,1},{1,0},{2,3},{3,2},{4,5},{5,4},{6,7},{7,6},{8,9},{9,8},{10,11... | collective-permute-start | bytes 589832 | tf_op jit(solution)/shard_map/ppermute | solution.py:66
  70.4 6.0 %collective-permute-start.26 = (f32[32,384]{1,0:T(8,128)S(1)}, f32[32,384]{1,0:T(8,128)S(1)}, u32[]{:S(2)}, u32[]{:S(2)}) collective-permute-start(f32[32,384]{1,0:T(8,128)S(1)} %fusion.1), channel_id=1, source_target_pairs={{0,6},{1,7},{2,4},{3,5},{4,2},{5,3},{6,0},{7,1},{8,14},{9,15},{10,... | collective-permute-start | bytes 147464 | tf_op jit(solution)/shard_map/ppermute | solution.py:66
  72.3 5.5 %collective-permute-start.25 = (f32[32,384]{1,0:T(8,128)S(1)}, f32[32,384]{1,0:T(8,128)S(1)}, u32[]{:S(2)}, u32[]{:S(2)}) collective-permute-start(f32[32,384]{1,0:T(8,128)S(1)} %fusion.1), channel_id=1, source_target_pairs={{0,4},{1,5},{2,6},{3,7},{4,0},{5,1},{6,2},{7,3},{8,12},{9,13},{10,... | collective-permute-start | bytes 147464 | tf_op jit(solution)/shard_map/ppermute | solution.py:66
  77.9 8.9 %collective-permute-start.29 = (f32[32,1536]{1,0:T(8,128)S(1)}, f32[32,1536]{1,0:T(8,128)S(1)}, u32[]{:S(2)}, u32[]{:S(2)}) collective-permute-start(f32[32,1536]{1,0:T(8,128)S(1)} %pad_maximum_fusion.9), channel_id=1, source_target_pairs={{0,17},{1,16},{2,19},{3,18},{4,21},{5,20},{6,23},{7,22},{8,25},{9,... | collective-permute-start | bytes 589832 | tf_op jit(solution)/shard_map/ppermute | solution.py:66
  79.6 7.1 %collective-permute-start.28 = (f32[32,1536]{1,0:T(8,128)S(1)}, f32[32,1536]{1,0:T(8,128)S(1)}, u32[]{:S(2)}, u32[]{:S(2)}) collective-permute-start(f32[32,1536]{1,0:T(8,128)S(1)} %pad_maximum_fusion.9), channel_id=1, source_target_pairs={{0,1},{1,0},{2,3},{3,2},{4,5},{5,4},{6,7},{7,6},{8,9},{9,8},{10,11... | collective-permute-start | bytes 589832 | tf_op jit(solution)/shard_map/ppermute | solution.py:66
  80.1 6.5 %collective-permute-start.27 = (f32[32,1536]{1,0:T(8,128)S(1)}, f32[32,1536]{1,0:T(8,128)S(1)}, u32[]{:S(2)}, u32[]{:S(2)}) collective-permute-start(f32[32,1536]{1,0:T(8,128)S(1)} %pad_maximum_fusion.9), channel_id=1, source_target_pairs={{0,16},{1,17},{2,18},{3,19},{4,20},{5,21},{6,22},{7,23},{8,24},{9,... | collective-permute-start | bytes 589832 | tf_op jit(solution)/shard_map/ppermute | solution.py:66
  93.1 7.7 %collective-permute-start.40 = (f32[128,384]{1,0:T(8,128)S(1)}, f32[128,384]{1,0:T(8,128)S(1)}, u32[]{:S(2)}, u32[]{:S(2)}) collective-permute-start(f32[128,384]{1,0:T(8,128)S(1)} %get-tuple-element.105), channel_id=1, source_target_pairs={{0,24},{1,25},{2,26},{3,27},{4,28},{5,29},{6,30},{7,31},{8,16},{9,... | collective-permute-start | bytes 589832 | tf_op jit(solution)/shard_map/ppermute | solution.py:66
  93.3 7.5 %collective-permute-start.39 = (f32[128,384]{1,0:T(8,128)S(1)}, f32[128,384]{1,0:T(8,128)S(1)}, u32[]{:S(2)}, u32[]{:S(2)}) collective-permute-start(f32[128,384]{1,0:T(8,128)S(1)} %get-tuple-element.105), channel_id=1, source_target_pairs={{0,8},{1,9},{2,10},{3,11},{4,12},{5,13},{6,14},{7,15},{8,0},{9,1},... | collective-permute-start | bytes 589832 | tf_op jit(solution)/shard_map/ppermute | solution.py:66
  96.3 6.2 %collective-permute-start.37 = (f32[32,384]{1,0:T(8,128)S(1)}, f32[32,384]{1,0:T(8,128)S(1)}, u32[]{:S(2)}, u32[]{:S(2)}) collective-permute-start(f32[32,384]{1,0:T(8,128)S(1)} %select_select_fusion.3), channel_id=1, source_target_pairs={{0,6},{1,7},{2,4},{3,5},{4,2},{5,3},{6,0},{7,1},{8,14},{9,15},{10,... | collective-permute-start | bytes 147464 | tf_op jit(solution)/shard_map/ppermute | solution.py:66
  98.5 5.3 %collective-permute-start.36 = (f32[32,384]{1,0:T(8,128)S(1)}, f32[32,384]{1,0:T(8,128)S(1)}, u32[]{:S(2)}, u32[]{:S(2)}) collective-permute-start(f32[32,384]{1,0:T(8,128)S(1)} %select_select_fusion.3), channel_id=1, source_target_pairs={{0,4},{1,5},{2,6},{3,7},{4,0},{5,1},{6,2},{7,3},{8,12},{9,13},{10,... | collective-permute-start | bytes 147464 | tf_op jit(solution)/shard_map/ppermute | solution.py:66
  103.8 5.7 %collective-permute-start.38 = (f32[32,1536]{1,0:T(8,128)S(1)}, f32[32,1536]{1,0:T(8,128)S(1)}, u32[]{:S(2)}, u32[]{:S(2)}) collective-permute-start(f32[32,1536]{1,0:T(8,128)S(1)} %pad_maximum_fusion.10), channel_id=1, source_target_pairs={{0,1},{1,0},{2,3},{3,2},{4,5},{5,4},{6,7},{7,6},{8,9},{9,8},{10,11... | collective-permute-start | bytes 589832 | tf_op jit(solution)/shard_map/ppermute | solution.py:66
  110.6 6.0 %collective-permute-start.43 = (f32[32,384]{1,0:T(8,128)S(1)}, f32[32,384]{1,0:T(8,128)S(1)}, u32[]{:S(2)}, u32[]{:S(2)}) collective-permute-start(f32[32,384]{1,0:T(8,128)S(1)} %fusion), channel_id=1, source_target_pairs={{0,6},{1,7},{2,4},{3,5},{4,2},{5,3},{6,0},{7,1},{8,14},{9,15},{10,... | collective-permute-start | bytes 147464 | tf_op jit(solution)/shard_map/ppermute | solution.py:66
  112.7 5.1 %collective-permute-start.42 = (f32[32,384]{1,0:T(8,128)S(1)}, f32[32,384]{1,0:T(8,128)S(1)}, u32[]{:S(2)}, u32[]{:S(2)}) collective-permute-start(f32[32,384]{1,0:T(8,128)S(1)} %fusion), channel_id=1, source_target_pairs={{0,4},{1,5},{2,6},{3,7},{4,0},{5,1},{6,2},{7,3},{8,12},{9,13},{10,... | collective-permute-start | bytes 147464 | tf_op jit(solution)/shard_map/ppermute | solution.py:66
  115.1 15.6 %collective-permute-start.50 = (f32[128,384]{1,0:T(8,128)S(1)}, f32[128,384]{1,0:T(8,128)S(1)}, u32[]{:S(2)}, u32[]{:S(2)}) collective-permute-start(f32[128,384]{1,0:T(8,128)S(1)} %get-tuple-element.111), channel_id=1, source_target_pairs={{0,24},{1,25},{2,26},{3,27},{4,28},{5,29},{6,30},{7,31},{8,16},{9,... | collective-permute-start | bytes 589832 | tf_op jit(solution)/shard_map/ppermute | solution.py:66
  115.1 15.6 %collective-permute-start.49 = (f32[128,384]{1,0:T(8,128)S(1)}, f32[128,384]{1,0:T(8,128)S(1)}, u32[]{:S(2)}, u32[]{:S(2)}) collective-permute-start(f32[128,384]{1,0:T(8,128)S(1)} %get-tuple-element.111), channel_id=1, source_target_pairs={{0,8},{1,9},{2,10},{3,11},{4,12},{5,13},{6,14},{7,15},{8,0},{9,1},... | collective-permute-start | bytes 589832 | tf_op jit(solution)/shard_map/ppermute | solution.py:66
  117.9 12.4 %collective-permute-start.46 = (f32[32,1536]{1,0:T(8,128)S(1)}, f32[32,1536]{1,0:T(8,128)S(1)}, u32[]{:S(2)}, u32[]{:S(2)}) collective-permute-start(f32[32,1536]{1,0:T(8,128)S(1)} %pad_maximum_fusion.11), channel_id=1, source_target_pairs={{0,17},{1,16},{2,19},{3,18},{4,21},{5,20},{6,23},{7,22},{8,25},{9,... | collective-permute-start | bytes 589832 | tf_op jit(solution)/shard_map/ppermute | solution.py:66
  120.1 10.1 %collective-permute-start.45 = (f32[32,1536]{1,0:T(8,128)S(1)}, f32[32,1536]{1,0:T(8,128)S(1)}, u32[]{:S(2)}, u32[]{:S(2)}) collective-permute-start(f32[32,1536]{1,0:T(8,128)S(1)} %pad_maximum_fusion.11), channel_id=1, source_target_pairs={{0,1},{1,0},{2,3},{3,2},{4,5},{5,4},{6,7},{7,6},{8,9},{9,8},{10,11... | collective-permute-start | bytes 589832 | tf_op jit(solution)/shard_map/ppermute | solution.py:66
  120.7 9.3 %collective-permute-start.44 = (f32[32,1536]{1,0:T(8,128)S(1)}, f32[32,1536]{1,0:T(8,128)S(1)}, u32[]{:S(2)}, u32[]{:S(2)}) collective-permute-start(f32[32,1536]{1,0:T(8,128)S(1)} %pad_maximum_fusion.11), channel_id=1, source_target_pairs={{0,16},{1,17},{2,18},{3,19},{4,20},{5,21},{6,22},{7,23},{8,24},{9,... | collective-permute-start | bytes 589832 | tf_op jit(solution)/shard_map/ppermute | solution.py:66
  (23 other events, 83.0 us)

commit v2 on v1

--- a/solution.py
+++ b/solution.py
@@ -90,6 +90,10 @@
     return both[:n] + both[n:] + contract(vh, ml)
 
 
+VMEM = pl.BlockSpec(memory_space=pltpu.VMEM)
+SMEM = pl.BlockSpec(memory_space=pltpu.SMEM)
+
+
 def turn_first_kernel(history_ref, loads_ref, past_ref, rhs_ref):
     past_ref[...] = history_ref[0].T
     rhs_ref[...] = loads_ref[0].T - past_ref[...]
@@ -130,36 +134,65 @@
     )(history, loads)
 
 
-def split_kernel(order_ref, m_ref, high_ref, low_ref):
-    high_ref[...], low_ref[...] = split_here(m_ref[...])
-
-
-def split_blocks(matrix, order, size, lag=None):
+def split_kernel(lag, picks, order_ref, *refs):
+    high_ref, low_ref, buffer, arrived = refs[-4:]
+    size = buffer.shape[1] // order_ref.shape[0]
+
+    def copies(source_ref):
+        view = source_ref if lag is None else source_ref.at[lag]
+        return [
+            pltpu.make_async_copy(
+                view.at[:, pl.ds(pl.multiple_of(order_ref[i] * size, 128), size)],
+                buffer.at[:, pl.ds(i * size, size)],
+                arrived.at[i],
+            )
+            for i in range(order_ref.shape[0])
+        ]
+
+    if picks:
+        pick_ref, first_ref, second_ref = refs[:3]
+
+        @pl.when(pick_ref[0] == 0)
+        def _():
+            for copy in copies(first_ref):
+                copy.start()
+
+        @pl.when(pick_ref[0] != 0)
+        def _():
+            for copy in copies(second_ref):
+                copy.start()
+    else:
+        first_ref = refs[0]
+        for copy in copies(first_ref):
+            copy.start()
+    for i, copy in enumerate(copies(first_ref)):
+        copy.wait()
+        part = pl.ds(i * size, size)
+        high_ref[:, part], low_ref[:, part] = split_here(buffer[:, part])
+
+
+def split_blocks(matrix, order, lag=None, pick=None, other=None):
     rows, cols = matrix.shape[-2:]
     out = jax.ShapeDtypeStruct((rows, cols), jnp.bfloat16)
-    spec = pl.BlockSpec((rows, size), lambda i, o: (0, i))
-    if lag is None:
-        source = pl.BlockSpec((rows, size), lambda i, o: (0, o[i]))
-    else:
-        source = pl.BlockSpec((None, rows, size), lambda i, o: (lag, 0, o[i]))
-    return pl.pallas_call(
-        split_kernel,
+    inputs, specs = [order], [SMEM]
+    if pick is not None:
+        inputs, specs = inputs + [pick], specs + [SMEM]
+    sources = [matrix] if other is None else [matrix, other]
+    return pl.pallas_call(
+        functools.partial(split_kernel, lag, pick is not None),
         out_shape=(out, out),
-        grid_spec=pltpu.PrefetchScalarGridSpec(
-            num_scalar_prefetch=1,
-            grid=(cols // size,),
-            in_specs=[source],
-            out_specs=(spec, spec),
-        ),
+        in_specs=specs + [pl.BlockSpec(memory_space=pltpu.HBM)] * len(sources),
+        out_specs=(VMEM, VMEM),
+        scratch_shapes=[
+            pltpu.VMEM((rows, cols), jnp.float32),
+            pltpu.SemaphoreType.DMA((order.shape[0],)),
+        ],
         compiler_params=pltpu.CompilerParams(vmem_limit_bytes=8 << 20),
         cost_estimate=pl.CostEstimate(
             flops=0, bytes_accessed=8 * rows * cols, transcendentals=0
         ),
         name="split_blocks",
-    )(order, matrix)
-
-
-VMEM = pl.BlockSpec(memory_space=pltpu.VMEM)
+    )(*inputs, *sources)
 
 
 def times(vh, vl, high_ref, low_ref):
@@ -168,14 +201,8 @@
     return both[:, :n] + both[:, n:] + contract(low_ref[...], vh)
 
 
-def field_kernel(step, high_ref, low_ref, v_ref, base_ref, *refs):
-    total = base_ref[...] + times(*split_here(v_ref[...]), high_ref, low_ref).T
-    if len(refs) == 1:
-        refs[0][...] = total
-    else:
-        given_ref, out_ref, rhs_ref = refs
-        out_ref[...] = total
-        rhs_ref[...] = given_ref[step] - total
+def field_kernel(high_ref, low_ref, v_ref, base_ref, out_ref):
+    out_ref[...] = base_ref[...] + times(*split_here(v_ref[...]), high_ref, low_ref).T
 
 
 def costs(rows, cols, n):
@@ -184,20 +211,41 @@
     )
 
 
-def field(op, current, base, loads=None, step=0):
+def field(op, current, base):
     high, low = op
     n = current.shape[0]
-    shape = jax.ShapeDtypeStruct((n, high.shape[0]), jnp.float32)
-    inputs = [high, low, current, base] + ([] if loads is None else [loads])
-    return pl.pallas_call(
-        functools.partial(field_kernel, step),
-        out_shape=shape if loads is None else (shape, shape),
-        in_specs=[VMEM] * len(inputs),
-        out_specs=VMEM if loads is None else (VMEM, VMEM),
+    return pl.pallas_call(
+        field_kernel,
+        out_shape=jax.ShapeDtypeStruct((n, high.shape[0]), jnp.float32),
+        in_specs=[VMEM] * 4,
+        out_specs=VMEM,
         compiler_params=pltpu.CompilerParams(vmem_limit_bytes=8 << 20),
         cost_estimate=costs(*high.shape, n),
         name="field",
-    )(*inputs)
+    )(high, low, current, base)
+
+
+def lead_kernel(high_ref, low_ref, near_ref, far_ref, rest_ref, mine_ref, theirs_ref):
+    v = jnp.concatenate([near_ref[...], far_ref[...]], 1)
+    rhs = rest_ref[...] - times(*split_here(v), high_ref, low_ref).T
+    n = mine_ref.shape[0]
+    mine_ref[...] = rhs[:n]
+    theirs_ref[...] = rhs[n:]
+
+
+def lead(op, near, far, rest):
+    high, low = op
+    n = near.shape[0]
+    shape = jax.ShapeDtypeStruct((n // 2, high.shape[0]), jnp.float32)
+    return pl.pallas_call(
+        lead_kernel,
+        out_shape=(shape, shape),
+        in_specs=[VMEM] * 5,
+        out_specs=(VMEM, VMEM),
+        compiler_params=pltpu.CompilerParams(vmem_limit_bytes=8 << 20),
+        cost_estimate=costs(*high.shape, n),
+        name="lead",
+    )(high, low, near, far, rest)
 
 
 def last_kernel(h0_ref, l0_ref, h1_ref, l1_ref, v_ref, b0_ref, b1_ref, current_ref, out_ref):
@@ -245,10 +293,11 @@
         got = [parts[0]] + [swap(parts[j], j, 0) for j in (3, 2, 1)][::-1]
         return lax.select_n(g, *got)
 
-    def full(a):
+    def exchange(a):
         near_y, far_y, far = swap(a, 2, 0), swap(a, 2, 1), swap(a, 0, 1)
-        near_ = jnp.concatenate([a, near_y], 0)
-        far_ = jnp.concatenate([far, far_y], 0)
+        return jnp.concatenate([a, near_y], 0), jnp.concatenate([far, far_y], 0)
+
+    def full(near_, far_):
         v = jnp.concatenate([near_, far_], 1)
         w = jnp.concatenate([swap(near_, 1, 0), swap(far_, 1, 0)], 1)
         chunks = [v[:width], w[:width], v[width:], w[width:]]
@@ -258,44 +307,68 @@
         )
 
     def behind(array):
-        near_, far = swap(array, 1, 0), swap(array, 3, 0)
+        return swap(array, 1, 0), swap(array, 3, 0)
+
+    def choose(received):
+        near_, far = received
         return jnp.where(first_core, near_, jnp.where(first_plane, far, 0.0))
+
+    def pick(array, j):
+        return jnp.concatenate([array[(j + k) * width : (j + k + 1) * width] for k in (0, 2)], 0)
+
+    def pair(array):
+        return jnp.where(first_core, pick(array, 0), swap(pick(array, 1), 1, 0))
 
     tie = lax.optimization_barrier
     keep = functools.partial(pltpu.with_memory_space_constraint, memory_space=pltpu.HBM)
     acc0, rhs = turn_first(keep(history), keep(loads))
-    rhs, first_plane, first_core, g, order = tie((rhs, first_plane, first_core, g, order))
+    rhs, first_plane, first_core, g = tie((rhs, first_plane, first_core, g))
+    which = (g & 1).reshape(1)
+    rhs = scatter(rhs)
+    rhs, acc0, sent_ops = tie((rhs, acc0, lag_ops))
+    other_ops = swap(sent_ops, 1, 0)
     for step in range(STEPS):
-        rhs = scatter(rhs)
         if step == 0:
-            rhs, order = tie((rhs, order))
-            high, low = split_blocks(inverse, order, height)
+            rhs, order, which = tie((rhs, order, which))
+            high, low = split_blocks(keep(inverse), order)
             inv = [(high[:, :cut], low[:, :cut]), (high[:, cut:], low[:, cut:])]
             a = line(rhs)
             a, inv = tie((a, inv))
-            a, acc0, order = tie((a, acc0, order))
             acc1, given = turn(history, loads)
-            op0 = split_blocks(lag_ops, order, height, 0)
             b = swap(a, 0, 1)
-            b, acc1, given, op0 = tie((b, acc1, given, op0))
+            b, acc1, given = tie((b, acc1, given))
         else:
+            current = full(near_, far_)
+            rhs, current, received = tie((rhs, current, received))
+            below = choose(received)
+            new0 = field(own0, current, acc1)
             a = line(rhs)
-            a, acc0, current = tie((a, acc0, current))
-            acc1 = field(op1, current, below)
+            a, acc0, current = tie((a, new0, current))
+            acc1 = field(own1, current, below)
             b = swap(a, 0, 1)
             b, acc1 = tie((b, acc1))
-        ahead = behind(acc0)
+        received = behind(acc0)
         solved = product(split(a), inv[0]) + product(split(b), inv[1])
         if step == 0:
-            solved, order = tie((solved, order))
-            op1 = split_blocks(lag_ops, order, height, 1)
+            solved, order, which = tie((solved, order, which))
+            first = split_blocks(keep(lag_ops), order, 0, which, keep(other_ops))
         a = line(solved)
-        a, op1 = tie((a, op1))
-        current = full(a)
-        below = ahead
         if step < STEPS - 1:
-            acc0, rhs = field(op0, current, acc1, given, step)
-    return last(op0, op1, current, acc1, below)
+            led = pair(acc1)
+            rest = jnp.where(first_core, pick(given[step], 0), pick(given[step], 1)) - led
+        if step == 0:
+            a, first, order = tie((a, first, order))
+            own0 = split_blocks(keep(lag_ops), order, 0)
+            own1 = split_blocks(keep(lag_ops), order, 1)
+        near_, far_ = exchange(a)
+        if step == 0:
+            near_, far_, own0, own1 = tie((near_, far_, own0, own1))
+        if step < STEPS - 1:
+            near_, far_, rest = tie((near_, far_, rest))
+            mine, theirs = lead(first, near_, far_, rest)
+            rhs = jnp.where(first_plane, mine, swap(theirs, 2, 0))
+    current = full(near_, far_)
+    return last(own0, own1, current, acc1, choose(received))
 
 
 def solution(mesh):

time: 137 us -> 141 us (1.029)
  Pallas kernels: 19.3 us -> 26.5 us
  waiting for transfers between devices: 47.7 us -> 54.6 us
  starting transfers between devices: 55.3 us -> 50.4 us
  local copies, waits for them, and re-layouts: 4.74 us -> 0.74 us
    pallas_call x7 -> x10, Pallas kernels: 14.4 us -> 21.5 us  [the longest x4 12.2 us: split_blocks(): pl.pallas_call(functools.partial(split_kernel, lag, pick is not None), ou...]
    ppermute x51 -> x50, waiting for transfers between devices: 47.7 us -> 54.6 us  [swap(): return lax.ppermute(array, AXES, pairs)]
    ppermute x51 -> x50, starting transfers between devices: 55.3 us -> 50.4 us  [swap(): return lax.ppermute(array, AXES, pairs)]
    unnamed x17 -> x12, local copies, waits for them, and re-layouts: 4.1 us -> 0.17 us
  transfers between devices with their start and end apart: 51 -> 50, of which waited for: 26 -> 27; matrix products, arithmetic and copies ran while one was open for 3% -> 5% of each run, Pallas kernels for 8% -> 15%
where the time goes in v2:
time: 141 us
  waiting for transfers between devices  54.6 us (39%)
  starting transfers between devices  50.4 us (36%)
  Pallas kernels  26.5 us (19%)
  matrix products  5.98 us (4%)
  other arithmetic  1.5 us (1%)
    ppermute x50, waiting for transfers between devices, swap(): return lax.ppermute(array, AXES, pairs)  54.6 us
    ppermute x50, starting transfers between devices, swap(): return lax.ppermute(array, AXES, pairs)  50.4 us
    pallas_call x4, Pallas kernels, split_blocks(): pl.pallas_call(functools.partial(split_kernel, lag, pick is not None), ou...  12.2 us
    pallas_call x4, Pallas kernels, field(): pl.pallas_call(field_kernel, out_shape=jax.ShapeDtypeStruct((n, high.shap...  6.27 us
    dot_general x12, matrix products, contract(): lax.dot_general(a, b, (((1,), (1,)), ((), ())), preferred_element_type=jn...  5.98 us
    pallas_call x1, Pallas kernels, last(): pl.pallas_call(last_kernel, out_shape=(jax.ShapeDtypeStruct((rows, n), jn...  3.43 us
    pallas_call x2, Pallas kernels, lead(): pl.pallas_call(lead_kernel, out_shape=(shape, shape), in_specs=[VMEM] * 5...  3.03 us
  transfers between devices with their start and end apart: 50, of which 27 were waited for; matrix products, arithmetic and copies ran while one was open for 5% of the time, Pallas kernels for 15%

profile of v2, /device:TPU:0, one launch (start us, length us, event | category | flops | bytes accessed | tf_op | source)
XLA Modules:
  0.0 141.0 jit_solution(5784244831801512831)
XLA Ops:
  2.0 3.1 %collective-permute-start.1 = (f32[32,384]{1,0:T(8,128)S(1)}, f32[32,384]{1,0:T(8,128)S(1)}, u32[]{:S(2)}, u32[]{:S(2)}) collective-permute-start(f32[32,384]{1,0:T(8,128)S(1)} %get-tuple-element.190), channel_id=1, source_target_pairs={{0,16},{1,17},{2,18},{3,19},{4,20},{5,21},{6,22},{7,23},{8,24},{9,... | collective-permute-start | bytes 147464 | tf_op jit(solution)/shard_map/ppermute | solution.py:66
  5.2 1.9 %collective-permute-done.1 = f32[32,384]{1,0:T(8,128)S(1)} collective-permute-done((f32[32,384]{1,0:T(8,128)S(1)}, f32[32,384]{1,0:T(8,128)S(1)}, u32[]{:S(2)}, u32[]{:S(2)}) %collective-permute-start.1) | collective-permute-done | bytes 49184 | tf_op jit(solution)/shard_map/ppermute | solution.py:66
  7.1 1.7 %collective-permute-done.2 = f32[32,384]{1,0:T(8,128)S(1)} collective-permute-done((f32[32,384]{1,0:T(8,128)S(1)}, f32[32,384]{1,0:T(8,128)S(1)}, u32[]{:S(2)}, u32[]{:S(2)}) %collective-permute-start.2) | collective-permute-done | bytes 49184 | tf_op jit(solution)/shard_map/ppermute | solution.py:66
  9.2 3.7 %collective-permute-start.5 = (f32[32,384]{1,0:T(8,128)S(1)}, f32[32,384]{1,0:T(8,128)S(1)}, u32[]{:S(2)}, u32[]{:S(2)}) collective-permute-start(f32[32,384]{1,0:T(8,128)S(1)} %select_select_fusion.3), channel_id=1, source_target_pairs={{0,6},{1,7},{2,4},{3,5},{4,2},{5,3},{6,0},{7,1},{8,14},{9,15},{10,... | collective-permute-start | bytes 147464 | tf_op jit(solution)/shard_map/ppermute | solution.py:66
  13.6 3.1 %split_blocks.4 = (bf16[384,3072]{1,0:T(8,128)(2,1)S(1)}, bf16[384,3072]{1,0:T(8,128)(2,1)S(1)}) custom-call(s32[8]{0:T(128)S(1)} %broadcast_xor_fusion.order_ref, f32[384,3072]{1,0:T(8,128)} %refs_0_.3), custom_call_target="tpu_custom_call" | custom-call | bytes 9437184 | tf_op jit(solution)/shard_map/split_blocks/pallas_call | solution.py:181
  20.6 3.9 %collective-permute-done.6 = f32[32,1536]{1,0:T(8,128)S(1)} collective-permute-done((f32[32,1536]{1,0:T(8,128)S(1)}, f32[32,1536]{1,0:T(8,128)S(1)}, u32[]{:S(2)}, u32[]{:S(2)}) %collective-permute-start.6) | collective-permute-done | bytes 196640 | tf_op jit(solution)/shard_map/ppermute | solution.py:66
  25.6 3.7 %collective-permute-start.9 = (f32[32,384]{1,0:T(8,128)S(1)}, f32[32,384]{1,0:T(8,128)S(1)}, u32[]{:S(2)}, u32[]{:S(2)}) collective-permute-start(f32[32,384]{1,0:T(8,128)S(1)} %fusion.2), channel_id=1, source_target_pairs={{0,6},{1,7},{2,4},{3,5},{4,2},{5,3},{6,0},{7,1},{8,14},{9,15},{10,... | collective-permute-start | bytes 147464 | tf_op jit(solution)/shard_map/ppermute | solution.py:66
  31.5 2.7 %collective-permute-done.8 = f32[32,384]{1,0:T(8,128)S(1)} collective-permute-done((f32[32,384]{1,0:T(8,128)S(1)}, f32[32,384]{1,0:T(8,128)S(1)}, u32[]{:S(2)}, u32[]{:S(2)}) %collective-permute-start.8) | collective-permute-done | bytes 49184 | tf_op jit(solution)/shard_map/ppermute | solution.py:66
  34.3 3.1 %split_blocks.5 = (bf16[384,3072]{1,0:T(8,128)(2,1)S(1)}, bf16[384,3072]{1,0:T(8,128)(2,1)S(1)}) custom-call(s32[8]{0:T(128)S(1)} %broadcast_xor_fusion.order_ref, s32[1]{0:T(128)} %bitcast.refs_0_, f32[2,384,3072]{2,1,0:T(8,128)} %refs_0_.5, f32[2,384,3072]{2,1,0:T(8,128)} %collective-permute-done.10.refs_2_), custom_call_target="tpu_custom_call" | custom-call | bytes 9437184 | tf_op jit(solution)/shard_map/split_blocks/pallas_call | solution.py:181
  38.5 1.9 %collective-permute-start.13 = (f32[32,1536]{1,0:T(8,128)S(1)}, f32[32,1536]{1,0:T(8,128)S(1)}, u32[]{:S(2)}, u32[]{:S(2)}) collective-permute-start(f32[32,1536]{1,0:T(8,128)S(1)} %pad_maximum_fusion.10), channel_id=1, source_target_pairs={{0,17},{1,16},{2,19},{3,18},{4,21},{5,20},{6,23},{7,22},{8,25},{9,... | collective-permute-start | bytes 589832 | tf_op jit(solution)/shard_map/ppermute | solution.py:66
  41.0 3.1 %split_blocks.6 = (bf16[384,3072]{1,0:T(8,128)(2,1)S(1)}, bf16[384,3072]{1,0:T(8,128)(2,1)S(1)}) custom-call(s32[8]{0:T(128)S(1)} %broadcast_xor_fusion.order_ref, f32[2,384,3072]{2,1,0:T(8,128)} %refs_0_.5), custom_call_target="tpu_custom_call" | custom-call | bytes 9437184 | tf_op jit(solution)/shard_map/split_blocks/pallas_call | solution.py:181
  44.0 3.1 %split_blocks.7 = (bf16[384,3072]{1,0:T(8,128)(2,1)S(1)}, bf16[384,3072]{1,0:T(8,128)(2,1)S(1)}) custom-call(s32[8]{0:T(128)S(1)} %broadcast_xor_fusion.order_ref, f32[2,384,3072]{2,1,0:T(8,128)} %refs_0_.5), custom_call_target="tpu_custom_call" | custom-call | bytes 9437184 | tf_op jit(solution)/shard_map/split_blocks/pallas_call | solution.py:181
  47.1 1.8 %collective-permute-done.11 = f32[32,1536]{1,0:T(8,128)S(1)} collective-permute-done((f32[32,1536]{1,0:T(8,128)S(1)}, f32[32,1536]{1,0:T(8,128)S(1)}, u32[]{:S(2)}, u32[]{:S(2)}) %collective-permute-start.11) | collective-permute-done | bytes 196640 | tf_op jit(solution)/shard_map/ppermute | solution.py:66
  53.7 3.0 %collective-permute-done.15 = f32[32,384]{1,0:T(8,128)S(1)} collective-permute-done((f32[32,384]{1,0:T(8,128)S(1)}, f32[32,384]{1,0:T(8,128)S(1)}, u32[]{:S(2)}, u32[]{:S(2)}) %collective-permute-start.15) | collective-permute-done | bytes 49184 | tf_op jit(solution)/shard_map/ppermute | solution.py:66
  57.1 1.9 %collective-permute-start.22 = (f32[32,384]{1,0:T(8,128)S(1)}, f32[32,384]{1,0:T(8,128)S(1)}, u32[]{:S(2)}, u32[]{:S(2)}) collective-permute-start(f32[32,384]{1,0:T(8,128)S(1)} %broadcast_select_fusion.13), channel_id=1, source_target_pairs={{0,6},{1,7},{2,4},{3,5},{4,2},{5,3},{6,0},{7,1},{8,14},{9,15},{10,... | collective-permute-start | bytes 147464 | tf_op jit(solution)/shard_map/ppermute | solution.py:66
  59.0 2.5 %collective-permute-start.20 = (f32[32,384]{1,0:T(8,128)S(1)}, f32[32,384]{1,0:T(8,128)S(1)}, u32[]{:S(2)}, u32[]{:S(2)}) collective-permute-start(f32[32,384]{1,0:T(8,128)S(1)} %broadcast_select_fusion.13), channel_id=1, source_target_pairs={{0,2},{1,3},{2,0},{3,1},{4,6},{5,7},{6,4},{7,5},{8,10},{9,11},{10,... | collective-permute-start | bytes 147464 | tf_op jit(solution)/shard_map/ppermute | solution.py:66
  67.5 1.7 %field.5.base_ref = f32[128,384]{1,0:T(8,128)S(1)} custom-call(bf16[384,3072]{1,0:T(8,128)(2,1)S(1)} %get-tuple-element.105.high_ref.h1_ref, bf16[384,3072]{1,0:T(8,128)(2,1)S(1)} %get-tuple-element.106.low_ref.l1_ref, f32[128,3072]{1,0:T(8,128)S(1)} %pad_maximum_fusion.v_ref, f32[128,384]{1,0:T(8,128)S(1)} %select_select_fusion.2.base_ref), custom_call_target="tpu_custom_call" | custom-call | flops 905969664 | bytes 4718592 | tf_op jit(solution)/shard_map/field/pallas_call | solution.py:217
  71.2 2.0 %collective-permute-start.26 = (f32[32,384]{1,0:T(8,128)S(1)}, f32[32,384]{1,0:T(8,128)S(1)}, u32[]{:S(2)}, u32[]{:S(2)}) collective-permute-start(f32[32,384]{1,0:T(8,128)S(1)} %fusion.1), channel_id=1, source_target_pairs={{0,6},{1,7},{2,4},{3,5},{4,2},{5,3},{6,0},{7,1},{8,14},{9,15},{10,... | collective-permute-start | bytes 147464 | tf_op jit(solution)/shard_map/ppermute | solution.py:66
  77.2 1.8 %collective-permute-done.25 = f32[32,384]{1,0:T(8,128)S(1)} collective-permute-done((f32[32,384]{1,0:T(8,128)S(1)}, f32[32,384]{1,0:T(8,128)S(1)}, u32[]{:S(2)}, u32[]{:S(2)}) %collective-permute-start.25) | collective-permute-done | bytes 49184 | tf_op jit(solution)/shard_map/ppermute | solution.py:66
  82.6 7.1 %collective-permute-done.27 = f32[32,1536]{1,0:T(8,128)S(1)} collective-permute-done((f32[32,1536]{1,0:T(8,128)S(1)}, f32[32,1536]{1,0:T(8,128)S(1)}, u32[]{:S(2)}, u32[]{:S(2)}) %collective-permute-start.27) | collective-permute-done | bytes 196640 | tf_op jit(solution)/shard_map/ppermute | solution.py:66
  94.3 3.0 %collective-permute-done.31 = f32[32,384]{1,0:T(8,128)S(1)} collective-permute-done((f32[32,384]{1,0:T(8,128)S(1)}, f32[32,384]{1,0:T(8,128)S(1)}, u32[]{:S(2)}, u32[]{:S(2)}) %collective-permute-start.31) | collective-permute-done | bytes 49184 | tf_op jit(solution)/shard_map/ppermute | solution.py:66
  97.8 2.2 %collective-permute-start.38 = (f32[32,384]{1,0:T(8,128)S(1)}, f32[32,384]{1,0:T(8,128)S(1)}, u32[]{:S(2)}, u32[]{:S(2)}) collective-permute-start(f32[32,384]{1,0:T(8,128)S(1)} %broadcast_select_fusion.12), channel_id=1, source_target_pairs={{0,6},{1,7},{2,4},{3,5},{4,2},{5,3},{6,0},{7,1},{8,14},{9,15},{10,... | collective-permute-start | bytes 147464 | tf_op jit(solution)/shard_map/ppermute | solution.py:66
  100.1 2.1 %collective-permute-start.36 = (f32[32,384]{1,0:T(8,128)S(1)}, f32[32,384]{1,0:T(8,128)S(1)}, u32[]{:S(2)}, u32[]{:S(2)}) collective-permute-start(f32[32,384]{1,0:T(8,128)S(1)} %broadcast_select_fusion.12), channel_id=1, source_target_pairs={{0,2},{1,3},{2,0},{3,1},{4,6},{5,7},{6,4},{7,5},{8,10},{9,11},{10,... | collective-permute-start | bytes 147464 | tf_op jit(solution)/shard_map/ppermute | solution.py:66
  108.5 2.7 %collective-permute-done.39 = f32[32,1536]{1,0:T(8,128)S(1)} collective-permute-done((f32[32,1536]{1,0:T(8,128)S(1)}, f32[32,1536]{1,0:T(8,128)S(1)}, u32[]{:S(2)}, u32[]{:S(2)}) %collective-permute-start.39) | collective-permute-done | bytes 196640 | tf_op jit(solution)/shard_map/ppermute | solution.py:66
  112.2 1.8 %collective-permute-start.42 = (f32[32,384]{1,0:T(8,128)S(1)}, f32[32,384]{1,0:T(8,128)S(1)}, u32[]{:S(2)}, u32[]{:S(2)}) collective-permute-start(f32[32,384]{1,0:T(8,128)S(1)} %fusion), channel_id=1, source_target_pairs={{0,6},{1,7},{2,4},{3,5},{4,2},{5,3},{6,0},{7,1},{8,14},{9,15},{10,... | collective-permute-start | bytes 147464 | tf_op jit(solution)/shard_map/ppermute | solution.py:66
  114.7 1.9 %collective-permute-start.40 = (f32[32,384]{1,0:T(8,128)S(1)}, f32[32,384]{1,0:T(8,128)S(1)}, u32[]{:S(2)}, u32[]{:S(2)}) collective-permute-start(f32[32,384]{1,0:T(8,128)S(1)} %fusion), channel_id=1, source_target_pairs={{0,2},{1,3},{2,0},{3,1},{4,6},{5,7},{6,4},{7,5},{8,10},{9,11},{10,... | collective-permute-start | bytes 147464 | tf_op jit(solution)/shard_map/ppermute | solution.py:66
  120.5 2.7 %collective-permute-done.49 = f32[128,384]{1,0:T(8,128)S(1)} collective-permute-done((f32[128,384]{1,0:T(8,128)S(1)}, f32[128,384]{1,0:T(8,128)S(1)}, u32[]{:S(2)}, u32[]{:S(2)}) %collective-permute-start.49) | collective-permute-done | bytes 196640 | tf_op jit(solution)/shard_map/ppermute | solution.py:66
  123.7 1.9 %collective-permute-start.45 = (f32[32,1536]{1,0:T(8,128)S(1)}, f32[32,1536]{1,0:T(8,128)S(1)}, u32[]{:S(2)}, u32[]{:S(2)}) collective-permute-start(f32[32,1536]{1,0:T(8,128)S(1)} %pad_maximum_fusion.14), channel_id=1, source_target_pairs={{0,17},{1,16},{2,19},{3,18},{4,21},{5,20},{6,23},{7,22},{8,25},{9,... | collective-permute-start | bytes 589832 | tf_op jit(solution)/shard_map/ppermute | solution.py:66
  125.7 2.4 %collective-permute-done.43 = f32[32,1536]{1,0:T(8,128)S(1)} collective-permute-done((f32[32,1536]{1,0:T(8,128)S(1)}, f32[32,1536]{1,0:T(8,128)S(1)}, u32[]{:S(2)}, u32[]{:S(2)}) %collective-permute-start.43) | collective-permute-done | bytes 196640 | tf_op jit(solution)/shard_map/ppermute | solution.py:66
  128.1 2.6 %collective-permute-done.44 = f32[32,1536]{1,0:T(8,128)S(1)} collective-permute-done((f32[32,1536]{1,0:T(8,128)S(1)}, f32[32,1536]{1,0:T(8,128)S(1)}, u32[]{:S(2)}, u32[]{:S(2)}) %collective-permute-start.44) | collective-permute-done | bytes 196640 | tf_op jit(solution)/shard_map/ppermute | solution.py:66
  130.8 4.6 %collective-permute-done.45 = f32[32,1536]{1,0:T(8,128)S(1)} collective-permute-done((f32[32,1536]{1,0:T(8,128)S(1)}, f32[32,1536]{1,0:T(8,128)S(1)}, u32[]{:S(2)}, u32[]{:S(2)}) %collective-permute-start.45) | collective-permute-done | bytes 196640 | tf_op jit(solution)/shard_map/ppermute | solution.py:66
  137.5 3.4 %last.1 = (f32[384,128]{1,0:T(8,128)}, f32[2,384,128]{2,1,0:T(8,128)}) custom-call(bf16[384,3072]{1,0:T(8,128)(2,1)S(1)} %get-tuple-element.103.high_ref.h0_ref, bf16[384,3072]{1,0:T(8,128)(2,1)S(1)} %get-tuple-element.104.low_ref.l0_ref, bf16[384,3072]{1,0:T(8,128)(2,1)S(1)} %get-tuple-element.105.high_ref.h1_ref, ...), custom_call_target="tpu_custom_call" | custom-call | flops 1811939328 | bytes 9437184 | tf_op jit(solution)/shard_map/last/pallas_call | solution.py:262
  (151 shorter events, 51.7 us)
Async XLA Ops:
  8.8 25.4 %collective-permute-start.10 = (f32[2,384,3072]{2,1,0:T(8,128)}, f32[2,384,3072]{2,1,0:T(8,128)}, u32[]{:S(2)}, u32[]{:S(2)}) collective-permute-start(f32[2,384,3072]{2,1,0:T(8,128)} %refs_0_.5), channel_id=1, source_target_pairs={{0,8},{1,9},{2,10},{3,11},{4,12},{5,13},{6,14},{7,15},{8,0},{9,1},... | collective-permute-start | bytes 28311560 | tf_op jit(solution)/shard_map/ppermute | solution.py:66
  9.2 7.9 %collective-permute-start.5 = (f32[32,384]{1,0:T(8,128)S(1)}, f32[32,384]{1,0:T(8,128)S(1)}, u32[]{:S(2)}, u32[]{:S(2)}) collective-permute-start(f32[32,384]{1,0:T(8,128)S(1)} %select_select_fusion.3), channel_id=1, source_target_pairs={{0,6},{1,7},{2,4},{3,5},{4,2},{5,3},{6,0},{7,1},{8,14},{9,15},{10,... | collective-permute-start | bytes 147464 | tf_op jit(solution)/shard_map/ppermute | solution.py:66
  13.6 43.4 %collective-permute-start.18 = (f32[128,384]{1,0:T(8,128)S(1)}, f32[128,384]{1,0:T(8,128)S(1)}, u32[]{:S(2)}, u32[]{:S(2)}) collective-permute-start(f32[128,384]{1,0:T(8,128)S(1)} %get-tuple-element.120), channel_id=1, source_target_pairs={{0,8},{1,9},{2,10},{3,11},{4,12},{5,13},{6,14},{7,15},{8,0},{9,1},... | collective-permute-start | bytes 589832 | tf_op jit(solution)/shard_map/ppermute | solution.py:66
  18.0 6.5 %collective-permute-start.6 = (f32[32,1536]{1,0:T(8,128)S(1)}, f32[32,1536]{1,0:T(8,128)S(1)}, u32[]{:S(2)}, u32[]{:S(2)}) collective-permute-start(f32[32,1536]{1,0:T(8,128)S(1)} %pad_maximum_fusion.9), channel_id=1, source_target_pairs={{0,1},{1,0},{2,3},{3,2},{4,5},{5,4},{6,7},{7,6},{8,9},{9,8},{10,11... | collective-permute-start | bytes 589832 | tf_op jit(solution)/shard_map/ppermute | solution.py:66
  25.6 6.0 %collective-permute-start.9 = (f32[32,384]{1,0:T(8,128)S(1)}, f32[32,384]{1,0:T(8,128)S(1)}, u32[]{:S(2)}, u32[]{:S(2)}) collective-permute-start(f32[32,384]{1,0:T(8,128)S(1)} %fusion.2), channel_id=1, source_target_pairs={{0,6},{1,7},{2,4},{3,5},{4,2},{5,3},{6,0},{7,1},{8,14},{9,15},{10,... | collective-permute-start | bytes 147464 | tf_op jit(solution)/shard_map/ppermute | solution.py:66
  31.5 25.5 %collective-permute-start.19 = (f32[128,384]{1,0:T(8,128)S(1)}, f32[128,384]{1,0:T(8,128)S(1)}, u32[]{:S(2)}, u32[]{:S(2)}) collective-permute-start(f32[128,384]{1,0:T(8,128)S(1)} %get-tuple-element.120), channel_id=1, source_target_pairs={{0,24},{1,25},{2,26},{3,27},{4,28},{5,29},{6,30},{7,31},{8,16},{9,... | collective-permute-start | bytes 589832 | tf_op jit(solution)/shard_map/ppermute | solution.py:66
  37.3 11.6 %collective-permute-start.11 = (f32[32,1536]{1,0:T(8,128)S(1)}, f32[32,1536]{1,0:T(8,128)S(1)}, u32[]{:S(2)}, u32[]{:S(2)}) collective-permute-start(f32[32,1536]{1,0:T(8,128)S(1)} %pad_maximum_fusion.10), channel_id=1, source_target_pairs={{0,16},{1,17},{2,18},{3,19},{4,20},{5,21},{6,22},{7,23},{8,24},{9,... | collective-permute-start | bytes 589832 | tf_op jit(solution)/shard_map/ppermute | solution.py:66
  38.5 10.5 %collective-permute-start.13 = (f32[32,1536]{1,0:T(8,128)S(1)}, f32[32,1536]{1,0:T(8,128)S(1)}, u32[]{:S(2)}, u32[]{:S(2)}) collective-permute-start(f32[32,1536]{1,0:T(8,128)S(1)} %pad_maximum_fusion.10), channel_id=1, source_target_pairs={{0,17},{1,16},{2,19},{3,18},{4,21},{5,20},{6,23},{7,22},{8,25},{9,... | collective-permute-start | bytes 589832 | tf_op jit(solution)/shard_map/ppermute | solution.py:66
  40.4 9.8 %collective-permute-start.12 = (f32[32,1536]{1,0:T(8,128)S(1)}, f32[32,1536]{1,0:T(8,128)S(1)}, u32[]{:S(2)}, u32[]{:S(2)}) collective-permute-start(f32[32,1536]{1,0:T(8,128)S(1)} %pad_maximum_fusion.10), channel_id=1, source_target_pairs={{0,1},{1,0},{2,3},{3,2},{4,5},{5,4},{6,7},{7,6},{8,9},{9,8},{10,11... | collective-permute-start | bytes 589832 | tf_op jit(solution)/shard_map/ppermute | solution.py:66
  50.3 6.4 %collective-permute-start.16 = (f32[64,1536]{1,0:T(8,128)S(1)}, f32[64,1536]{1,0:T(8,128)S(1)}, u32[]{:S(2)}, u32[]{:S(2)}) collective-permute-start(f32[64,1536]{1,0:T(8,128)S(1)} %pad_maximum_fusion.4.near_ref), channel_id=1, source_target_pairs={{0,8},{1,9},{2,10},{3,11},{4,12},{5,13},{6,14},{7,15},{8,0},{9,1},... | collective-permute-start | bytes 1179656 | tf_op jit(solution)/shard_map/ppermute | solution.py:66
  50.4 6.3 %collective-permute-start.17 = (f32[64,1536]{1,0:T(8,128)S(1)}, f32[64,1536]{1,0:T(8,128)S(1)}, u32[]{:S(2)}, u32[]{:S(2)}) collective-permute-start(f32[64,1536]{1,0:T(8,128)S(1)} %pad_maximum_fusion.5.far_ref), channel_id=1, source_target_pairs={{0,8},{1,9},{2,10},{3,11},{4,12},{5,13},{6,14},{7,15},{8,0},{9,1},... | collective-permute-start | bytes 1179656 | tf_op jit(solution)/shard_map/ppermute | solution.py:66
  57.1 6.3 %collective-permute-start.22 = (f32[32,384]{1,0:T(8,128)S(1)}, f32[32,384]{1,0:T(8,128)S(1)}, u32[]{:S(2)}, u32[]{:S(2)}) collective-permute-start(f32[32,384]{1,0:T(8,128)S(1)} %broadcast_select_fusion.13), channel_id=1, source_target_pairs={{0,6},{1,7},{2,4},{3,5},{4,2},{5,3},{6,0},{7,1},{8,14},{9,15},{10,... | collective-permute-start | bytes 147464 | tf_op jit(solution)/shard_map/ppermute | solution.py:66
  59.0 5.4 %collective-permute-start.20 = (f32[32,384]{1,0:T(8,128)S(1)}, f32[32,384]{1,0:T(8,128)S(1)}, u32[]{:S(2)}, u32[]{:S(2)}) collective-permute-start(f32[32,384]{1,0:T(8,128)S(1)} %broadcast_select_fusion.13), channel_id=1, source_target_pairs={{0,2},{1,3},{2,0},{3,1},{4,6},{5,7},{6,4},{7,5},{8,10},{9,11},{10,... | collective-permute-start | bytes 147464 | tf_op jit(solution)/shard_map/ppermute | solution.py:66
  64.4 5.7 %collective-permute-start.23 = (f32[32,1536]{1,0:T(8,128)S(1)}, f32[32,1536]{1,0:T(8,128)S(1)}, u32[]{:S(2)}, u32[]{:S(2)}) collective-permute-start(f32[32,1536]{1,0:T(8,128)S(1)} %pad_maximum_fusion.11), channel_id=1, source_target_pairs={{0,1},{1,0},{2,3},{3,2},{4,5},{5,4},{6,7},{7,6},{8,9},{9,8},{10,11... | collective-permute-start | bytes 589832 | tf_op jit(solution)/shard_map/ppermute | solution.py:66
  66.0 31.8 %collective-permute-start.34 = (f32[128,384]{1,0:T(8,128)S(1)}, f32[128,384]{1,0:T(8,128)S(1)}, u32[]{:S(2)}, u32[]{:S(2)}) collective-permute-start(f32[128,384]{1,0:T(8,128)S(1)} %field.4), channel_id=1, source_target_pairs={{0,8},{1,9},{2,10},{3,11},{4,12},{5,13},{6,14},{7,15},{8,0},{9,1},... | collective-permute-start | bytes 589832 | tf_op jit(solution)/shard_map/ppermute | solution.py:66
  66.0 31.8 %collective-permute-start.35 = (f32[128,384]{1,0:T(8,128)S(1)}, f32[128,384]{1,0:T(8,128)S(1)}, u32[]{:S(2)}, u32[]{:S(2)}) collective-permute-start(f32[128,384]{1,0:T(8,128)S(1)} %field.4), channel_id=1, source_target_pairs={{0,24},{1,25},{2,26},{3,27},{4,28},{5,29},{6,30},{7,31},{8,16},{9,... | collective-permute-start | bytes 589832 | tf_op jit(solution)/shard_map/ppermute | solution.py:66
  71.2 6.0 %collective-permute-start.26 = (f32[32,384]{1,0:T(8,128)S(1)}, f32[32,384]{1,0:T(8,128)S(1)}, u32[]{:S(2)}, u32[]{:S(2)}) collective-permute-start(f32[32,384]{1,0:T(8,128)S(1)} %fusion.1), channel_id=1, source_target_pairs={{0,6},{1,7},{2,4},{3,5},{4,2},{5,3},{6,0},{7,1},{8,14},{9,15},{10,... | collective-permute-start | bytes 147464 | tf_op jit(solution)/shard_map/ppermute | solution.py:66
  73.2 5.7 %collective-permute-start.25 = (f32[32,384]{1,0:T(8,128)S(1)}, f32[32,384]{1,0:T(8,128)S(1)}, u32[]{:S(2)}, u32[]{:S(2)}) collective-permute-start(f32[32,384]{1,0:T(8,128)S(1)} %fusion.1), channel_id=1, source_target_pairs={{0,4},{1,5},{2,6},{3,7},{4,0},{5,1},{6,2},{7,3},{8,12},{9,13},{10,... | collective-permute-start | bytes 147464 | tf_op jit(solution)/shard_map/ppermute | solution.py:66
  79.0 10.7 %collective-permute-start.27 = (f32[32,1536]{1,0:T(8,128)S(1)}, f32[32,1536]{1,0:T(8,128)S(1)}, u32[]{:S(2)}, u32[]{:S(2)}) collective-permute-start(f32[32,1536]{1,0:T(8,128)S(1)} %pad_maximum_fusion.12), channel_id=1, source_target_pairs={{0,16},{1,17},{2,18},{3,19},{4,20},{5,21},{6,22},{7,23},{8,24},{9,... | collective-permute-start | bytes 589832 | tf_op jit(solution)/shard_map/ppermute | solution.py:66
  80.1 9.6 %collective-permute-start.29 = (f32[32,1536]{1,0:T(8,128)S(1)}, f32[32,1536]{1,0:T(8,128)S(1)}, u32[]{:S(2)}, u32[]{:S(2)}) collective-permute-start(f32[32,1536]{1,0:T(8,128)S(1)} %pad_maximum_fusion.12), channel_id=1, source_target_pairs={{0,17},{1,16},{2,19},{3,18},{4,21},{5,20},{6,23},{7,22},{8,25},{9,... | collective-permute-start | bytes 589832 | tf_op jit(solution)/shard_map/ppermute | solution.py:66
  81.6 9.3 %collective-permute-start.28 = (f32[32,1536]{1,0:T(8,128)S(1)}, f32[32,1536]{1,0:T(8,128)S(1)}, u32[]{:S(2)}, u32[]{:S(2)}) collective-permute-start(f32[32,1536]{1,0:T(8,128)S(1)} %pad_maximum_fusion.12), channel_id=1, source_target_pairs={{0,1},{1,0},{2,3},{3,2},{4,5},{5,4},{6,7},{7,6},{8,9},{9,8},{10,11... | collective-permute-start | bytes 589832 | tf_op jit(solution)/shard_map/ppermute | solution.py:66
  91.0 6.4 %collective-permute-start.32 = (f32[64,1536]{1,0:T(8,128)S(1)}, f32[64,1536]{1,0:T(8,128)S(1)}, u32[]{:S(2)}, u32[]{:S(2)}) collective-permute-start(f32[64,1536]{1,0:T(8,128)S(1)} %pad_maximum_fusion.6.near_ref), channel_id=1, source_target_pairs={{0,8},{1,9},{2,10},{3,11},{4,12},{5,13},{6,14},{7,15},{8,0},{9,1},... | collective-permute-start | bytes 1179656 | tf_op jit(solution)/shard_map/ppermute | solution.py:66
  91.1 6.3 %collective-permute-start.33 = (f32[64,1536]{1,0:T(8,128)S(1)}, f32[64,1536]{1,0:T(8,128)S(1)}, u32[]{:S(2)}, u32[]{:S(2)}) collective-permute-start(f32[64,1536]{1,0:T(8,128)S(1)} %pad_maximum_fusion.7.far_ref), channel_id=1, source_target_pairs={{0,8},{1,9},{2,10},{3,11},{4,12},{5,13},{6,14},{7,15},{8,0},{9,1},... | collective-permute-start | bytes 1179656 | tf_op jit(solution)/shard_map/ppermute | solution.py:66
  97.8 6.4 %collective-permute-start.38 = (f32[32,384]{1,0:T(8,128)S(1)}, f32[32,384]{1,0:T(8,128)S(1)}, u32[]{:S(2)}, u32[]{:S(2)}) collective-permute-start(f32[32,384]{1,0:T(8,128)S(1)} %broadcast_select_fusion.12), channel_id=1, source_target_pairs={{0,6},{1,7},{2,4},{3,5},{4,2},{5,3},{6,0},{7,1},{8,14},{9,15},{10,... | collective-permute-start | bytes 147464 | tf_op jit(solution)/shard_map/ppermute | solution.py:66
  105.4 5.7 %collective-permute-start.39 = (f32[32,1536]{1,0:T(8,128)S(1)}, f32[32,1536]{1,0:T(8,128)S(1)}, u32[]{:S(2)}, u32[]{:S(2)}) collective-permute-start(f32[32,1536]{1,0:T(8,128)S(1)} %pad_maximum_fusion.13), channel_id=1, source_target_pairs={{0,1},{1,0},{2,3},{3,2},{4,5},{5,4},{6,7},{7,6},{8,9},{9,8},{10,11... | collective-permute-start | bytes 589832 | tf_op jit(solution)/shard_map/ppermute | solution.py:66
  112.2 6.0 %collective-permute-start.42 = (f32[32,384]{1,0:T(8,128)S(1)}, f32[32,384]{1,0:T(8,128)S(1)}, u32[]{:S(2)}, u32[]{:S(2)}) collective-permute-start(f32[32,384]{1,0:T(8,128)S(1)} %fusion), channel_id=1, source_target_pairs={{0,6},{1,7},{2,4},{3,5},{4,2},{5,3},{6,0},{7,1},{8,14},{9,15},{10,... | collective-permute-start | bytes 147464 | tf_op jit(solution)/shard_map/ppermute | solution.py:66
  113.9 5.5 %collective-permute-start.41 = (f32[32,384]{1,0:T(8,128)S(1)}, f32[32,384]{1,0:T(8,128)S(1)}, u32[]{:S(2)}, u32[]{:S(2)}) collective-permute-start(f32[32,384]{1,0:T(8,128)S(1)} %fusion), channel_id=1, source_target_pairs={{0,4},{1,5},{2,6},{3,7},{4,0},{5,1},{6,2},{7,3},{8,12},{9,13},{10,... | collective-permute-start | bytes 147464 | tf_op jit(solution)/shard_map/ppermute | solution.py:66
  116.6 6.5 %collective-permute-start.49 = (f32[128,384]{1,0:T(8,128)S(1)}, f32[128,384]{1,0:T(8,128)S(1)}, u32[]{:S(2)}, u32[]{:S(2)}) collective-permute-start(f32[128,384]{1,0:T(8,128)S(1)} %field.6), channel_id=1, source_target_pairs={{0,24},{1,25},{2,26},{3,27},{4,28},{5,29},{6,30},{7,31},{8,16},{9,... | collective-permute-start | bytes 589832 | tf_op jit(solution)/shard_map/ppermute | solution.py:66
  119.4 8.6 %collective-permute-start.43 = (f32[32,1536]{1,0:T(8,128)S(1)}, f32[32,1536]{1,0:T(8,128)S(1)}, u32[]{:S(2)}, u32[]{:S(2)}) collective-permute-start(f32[32,1536]{1,0:T(8,128)S(1)} %pad_maximum_fusion.14), channel_id=1, source_target_pairs={{0,16},{1,17},{2,18},{3,19},{4,20},{5,21},{6,22},{7,23},{8,24},{9,... | collective-permute-start | bytes 589832 | tf_op jit(solution)/shard_map/ppermute | solution.py:66
  123.2 7.6 %collective-permute-start.44 = (f32[32,1536]{1,0:T(8,128)S(1)}, f32[32,1536]{1,0:T(8,128)S(1)}, u32[]{:S(2)}, u32[]{:S(2)}) collective-permute-start(f32[32,1536]{1,0:T(8,128)S(1)} %pad_maximum_fusion.14), channel_id=1, source_target_pairs={{0,1},{1,0},{2,3},{3,2},{4,5},{5,4},{6,7},{7,6},{8,9},{9,8},{10,11... | collective-permute-start | bytes 589832 | tf_op jit(solution)/shard_map/ppermute | solution.py:66
  123.7 11.7 %collective-permute-start.45 = (f32[32,1536]{1,0:T(8,128)S(1)}, f32[32,1536]{1,0:T(8,128)S(1)}, u32[]{:S(2)}, u32[]{:S(2)}) collective-permute-start(f32[32,1536]{1,0:T(8,128)S(1)} %pad_maximum_fusion.14), channel_id=1, source_target_pairs={{0,17},{1,16},{2,19},{3,18},{4,21},{5,20},{6,23},{7,22},{8,25},{9,... | collective-permute-start | bytes 589832 | tf_op jit(solution)/shard_map/ppermute | solution.py:66
  128.1 7.6 %collective-permute-start.46 = (f32[64,1536]{1,0:T(8,128)S(1)}, f32[64,1536]{1,0:T(8,128)S(1)}, u32[]{:S(2)}, u32[]{:S(2)}) collective-permute-start(f32[64,1536]{1,0:T(8,128)S(1)} %pad_maximum_fusion.8), channel_id=1, source_target_pairs={{0,8},{1,9},{2,10},{3,11},{4,12},{5,13},{6,14},{7,15},{8,0},{9,1},... | collective-permute-start | bytes 1179656 | tf_op jit(solution)/shard_map/ppermute | solution.py:66
  (21 other events, 106.3 us)

commit v3 on v2

--- a/solution.py
+++ b/solution.py
@@ -285,8 +285,13 @@
     cut = len(near) * height
     order = r ^ jnp.array(steps, jnp.int32)
 
+    tie = lax.optimization_barrier
+
     def line(v):
-        return jnp.concatenate([v] + [swap(v, 0, k) for k in near[1:]], 1)
+        parts = [v]
+        for k in near[1:]:
+            parts.append(swap(v, 0, k))
+        return jnp.concatenate(parts, 1)
 
     def scatter(rhs):
         parts = [rhs[j * width : (j + 1) * width] for j in range(4)]
@@ -294,7 +299,9 @@
         return lax.select_n(g, *got)
 
     def exchange(a):
-        near_y, far_y, far = swap(a, 2, 0), swap(a, 2, 1), swap(a, 0, 1)
+        near_y = swap(a, 2, 0)
+        far_y = swap(a, 2, 1)
+        far = swap(a, 0, 1)
         return jnp.concatenate([a, near_y], 0), jnp.concatenate([far, far_y], 0)
 
     def full(near_, far_):
@@ -319,7 +326,6 @@
     def pair(array):
         return jnp.where(first_core, pick(array, 0), swap(pick(array, 1), 1, 0))
 
-    tie = lax.optimization_barrier
     keep = functools.partial(pltpu.with_memory_space_constraint, memory_space=pltpu.HBM)
     acc0, rhs = turn_first(keep(history), keep(loads))
     rhs, first_plane, first_core, g = tie((rhs, first_plane, first_core, g))
@@ -335,11 +341,13 @@
             a = line(rhs)
             a, inv = tie((a, inv))
             acc1, given = turn(history, loads)
+            a, order = tie((a, order))
+            own1 = split_blocks(keep(lag_ops), order, 1)
             b = swap(a, 0, 1)
-            b, acc1, given = tie((b, acc1, given))
+            b, acc1, given, own1 = tie((b, acc1, given, own1))
         else:
             current = full(near_, far_)
-            rhs, current, received = tie((rhs, current, received))
+            rhs, received = tie((rhs, received))
             below = choose(received)
             new0 = field(own0, current, acc1)
             a = line(rhs)
@@ -348,21 +356,18 @@
             b = swap(a, 0, 1)
             b, acc1 = tie((b, acc1))
         received = behind(acc0)
-        solved = product(split(a), inv[0]) + product(split(b), inv[1])
-        if step == 0:
-            solved, order, which = tie((solved, order, which))
-            first = split_blocks(keep(lag_ops), order, 0, which, keep(other_ops))
+        solved = field(inv[1], b, product(split(a), inv[0]))
         a = line(solved)
         if step < STEPS - 1:
             led = pair(acc1)
             rest = jnp.where(first_core, pick(given[step], 0), pick(given[step], 1)) - led
         if step == 0:
-            a, first, order = tie((a, first, order))
+            a, order, which = tie((a, order, which))
+            first = split_blocks(keep(lag_ops), order, 0, which, keep(other_ops))
             own0 = split_blocks(keep(lag_ops), order, 0)
-            own1 = split_blocks(keep(lag_ops), order, 1)
         near_, far_ = exchange(a)
         if step == 0:
-            near_, far_, own0, own1 = tie((near_, far_, own0, own1))
+            near_, far_, own0, first = tie((near_, far_, own0, first))
         if step < STEPS - 1:
             near_, far_, rest = tie((near_, far_, rest))
             mine, theirs = lead(first, near_, far_, rest)

time: 141 us -> 153 us (1.085)
  waiting for transfers between devices: 54.6 us -> 66.8 us
  matrix products: 5.98 us -> 2.99 us
  Pallas kernels: 26.5 us -> 29.1 us
    ppermute x50, waiting for transfers between devices: 54.6 us -> 66.8 us  [swap(): return lax.ppermute(array, AXES, pairs)]
    dot_general x12 -> x6, matrix products: 5.98 us -> 2.99 us  [contract(): lax.dot_general(a, b, (((1,), (1,)), ((), ())), preferred_element_type=jn...]
    pallas_call x4 -> x7, Pallas kernels: 6.27 us -> 8.89 us  [field(): pl.pallas_call(field_kernel, out_shape=jax.ShapeDtypeStruct((n, high.shap...]
  transfers between devices with their start and end apart: 50 -> 50, of which waited for: 27 -> 25; matrix products, arithmetic and copies ran while one was open for 5% -> 3% of each run, Pallas kernels for 15% -> 13%
where the time goes in v3:
time: 153 us; the launch traced here: 152 us
  waiting for transfers between devices  66.8 us (44%)
  starting transfers between devices  50 us (33%)
  Pallas kernels  29.1 us (19%)
  matrix products  2.99 us (2%)
    ppermute x50, waiting for transfers between devices, swap(): return lax.ppermute(array, AXES, pairs)  66.8 us
    ppermute x50, starting transfers between devices, swap(): return lax.ppermute(array, AXES, pairs)  50 us
    pallas_call x4, Pallas kernels, split_blocks(): pl.pallas_call(functools.partial(split_kernel, lag, pick is not None), ou...  12.2 us
    pallas_call x7, Pallas kernels, field(): pl.pallas_call(field_kernel, out_shape=jax.ShapeDtypeStruct((n, high.shap...  8.89 us
    pallas_call x1, Pallas kernels, last(): pl.pallas_call(last_kernel, out_shape=(jax.ShapeDtypeStruct((rows, n), jn...  3.43 us
  transfers between devices with their start and end apart: 50, of which 25 were waited for; matrix products, arithmetic and copies ran while one was open for 3% of the time, Pallas kernels for 13%

profile of v3, /device:TPU:0, one launch (start us, length us, event | category | flops | bytes accessed | tf_op | source)
XLA Modules:
  0.0 152.4 jit_solution(11672853561093150828)
XLA Ops:
  2.5 2.6 %collective-permute-start.1 = (f32[32,384]{1,0:T(8,128)S(1)}, f32[32,384]{1,0:T(8,128)S(1)}, u32[]{:S(2)}, u32[]{:S(2)}) collective-permute-start(f32[32,384]{1,0:T(8,128)S(1)} %get-tuple-element.180), channel_id=1, source_target_pairs={{0,16},{1,17},{2,18},{3,19},{4,20},{5,21},{6,22},{7,23},{8,24},{9,... | collective-permute-start | bytes 147464 | tf_op jit(solution)/shard_map/ppermute | solution.py:66
  5.2 2.3 %collective-permute-done.1 = f32[32,384]{1,0:T(8,128)S(1)} collective-permute-done((f32[32,384]{1,0:T(8,128)S(1)}, f32[32,384]{1,0:T(8,128)S(1)}, u32[]{:S(2)}, u32[]{:S(2)}) %collective-permute-start.1) | collective-permute-done | bytes 49184 | tf_op jit(solution)/shard_map/ppermute | solution.py:66
  11.0 2.6 %collective-permute-start.4 = (f32[32,384]{1,0:T(8,128)S(1)}, f32[32,384]{1,0:T(8,128)S(1)}, u32[]{:S(2)}, u32[]{:S(2)}) collective-permute-start(f32[32,384]{1,0:T(8,128)S(1)} %select_select_fusion.3), channel_id=1, source_target_pairs={{0,4},{1,5},{2,6},{3,7},{4,0},{5,1},{6,2},{7,3},{8,12},{9,13},{10,... | collective-permute-start | bytes 147464 | tf_op jit(solution)/shard_map/ppermute | solution.py:66
  13.8 3.1 %split_blocks.4 = (bf16[384,3072]{1,0:T(8,128)(2,1)S(1)}, bf16[384,3072]{1,0:T(8,128)(2,1)S(1)}) custom-call(s32[8]{0:T(128)S(1)} %broadcast_xor_fusion.order_ref, f32[384,3072]{1,0:T(8,128)} %refs_0_.3), custom_call_target="tpu_custom_call" | custom-call | bytes 9437184 | tf_op jit(solution)/shard_map/split_blocks/pallas_call | solution.py:181
  17.3 2.1 %collective-permute-done.5 = f32[32,384]{1,0:T(8,128)S(1)} collective-permute-done((f32[32,384]{1,0:T(8,128)S(1)}, f32[32,384]{1,0:T(8,128)S(1)}, u32[]{:S(2)}, u32[]{:S(2)}) %collective-permute-start.5) | collective-permute-done | bytes 49184 | tf_op jit(solution)/shard_map/ppermute | solution.py:66
  19.5 3.1 %split_blocks.5 = (bf16[384,3072]{1,0:T(8,128)(2,1)S(1)}, bf16[384,3072]{1,0:T(8,128)(2,1)S(1)}) custom-call(s32[8]{0:T(128)S(1)} %broadcast_xor_fusion.order_ref, f32[2,384,3072]{2,1,0:T(8,128)} %refs_1_.1), custom_call_target="tpu_custom_call" | custom-call | bytes 9437184 | tf_op jit(solution)/shard_map/split_blocks/pallas_call | solution.py:181
  25.1 3.1 %collective-permute-done.6.v_ref = f32[32,1536]{1,0:T(8,128)S(1)} collective-permute-done((f32[32,1536]{1,0:T(8,128)S(1)}, f32[32,1536]{1,0:T(8,128)S(1)}, u32[]{:S(2)}, u32[]{:S(2)}) %collective-permute-start.6) | collective-permute-done | bytes 196640 | tf_op jit(solution)/shard_map/ppermute | solution.py:66
  29.4 3.5 %collective-permute-start.8 = (f32[32,384]{1,0:T(8,128)S(1)}, f32[32,384]{1,0:T(8,128)S(1)}, u32[]{:S(2)}, u32[]{:S(2)}) collective-permute-start(f32[32,384]{1,0:T(8,128)S(1)} %field.7), channel_id=1, source_target_pairs={{0,4},{1,5},{2,6},{3,7},{4,0},{5,1},{6,2},{7,3},{8,12},{9,13},{10,... | collective-permute-start | bytes 147464 | tf_op jit(solution)/shard_map/ppermute | solution.py:66
  33.7 2.2 %collective-permute-done.8 = f32[32,384]{1,0:T(8,128)S(1)} collective-permute-done((f32[32,384]{1,0:T(8,128)S(1)}, f32[32,384]{1,0:T(8,128)S(1)}, u32[]{:S(2)}, u32[]{:S(2)}) %collective-permute-start.8) | collective-permute-done | bytes 49184 | tf_op jit(solution)/shard_map/ppermute | solution.py:66
  35.9 2.8 %collective-permute-done.9 = f32[32,384]{1,0:T(8,128)S(1)} collective-permute-done((f32[32,384]{1,0:T(8,128)S(1)}, f32[32,384]{1,0:T(8,128)S(1)}, u32[]{:S(2)}, u32[]{:S(2)}) %collective-permute-start.9) | collective-permute-done | bytes 49184 | tf_op jit(solution)/shard_map/ppermute | solution.py:66
  38.8 3.1 %split_blocks.6 = (bf16[384,3072]{1,0:T(8,128)(2,1)S(1)}, bf16[384,3072]{1,0:T(8,128)(2,1)S(1)}) custom-call(s32[8]{0:T(128)S(1)} %broadcast_xor_fusion.order_ref, f32[2,384,3072]{2,1,0:T(8,128)} %refs_1_.1), custom_call_target="tpu_custom_call" | custom-call | bytes 9437184 | tf_op jit(solution)/shard_map/split_blocks/pallas_call | solution.py:181
  44.5 4.6 %collective-permute-done.10 = f32[32,1536]{1,0:T(8,128)S(1)} collective-permute-done((f32[32,1536]{1,0:T(8,128)S(1)}, f32[32,1536]{1,0:T(8,128)S(1)}, u32[]{:S(2)}, u32[]{:S(2)}) %collective-permute-start.10) | collective-permute-done | bytes 196640 | tf_op jit(solution)/shard_map/ppermute | solution.py:66
  50.2 5.5 %collective-permute-done.12 = f32[32,1536]{1,0:T(8,128)S(1)} collective-permute-done((f32[32,1536]{1,0:T(8,128)S(1)}, f32[32,1536]{1,0:T(8,128)S(1)}, u32[]{:S(2)}, u32[]{:S(2)}) %collective-permute-start.12) | collective-permute-done | bytes 196640 | tf_op jit(solution)/shard_map/ppermute | solution.py:66
  55.7 3.1 %split_blocks.7 = (bf16[384,3072]{1,0:T(8,128)(2,1)S(1)}, bf16[384,3072]{1,0:T(8,128)(2,1)S(1)}) custom-call(s32[8]{0:T(128)S(1)} %broadcast_xor_fusion.order_ref, s32[1]{0:T(128)} %bitcast.refs_0_, f32[2,384,3072]{2,1,0:T(8,128)} %refs_1_.1, f32[2,384,3072]{2,1,0:T(8,128)} %collective-permute-done.13.refs_2_), custom_call_target="tpu_custom_call" | custom-call | bytes 9437184 | tf_op jit(solution)/shard_map/split_blocks/pallas_call | solution.py:181
  62.1 3.0 %collective-permute-done.15 = f32[32,384]{1,0:T(8,128)S(1)} collective-permute-done((f32[32,384]{1,0:T(8,128)S(1)}, f32[32,384]{1,0:T(8,128)S(1)}, u32[]{:S(2)}, u32[]{:S(2)}) %collective-permute-start.15) | collective-permute-done | bytes 49184 | tf_op jit(solution)/shard_map/ppermute | solution.py:66
  66.5 3.0 %collective-permute-start.20 = (f32[32,384]{1,0:T(8,128)S(1)}, f32[32,384]{1,0:T(8,128)S(1)}, u32[]{:S(2)}, u32[]{:S(2)}) collective-permute-start(f32[32,384]{1,0:T(8,128)S(1)} %broadcast_select_fusion.13), channel_id=1, source_target_pairs={{0,6},{1,7},{2,4},{3,5},{4,2},{5,3},{6,0},{7,1},{8,14},{9,15},{10,... | collective-permute-start | bytes 147464 | tf_op jit(solution)/shard_map/ppermute | solution.py:66
  76.8 1.7 %field.9.base_ref = f32[128,384]{1,0:T(8,128)S(1)} custom-call(bf16[384,3072]{1,0:T(8,128)(2,1)S(1)} %get-tuple-element.103.high_ref.h1_ref, bf16[384,3072]{1,0:T(8,128)(2,1)S(1)} %get-tuple-element.104.low_ref.l1_ref, f32[128,3072]{1,0:T(8,128)S(1)} %pad_maximum_fusion.v_ref, f32[128,384]{1,0:T(8,128)S(1)} %select_select_fusion.2.base_ref), custom_call_target="tpu_custom_call" | custom-call | flops 905969664 | bytes 4718592 | tf_op jit(solution)/shard_map/field/pallas_call | solution.py:217
  81.0 3.5 %collective-permute-start.25 = (f32[32,384]{1,0:T(8,128)S(1)}, f32[32,384]{1,0:T(8,128)S(1)}, u32[]{:S(2)}, u32[]{:S(2)}) collective-permute-start(f32[32,384]{1,0:T(8,128)S(1)} %field.10), channel_id=1, source_target_pairs={{0,4},{1,5},{2,6},{3,7},{4,0},{5,1},{6,2},{7,3},{8,12},{9,13},{10,... | collective-permute-start | bytes 147464 | tf_op jit(solution)/shard_map/ppermute | solution.py:66
  86.7 3.8 %collective-permute-done.26 = f32[32,384]{1,0:T(8,128)S(1)} collective-permute-done((f32[32,384]{1,0:T(8,128)S(1)}, f32[32,384]{1,0:T(8,128)S(1)}, u32[]{:S(2)}, u32[]{:S(2)}) %collective-permute-start.26) | collective-permute-done | bytes 49184 | tf_op jit(solution)/shard_map/ppermute | solution.py:66
  91.1 2.0 %collective-permute-start.29 = (f32[32,1536]{1,0:T(8,128)S(1)}, f32[32,1536]{1,0:T(8,128)S(1)}, u32[]{:S(2)}, u32[]{:S(2)}) collective-permute-start(f32[32,1536]{1,0:T(8,128)S(1)} %pad_maximum_fusion.12), channel_id=1, source_target_pairs={{0,17},{1,16},{2,19},{3,18},{4,21},{5,20},{6,23},{7,22},{8,25},{9,... | collective-permute-start | bytes 589832 | tf_op jit(solution)/shard_map/ppermute | solution.py:66
  94.1 6.9 %collective-permute-done.27 = f32[32,1536]{1,0:T(8,128)S(1)} collective-permute-done((f32[32,1536]{1,0:T(8,128)S(1)}, f32[32,1536]{1,0:T(8,128)S(1)}, u32[]{:S(2)}, u32[]{:S(2)}) %collective-permute-start.27) | collective-permute-done | bytes 196640 | tf_op jit(solution)/shard_map/ppermute | solution.py:66
  104.2 3.1 %collective-permute-done.31 = f32[32,384]{1,0:T(8,128)S(1)} collective-permute-done((f32[32,384]{1,0:T(8,128)S(1)}, f32[32,384]{1,0:T(8,128)S(1)}, u32[]{:S(2)}, u32[]{:S(2)}) %collective-permute-start.31) | collective-permute-done | bytes 49184 | tf_op jit(solution)/shard_map/ppermute | solution.py:66
  107.4 1.7 %collective-permute-start.35 = (f32[32,384]{1,0:T(8,128)S(1)}, f32[32,384]{1,0:T(8,128)S(1)}, u32[]{:S(2)}, u32[]{:S(2)}) collective-permute-start(f32[32,384]{1,0:T(8,128)S(1)} %broadcast_select_fusion.12), channel_id=1, source_target_pairs={{0,4},{1,5},{2,6},{3,7},{4,0},{5,1},{6,2},{7,3},{8,12},{9,13},{10,... | collective-permute-start | bytes 147464 | tf_op jit(solution)/shard_map/ppermute | solution.py:66
  109.2 2.6 %collective-permute-start.36 = (f32[32,384]{1,0:T(8,128)S(1)}, f32[32,384]{1,0:T(8,128)S(1)}, u32[]{:S(2)}, u32[]{:S(2)}) collective-permute-start(f32[32,384]{1,0:T(8,128)S(1)} %broadcast_select_fusion.12), channel_id=1, source_target_pairs={{0,6},{1,7},{2,4},{3,5},{4,2},{5,3},{6,0},{7,1},{8,14},{9,15},{10,... | collective-permute-start | bytes 147464 | tf_op jit(solution)/shard_map/ppermute | solution.py:66
  113.0 2.1 %collective-permute-done.36 = f32[32,384]{1,0:T(8,128)S(1)} collective-permute-done((f32[32,384]{1,0:T(8,128)S(1)}, f32[32,384]{1,0:T(8,128)S(1)}, u32[]{:S(2)}, u32[]{:S(2)}) %collective-permute-start.36) | collective-permute-done | bytes 49184 | tf_op jit(solution)/shard_map/ppermute | solution.py:66
  120.6 2.2 %collective-permute-done.39.v_ref = f32[32,1536]{1,0:T(8,128)S(1)} collective-permute-done((f32[32,1536]{1,0:T(8,128)S(1)}, f32[32,1536]{1,0:T(8,128)S(1)}, u32[]{:S(2)}, u32[]{:S(2)}) %collective-permute-start.39) | collective-permute-done | bytes 196640 | tf_op jit(solution)/shard_map/ppermute | solution.py:66
  123.7 3.2 %collective-permute-start.41 = (f32[32,384]{1,0:T(8,128)S(1)}, f32[32,384]{1,0:T(8,128)S(1)}, u32[]{:S(2)}, u32[]{:S(2)}) collective-permute-start(f32[32,384]{1,0:T(8,128)S(1)} %field.13), channel_id=1, source_target_pairs={{0,4},{1,5},{2,6},{3,7},{4,0},{5,1},{6,2},{7,3},{8,12},{9,13},{10,... | collective-permute-start | bytes 147464 | tf_op jit(solution)/shard_map/ppermute | solution.py:66
  129.2 3.6 %collective-permute-done.42 = f32[32,384]{1,0:T(8,128)S(1)} collective-permute-done((f32[32,384]{1,0:T(8,128)S(1)}, f32[32,384]{1,0:T(8,128)S(1)}, u32[]{:S(2)}, u32[]{:S(2)}) %collective-permute-start.42) | collective-permute-done | bytes 49184 | tf_op jit(solution)/shard_map/ppermute | solution.py:66
  137.1 2.4 %collective-permute-done.43 = f32[32,1536]{1,0:T(8,128)S(1)} collective-permute-done((f32[32,1536]{1,0:T(8,128)S(1)}, f32[32,1536]{1,0:T(8,128)S(1)}, u32[]{:S(2)}, u32[]{:S(2)}) %collective-permute-start.43) | collective-permute-done | bytes 196640 | tf_op jit(solution)/shard_map/ppermute | solution.py:66
  139.6 2.6 %collective-permute-done.44 = f32[32,1536]{1,0:T(8,128)S(1)} collective-permute-done((f32[32,1536]{1,0:T(8,128)S(1)}, f32[32,1536]{1,0:T(8,128)S(1)}, u32[]{:S(2)}, u32[]{:S(2)}) %collective-permute-start.44) | collective-permute-done | bytes 196640 | tf_op jit(solution)/shard_map/ppermute | solution.py:66
  142.3 4.6 %collective-permute-done.45 = f32[32,1536]{1,0:T(8,128)S(1)} collective-permute-done((f32[32,1536]{1,0:T(8,128)S(1)}, f32[32,1536]{1,0:T(8,128)S(1)}, u32[]{:S(2)}, u32[]{:S(2)}) %collective-permute-start.45) | collective-permute-done | bytes 196640 | tf_op jit(solution)/shard_map/ppermute | solution.py:66
  149.0 3.4 %last.1 = (f32[384,128]{1,0:T(8,128)}, f32[2,384,128]{2,1,0:T(8,128)}) custom-call(bf16[384,3072]{1,0:T(8,128)(2,1)S(1)} %get-tuple-element.101.high_ref.h0_ref, bf16[384,3072]{1,0:T(8,128)(2,1)S(1)} %get-tuple-element.102.low_ref.l0_ref, bf16[384,3072]{1,0:T(8,128)(2,1)S(1)} %get-tuple-element.103.high_ref.h1_ref, ...), custom_call_target="tpu_custom_call" | custom-call | flops 1811939328 | bytes 9437184 | tf_op jit(solution)/shard_map/last/pallas_call | solution.py:262
  (145 shorter events, 52.1 us)
Async XLA Ops:
  8.8 46.9 %collective-permute-start.13 = (f32[2,384,3072]{2,1,0:T(8,128)}, f32[2,384,3072]{2,1,0:T(8,128)}, u32[]{:S(2)}, u32[]{:S(2)}) collective-permute-start(f32[2,384,3072]{2,1,0:T(8,128)} %refs_1_.1), channel_id=1, source_target_pairs={{0,8},{1,9},{2,10},{3,11},{4,12},{5,13},{6,14},{7,15},{8,0},{9,1},... | collective-permute-start | bytes 28311560 | tf_op jit(solution)/shard_map/ppermute | solution.py:66
  9.3 8.0 %collective-permute-start.3 = (f32[32,384]{1,0:T(8,128)S(1)}, f32[32,384]{1,0:T(8,128)S(1)}, u32[]{:S(2)}, u32[]{:S(2)}) collective-permute-start(f32[32,384]{1,0:T(8,128)S(1)} %select_select_fusion.3), channel_id=1, source_target_pairs={{0,2},{1,3},{2,0},{3,1},{4,6},{5,7},{6,4},{7,5},{8,10},{9,11},{10,... | collective-permute-start | bytes 147464 | tf_op jit(solution)/shard_map/ppermute | solution.py:66
  11.0 6.3 %collective-permute-start.4 = (f32[32,384]{1,0:T(8,128)S(1)}, f32[32,384]{1,0:T(8,128)S(1)}, u32[]{:S(2)}, u32[]{:S(2)}) collective-permute-start(f32[32,384]{1,0:T(8,128)S(1)} %select_select_fusion.3), channel_id=1, source_target_pairs={{0,4},{1,5},{2,6},{3,7},{4,0},{5,1},{6,2},{7,3},{8,12},{9,13},{10,... | collective-permute-start | bytes 147464 | tf_op jit(solution)/shard_map/ppermute | solution.py:66
  13.5 5.9 %collective-permute-start.5 = (f32[32,384]{1,0:T(8,128)S(1)}, f32[32,384]{1,0:T(8,128)S(1)}, u32[]{:S(2)}, u32[]{:S(2)}) collective-permute-start(f32[32,384]{1,0:T(8,128)S(1)} %select_select_fusion.3), channel_id=1, source_target_pairs={{0,6},{1,7},{2,4},{3,5},{4,2},{5,3},{6,0},{7,1},{8,14},{9,15},{10,... | collective-permute-start | bytes 147464 | tf_op jit(solution)/shard_map/ppermute | solution.py:66
  13.8 51.3 %collective-permute-start.16 = (f32[128,384]{1,0:T(8,128)S(1)}, f32[128,384]{1,0:T(8,128)S(1)}, u32[]{:S(2)}, u32[]{:S(2)}) collective-permute-start(f32[128,384]{1,0:T(8,128)S(1)} %get-tuple-element.118), channel_id=1, source_target_pairs={{0,8},{1,9},{2,10},{3,11},{4,12},{5,13},{6,14},{7,15},{8,0},{9,1},... | collective-permute-start | bytes 589832 | tf_op jit(solution)/shard_map/ppermute | solution.py:66
  22.5 5.7 %collective-permute-start.6 = (f32[32,1536]{1,0:T(8,128)S(1)}, f32[32,1536]{1,0:T(8,128)S(1)}, u32[]{:S(2)}, u32[]{:S(2)}) collective-permute-start(f32[32,1536]{1,0:T(8,128)S(1)} %pad_maximum_fusion.9), channel_id=1, source_target_pairs={{0,1},{1,0},{2,3},{3,2},{4,5},{5,4},{6,7},{7,6},{8,9},{9,8},{10,11... | collective-permute-start | bytes 589832 | tf_op jit(solution)/shard_map/ppermute | solution.py:66
  29.4 6.5 %collective-permute-start.8 = (f32[32,384]{1,0:T(8,128)S(1)}, f32[32,384]{1,0:T(8,128)S(1)}, u32[]{:S(2)}, u32[]{:S(2)}) collective-permute-start(f32[32,384]{1,0:T(8,128)S(1)} %field.7), channel_id=1, source_target_pairs={{0,4},{1,5},{2,6},{3,7},{4,0},{5,1},{6,2},{7,3},{8,12},{9,13},{10,... | collective-permute-start | bytes 147464 | tf_op jit(solution)/shard_map/ppermute | solution.py:66
  32.9 5.9 %collective-permute-start.9 = (f32[32,384]{1,0:T(8,128)S(1)}, f32[32,384]{1,0:T(8,128)S(1)}, u32[]{:S(2)}, u32[]{:S(2)}) collective-permute-start(f32[32,384]{1,0:T(8,128)S(1)} %field.7), channel_id=1, source_target_pairs={{0,6},{1,7},{2,4},{3,5},{4,2},{5,3},{6,0},{7,1},{8,14},{9,15},{10,... | collective-permute-start | bytes 147464 | tf_op jit(solution)/shard_map/ppermute | solution.py:66
  33.7 31.4 %collective-permute-start.17 = (f32[128,384]{1,0:T(8,128)S(1)}, f32[128,384]{1,0:T(8,128)S(1)}, u32[]{:S(2)}, u32[]{:S(2)}) collective-permute-start(f32[128,384]{1,0:T(8,128)S(1)} %get-tuple-element.118), channel_id=1, source_target_pairs={{0,24},{1,25},{2,26},{3,27},{4,28},{5,29},{6,30},{7,31},{8,16},{9,... | collective-permute-start | bytes 589832 | tf_op jit(solution)/shard_map/ppermute | solution.py:66
  35.9 7.5 %collective-permute-start.14 = (f32[64,384]{1,0:T(8,128)S(1)}, f32[64,384]{1,0:T(8,128)S(1)}, u32[]{:S(2)}, u32[]{:S(2)}) collective-permute-start(f32[64,384]{1,0:T(8,128)S(1)} %pad_maximum_fusion.15), channel_id=1, source_target_pairs={{0,8},{1,9},{2,10},{3,11},{4,12},{5,13},{6,14},{7,15},{8,0},{9,1},... | collective-permute-start | bytes 294920 | tf_op jit(solution)/shard_map/ppermute | solution.py:66
  41.9 8.3 %collective-permute-start.11 = (f32[32,1536]{1,0:T(8,128)S(1)}, f32[32,1536]{1,0:T(8,128)S(1)}, u32[]{:S(2)}, u32[]{:S(2)}) collective-permute-start(f32[32,1536]{1,0:T(8,128)S(1)} %pad_maximum_fusion.10), channel_id=1, source_target_pairs={{0,1},{1,0},{2,3},{3,2},{4,5},{5,4},{6,7},{7,6},{8,9},{9,8},{10,11... | collective-permute-start | bytes 589832 | tf_op jit(solution)/shard_map/ppermute | solution.py:66
  49.1 6.6 %collective-permute-start.12 = (f32[32,1536]{1,0:T(8,128)S(1)}, f32[32,1536]{1,0:T(8,128)S(1)}, u32[]{:S(2)}, u32[]{:S(2)}) collective-permute-start(f32[32,1536]{1,0:T(8,128)S(1)} %pad_maximum_fusion.10), channel_id=1, source_target_pairs={{0,17},{1,16},{2,19},{3,18},{4,21},{5,20},{6,23},{7,22},{8,25},{9,... | collective-permute-start | bytes 589832 | tf_op jit(solution)/shard_map/ppermute | solution.py:66
  58.8 13.6 %collective-permute-start.21 = (f32[64,1536]{1,0:T(8,128)S(1)}, f32[64,1536]{1,0:T(8,128)S(1)}, u32[]{:S(2)}, u32[]{:S(2)}) collective-permute-start(f32[64,1536]{1,0:T(8,128)S(1)} %pad_maximum_fusion.4.near_ref), channel_id=1, source_target_pairs={{0,8},{1,9},{2,10},{3,11},{4,12},{5,13},{6,14},{7,15},{8,0},{9,1},... | collective-permute-start | bytes 1179656 | tf_op jit(solution)/shard_map/ppermute | solution.py:66
  58.9 13.6 %collective-permute-start.22 = (f32[64,1536]{1,0:T(8,128)S(1)}, f32[64,1536]{1,0:T(8,128)S(1)}, u32[]{:S(2)}, u32[]{:S(2)}) collective-permute-start(f32[64,1536]{1,0:T(8,128)S(1)} %pad_maximum_fusion.5.far_ref), channel_id=1, source_target_pairs={{0,8},{1,9},{2,10},{3,11},{4,12},{5,13},{6,14},{7,15},{8,0},{9,1},... | collective-permute-start | bytes 1179656 | tf_op jit(solution)/shard_map/ppermute | solution.py:66
  66.5 5.9 %collective-permute-start.20 = (f32[32,384]{1,0:T(8,128)S(1)}, f32[32,384]{1,0:T(8,128)S(1)}, u32[]{:S(2)}, u32[]{:S(2)}) collective-permute-start(f32[32,384]{1,0:T(8,128)S(1)} %broadcast_select_fusion.13), channel_id=1, source_target_pairs={{0,6},{1,7},{2,4},{3,5},{4,2},{5,3},{6,0},{7,1},{8,14},{9,15},{10,... | collective-permute-start | bytes 147464 | tf_op jit(solution)/shard_map/ppermute | solution.py:66
  75.0 32.3 %collective-permute-start.32 = (f32[128,384]{1,0:T(8,128)S(1)}, f32[128,384]{1,0:T(8,128)S(1)}, u32[]{:S(2)}, u32[]{:S(2)}) collective-permute-start(f32[128,384]{1,0:T(8,128)S(1)} %field.8), channel_id=1, source_target_pairs={{0,8},{1,9},{2,10},{3,11},{4,12},{5,13},{6,14},{7,15},{8,0},{9,1},... | collective-permute-start | bytes 589832 | tf_op jit(solution)/shard_map/ppermute | solution.py:66
  75.1 32.3 %collective-permute-start.33 = (f32[128,384]{1,0:T(8,128)S(1)}, f32[128,384]{1,0:T(8,128)S(1)}, u32[]{:S(2)}, u32[]{:S(2)}) collective-permute-start(f32[128,384]{1,0:T(8,128)S(1)} %field.8), channel_id=1, source_target_pairs={{0,24},{1,25},{2,26},{3,27},{4,28},{5,29},{6,30},{7,31},{8,16},{9,... | collective-permute-start | bytes 589832 | tf_op jit(solution)/shard_map/ppermute | solution.py:66
  84.6 5.9 %collective-permute-start.26 = (f32[32,384]{1,0:T(8,128)S(1)}, f32[32,384]{1,0:T(8,128)S(1)}, u32[]{:S(2)}, u32[]{:S(2)}) collective-permute-start(f32[32,384]{1,0:T(8,128)S(1)} %field.10), channel_id=1, source_target_pairs={{0,6},{1,7},{2,4},{3,5},{4,2},{5,3},{6,0},{7,1},{8,14},{9,15},{10,... | collective-permute-start | bytes 147464 | tf_op jit(solution)/shard_map/ppermute | solution.py:66
  85.5 7.7 %collective-permute-start.30 = (f32[64,384]{1,0:T(8,128)S(1)}, f32[64,384]{1,0:T(8,128)S(1)}, u32[]{:S(2)}, u32[]{:S(2)}) collective-permute-start(f32[64,384]{1,0:T(8,128)S(1)} %pad_maximum_fusion.16), channel_id=1, source_target_pairs={{0,8},{1,9},{2,10},{3,11},{4,12},{5,13},{6,14},{7,15},{8,0},{9,1},... | collective-permute-start | bytes 294920 | tf_op jit(solution)/shard_map/ppermute | solution.py:66
  90.5 10.5 %collective-permute-start.28 = (f32[32,1536]{1,0:T(8,128)S(1)}, f32[32,1536]{1,0:T(8,128)S(1)}, u32[]{:S(2)}, u32[]{:S(2)}) collective-permute-start(f32[32,1536]{1,0:T(8,128)S(1)} %pad_maximum_fusion.12), channel_id=1, source_target_pairs={{0,1},{1,0},{2,3},{3,2},{4,5},{5,4},{6,7},{7,6},{8,9},{9,8},{10,11... | collective-permute-start | bytes 589832 | tf_op jit(solution)/shard_map/ppermute | solution.py:66
  91.1 9.9 %collective-permute-start.29 = (f32[32,1536]{1,0:T(8,128)S(1)}, f32[32,1536]{1,0:T(8,128)S(1)}, u32[]{:S(2)}, u32[]{:S(2)}) collective-permute-start(f32[32,1536]{1,0:T(8,128)S(1)} %pad_maximum_fusion.12), channel_id=1, source_target_pairs={{0,17},{1,16},{2,19},{3,18},{4,21},{5,20},{6,23},{7,22},{8,25},{9,... | collective-permute-start | bytes 589832 | tf_op jit(solution)/shard_map/ppermute | solution.py:66
  93.1 7.8 %collective-permute-start.27 = (f32[32,1536]{1,0:T(8,128)S(1)}, f32[32,1536]{1,0:T(8,128)S(1)}, u32[]{:S(2)}, u32[]{:S(2)}) collective-permute-start(f32[32,1536]{1,0:T(8,128)S(1)} %pad_maximum_fusion.12), channel_id=1, source_target_pairs={{0,16},{1,17},{2,18},{3,19},{4,20},{5,21},{6,22},{7,23},{8,24},{9,... | collective-permute-start | bytes 589832 | tf_op jit(solution)/shard_map/ppermute | solution.py:66
  101.1 14.0 %collective-permute-start.37 = (f32[64,1536]{1,0:T(8,128)S(1)}, f32[64,1536]{1,0:T(8,128)S(1)}, u32[]{:S(2)}, u32[]{:S(2)}) collective-permute-start(f32[64,1536]{1,0:T(8,128)S(1)} %pad_maximum_fusion.6.near_ref), channel_id=1, source_target_pairs={{0,8},{1,9},{2,10},{3,11},{4,12},{5,13},{6,14},{7,15},{8,0},{9,1},... | collective-permute-start | bytes 1179656 | tf_op jit(solution)/shard_map/ppermute | solution.py:66
  101.2 14.0 %collective-permute-start.38 = (f32[64,1536]{1,0:T(8,128)S(1)}, f32[64,1536]{1,0:T(8,128)S(1)}, u32[]{:S(2)}, u32[]{:S(2)}) collective-permute-start(f32[64,1536]{1,0:T(8,128)S(1)} %pad_maximum_fusion.7.far_ref), channel_id=1, source_target_pairs={{0,8},{1,9},{2,10},{3,11},{4,12},{5,13},{6,14},{7,15},{8,0},{9,1},... | collective-permute-start | bytes 1179656 | tf_op jit(solution)/shard_map/ppermute | solution.py:66
  109.2 5.9 %collective-permute-start.36 = (f32[32,384]{1,0:T(8,128)S(1)}, f32[32,384]{1,0:T(8,128)S(1)}, u32[]{:S(2)}, u32[]{:S(2)}) collective-permute-start(f32[32,384]{1,0:T(8,128)S(1)} %broadcast_select_fusion.12), channel_id=1, source_target_pairs={{0,6},{1,7},{2,4},{3,5},{4,2},{5,3},{6,0},{7,1},{8,14},{9,15},{10,... | collective-permute-start | bytes 147464 | tf_op jit(solution)/shard_map/ppermute | solution.py:66
  126.9 5.9 %collective-permute-start.42 = (f32[32,384]{1,0:T(8,128)S(1)}, f32[32,384]{1,0:T(8,128)S(1)}, u32[]{:S(2)}, u32[]{:S(2)}) collective-permute-start(f32[32,384]{1,0:T(8,128)S(1)} %field.13), channel_id=1, source_target_pairs={{0,6},{1,7},{2,4},{3,5},{4,2},{5,3},{6,0},{7,1},{8,14},{9,15},{10,... | collective-permute-start | bytes 147464 | tf_op jit(solution)/shard_map/ppermute | solution.py:66
  128.1 5.7 %collective-permute-start.48 = (f32[128,384]{1,0:T(8,128)S(1)}, f32[128,384]{1,0:T(8,128)S(1)}, u32[]{:S(2)}, u32[]{:S(2)}) collective-permute-start(f32[128,384]{1,0:T(8,128)S(1)} %field.11), channel_id=1, source_target_pairs={{0,8},{1,9},{2,10},{3,11},{4,12},{5,13},{6,14},{7,15},{8,0},{9,1},... | collective-permute-start | bytes 589832 | tf_op jit(solution)/shard_map/ppermute | solution.py:66
  128.1 6.5 %collective-permute-start.49 = (f32[128,384]{1,0:T(8,128)S(1)}, f32[128,384]{1,0:T(8,128)S(1)}, u32[]{:S(2)}, u32[]{:S(2)}) collective-permute-start(f32[128,384]{1,0:T(8,128)S(1)} %field.11), channel_id=1, source_target_pairs={{0,24},{1,25},{2,26},{3,27},{4,28},{5,29},{6,30},{7,31},{8,16},{9,... | collective-permute-start | bytes 589832 | tf_op jit(solution)/shard_map/ppermute | solution.py:66
  132.8 6.7 %collective-permute-start.43 = (f32[32,1536]{1,0:T(8,128)S(1)}, f32[32,1536]{1,0:T(8,128)S(1)}, u32[]{:S(2)}, u32[]{:S(2)}) collective-permute-start(f32[32,1536]{1,0:T(8,128)S(1)} %pad_maximum_fusion.14), channel_id=1, source_target_pairs={{0,16},{1,17},{2,18},{3,19},{4,20},{5,21},{6,22},{7,23},{8,24},{9,... | collective-permute-start | bytes 589832 | tf_op jit(solution)/shard_map/ppermute | solution.py:66
  134.6 7.6 %collective-permute-start.44 = (f32[32,1536]{1,0:T(8,128)S(1)}, f32[32,1536]{1,0:T(8,128)S(1)}, u32[]{:S(2)}, u32[]{:S(2)}) collective-permute-start(f32[32,1536]{1,0:T(8,128)S(1)} %pad_maximum_fusion.14), channel_id=1, source_target_pairs={{0,1},{1,0},{2,3},{3,2},{4,5},{5,4},{6,7},{7,6},{8,9},{9,8},{10,11... | collective-permute-start | bytes 589832 | tf_op jit(solution)/shard_map/ppermute | solution.py:66
  135.7 11.2 %collective-permute-start.45 = (f32[32,1536]{1,0:T(8,128)S(1)}, f32[32,1536]{1,0:T(8,128)S(1)}, u32[]{:S(2)}, u32[]{:S(2)}) collective-permute-start(f32[32,1536]{1,0:T(8,128)S(1)} %pad_maximum_fusion.14), channel_id=1, source_target_pairs={{0,17},{1,16},{2,19},{3,18},{4,21},{5,20},{6,23},{7,22},{8,25},{9,... | collective-permute-start | bytes 589832 | tf_op jit(solution)/shard_map/ppermute | solution.py:66
  139.6 7.6 %collective-permute-start.46 = (f32[64,1536]{1,0:T(8,128)S(1)}, f32[64,1536]{1,0:T(8,128)S(1)}, u32[]{:S(2)}, u32[]{:S(2)}) collective-permute-start(f32[64,1536]{1,0:T(8,128)S(1)} %pad_maximum_fusion.8), channel_id=1, source_target_pairs={{0,8},{1,9},{2,10},{3,11},{4,12},{5,13},{6,14},{7,15},{8,0},{9,1},... | collective-permute-start | bytes 1179656 | tf_op jit(solution)/shard_map/ppermute | solution.py:66
  (21 other events, 110.2 us)

commit v4 on v3

--- a/solution.py
+++ b/solution.py
@@ -225,42 +225,51 @@
     )(high, low, current, base)
 
 
-def lead_kernel(high_ref, low_ref, near_ref, far_ref, rest_ref, mine_ref, theirs_ref):
-    v = jnp.concatenate([near_ref[...], far_ref[...]], 1)
-    rhs = rest_ref[...] - times(*split_here(v), high_ref, low_ref).T
-    n = mine_ref.shape[0]
-    mine_ref[...] = rhs[:n]
-    theirs_ref[...] = rhs[n:]
-
-
-def lead(op, near, far, rest):
+def lead_kernel(columns, high_ref, low_ref, v_ref, rest_ref, *out_refs):
+    high_ref, low_ref = high_ref.at[:, columns], low_ref.at[:, columns]
+    rhs = rest_ref[...] - times(*split_here(v_ref[...]), high_ref, low_ref).T
+    if len(out_refs) == 1:
+        out_refs[0][...] = rhs
+    else:
+        n = out_refs[0].shape[0]
+        out_refs[0][...] = rhs[:n]
+        out_refs[1][...] = rhs[n:]
+
+
+def lead(op, columns, current, rest, parts):
     high, low = op
-    n = near.shape[0]
-    shape = jax.ShapeDtypeStruct((n // 2, high.shape[0]), jnp.float32)
-    return pl.pallas_call(
-        lead_kernel,
-        out_shape=(shape, shape),
-        in_specs=[VMEM] * 5,
-        out_specs=(VMEM, VMEM),
-        compiler_params=pltpu.CompilerParams(vmem_limit_bytes=8 << 20),
-        cost_estimate=costs(*high.shape, n),
+    rows, n = high.shape[0], current.shape[0]
+    shape = jax.ShapeDtypeStruct((n // parts, rows), jnp.float32)
+    return pl.pallas_call(
+        functools.partial(lead_kernel, columns),
+        out_shape=(shape,) * parts,
+        in_specs=[VMEM] * 4,
+        out_specs=(VMEM,) * parts,
+        compiler_params=pltpu.CompilerParams(vmem_limit_bytes=8 << 20),
+        cost_estimate=costs(rows, current.shape[1], n),
         name="lead",
-    )(high, low, near, far, rest)
-
-
-def last_kernel(h0_ref, l0_ref, h1_ref, l1_ref, v_ref, b0_ref, b1_ref, current_ref, out_ref):
+    )(high, low, current, rest)
+
+
+def last_near_kernel(columns, h0_ref, l0_ref, h1_ref, l1_ref, v_ref, b0_ref, b1_ref, current_ref, out_ref):
     rows = current_ref.shape[0]
     vh, vl = split_here(v_ref[...])
     current_ref[...] = v_ref[:, :rows].T
-    out_ref[0] = b0_ref[...].T + times(vh, vl, h0_ref, l0_ref)
-    out_ref[1] = b1_ref[...].T + times(vh, vl, h1_ref, l1_ref)
-
-
-def last(op0, op1, current, base0, base1):
-    rows, cols = op0[0].shape
-    n = current.shape[0]
-    return pl.pallas_call(
-        last_kernel,
+    sides = (h0_ref, l0_ref, b0_ref), (h1_ref, l1_ref, b1_ref)
+    for i, (h_ref, l_ref, b_ref) in enumerate(sides):
+        out_ref[i] = b_ref[...].T + times(vh, vl, h_ref.at[:, columns], l_ref.at[:, columns])
+
+
+def last_far_kernel(columns, h0_ref, l0_ref, h1_ref, l1_ref, v_ref, base_ref, out_ref):
+    vh, vl = split_here(v_ref[...])
+    for i, (h_ref, l_ref) in enumerate(((h0_ref, l0_ref), (h1_ref, l1_ref))):
+        out_ref[i] = base_ref[i] + times(vh, vl, h_ref.at[:, columns], l_ref.at[:, columns])
+
+
+def last_near(op0, op1, columns, current, base0, base1):
+    rows, n = op0[0].shape[0], current.shape[0]
+    return pl.pallas_call(
+        functools.partial(last_near_kernel, columns),
         out_shape=(
             jax.ShapeDtypeStruct((rows, n), jnp.float32),
             jax.ShapeDtypeStruct((2, rows, n), jnp.float32),
@@ -268,9 +277,22 @@
         in_specs=[VMEM] * 7,
         out_specs=(VMEM, VMEM),
         compiler_params=pltpu.CompilerParams(vmem_limit_bytes=8 << 20),
-        cost_estimate=costs(2 * rows, cols, n),
-        name="last",
+        cost_estimate=costs(2 * rows, current.shape[1], n),
+        name="last_near",
     )(*op0, *op1, current, base0, base1)
+
+
+def last_far(op0, op1, columns, current, base):
+    rows, n = op0[0].shape[0], current.shape[0]
+    return pl.pallas_call(
+        functools.partial(last_far_kernel, columns),
+        out_shape=jax.ShapeDtypeStruct((2, rows, n), jnp.float32),
+        in_specs=[VMEM] * 6,
+        out_specs=VMEM,
+        compiler_params=pltpu.CompilerParams(vmem_limit_bytes=8 << 20),
+        cost_estimate=costs(2 * rows, current.shape[1], n),
+        name="last_far",
+    )(*op0, *op1, current, base)
 
 
 def quad_body(lag_ops, inverse, history, loads):
@@ -285,6 +307,7 @@
     cut = len(near) * height
     order = r ^ jnp.array(steps, jnp.int32)
 
+    near_columns, far_columns = pl.ds(0, cut), pl.ds(cut, cut)
     tie = lax.optimization_barrier
 
     def line(v):
@@ -304,9 +327,8 @@
         far = swap(a, 0, 1)
         return jnp.concatenate([a, near_y], 0), jnp.concatenate([far, far_y], 0)
 
-    def full(near_, far_):
-        v = jnp.concatenate([near_, far_], 1)
-        w = jnp.concatenate([swap(near_, 1, 0), swap(far_, 1, 0)], 1)
+    def full(v):
+        w = swap(v, 1, 0)
         chunks = [v[:width], w[:width], v[width:], w[width:]]
         even = [jnp.where(first_core, chunks[j], chunks[j ^ 1]) for j in range(4)]
         return jnp.concatenate(
@@ -346,7 +368,7 @@
             b = swap(a, 0, 1)
             b, acc1, given, own1 = tie((b, acc1, given, own1))
         else:
-            current = full(near_, far_)
+            current = jnp.concatenate([full(near_), full(far_)], 1)
             rhs, received = tie((rhs, received))
             below = choose(received)
             new0 = field(own0, current, acc1)
@@ -367,13 +389,17 @@
             own0 = split_blocks(keep(lag_ops), order, 0)
         near_, far_ = exchange(a)
         if step == 0:
-            near_, far_, own0, first = tie((near_, far_, own0, first))
+            near_, own0, first = tie((near_, own0, first))
         if step < STEPS - 1:
-            near_, far_, rest = tie((near_, far_, rest))
-            mine, theirs = lead(first, near_, far_, rest)
+            near_, rest = tie((near_, rest))
+            (rest,) = lead(first, near_columns, near_, rest, 1)
+            far_, rest = tie((far_, rest))
+            mine, theirs = lead(first, far_columns, far_, rest, 2)
             rhs = jnp.where(first_plane, mine, swap(theirs, 2, 0))
-    current = full(near_, far_)
-    return last(own0, own1, current, acc1, choose(received))
+    current = full(near_)
+    current, future = last_near(own0, own1, near_columns, current, acc1, choose(received))
+    far_ = full(far_)
+    return current, last_far(own0, own1, far_columns, far_, future)
 
 
 def solution(mesh):

time: 153 us -> 148 us (0.967)
  waiting for transfers between devices: 66.8 us -> 58.6 us
  starting transfers between devices: 50 us -> 52.4 us
    ppermute x50, waiting for transfers between devices: 66.8 us -> 58.6 us  [swap(): return lax.ppermute(array, AXES, pairs)]
    ppermute x50, starting transfers between devices: 50 us -> 52.4 us  [swap(): return lax.ppermute(array, AXES, pairs)]
    pallas_call x3 -> x6, Pallas kernels: 6.45 us -> 7.72 us  [the longest x4 3.56 us: lead(): pl.pallas_call(functools.partial(lead_kernel, columns), out_shape=(shape,...]
  transfers between devices with their start and end apart: 50 -> 50, of which waited for: 25 -> 30; matrix products, arithmetic and copies ran while one was open for 3% -> 3% of each run, Pallas kernels for 13% -> 11%
where the time goes in v4:
time: 148 us; the launch traced here: 147 us
  waiting for transfers between devices  58.6 us (40%)
  starting transfers between devices  52.4 us (35%)
  Pallas kernels  30.3 us (20%)
  matrix products  2.98 us (2%)
    ppermute x50, waiting for transfers between devices, swap(): return lax.ppermute(array, AXES, pairs)  58.6 us
    ppermute x50, starting transfers between devices, swap(): return lax.ppermute(array, AXES, pairs)  52.4 us
    pallas_call x4, Pallas kernels, split_blocks(): pl.pallas_call(functools.partial(split_kernel, lag, pick is not None), ou...  12.2 us
    pallas_call x7, Pallas kernels, field(): pl.pallas_call(field_kernel, out_shape=jax.ShapeDtypeStruct((n, high.shap...  8.87 us
    pallas_call x4, Pallas kernels, lead(): pl.pallas_call(functools.partial(lead_kernel, columns), out_shape=(shape,...  3.56 us
    dot_general x6, matrix products, contract(): lax.dot_general(a, b, (((1,), (1,)), ((), ())), preferred_element_type=jn...  2.98 us
  transfers between devices with their start and end apart: 50, of which 30 were waited for; matrix products, arithmetic and copies ran while one was open for 3% of the time, Pallas kernels for 11%

profile of v4, /device:TPU:0, one launch (start us, length us, event | category | flops | bytes accessed | tf_op | source)
XLA Modules:
  0.0 147.3 jit_solution(16034617987219758192)
XLA Ops:
  2.5 2.6 %collective-permute-start.1 = (f32[32,384]{1,0:T(8,128)S(1)}, f32[32,384]{1,0:T(8,128)S(1)}, u32[]{:S(2)}, u32[]{:S(2)}) collective-permute-start(f32[32,384]{1,0:T(8,128)S(1)} %get-tuple-element.198), channel_id=1, source_target_pairs={{0,16},{1,17},{2,18},{3,19},{4,20},{5,21},{6,22},{7,23},{8,24},{9,... | collective-permute-start | bytes 147464 | tf_op jit(solution)/shard_map/ppermute | solution.py:66
  5.2 2.3 %collective-permute-done.1 = f32[32,384]{1,0:T(8,128)S(1)} collective-permute-done((f32[32,384]{1,0:T(8,128)S(1)}, f32[32,384]{1,0:T(8,128)S(1)}, u32[]{:S(2)}, u32[]{:S(2)}) %collective-permute-start.1) | collective-permute-done | bytes 49184 | tf_op jit(solution)/shard_map/ppermute | solution.py:66
  11.0 2.6 %collective-permute-start.4 = (f32[32,384]{1,0:T(8,128)S(1)}, f32[32,384]{1,0:T(8,128)S(1)}, u32[]{:S(2)}, u32[]{:S(2)}) collective-permute-start(f32[32,384]{1,0:T(8,128)S(1)} %select_select_fusion.3), channel_id=1, source_target_pairs={{0,4},{1,5},{2,6},{3,7},{4,0},{5,1},{6,2},{7,3},{8,12},{9,13},{10,... | collective-permute-start | bytes 147464 | tf_op jit(solution)/shard_map/ppermute | solution.py:66
  13.8 3.1 %split_blocks.4 = (bf16[384,3072]{1,0:T(8,128)(2,1)S(1)}, bf16[384,3072]{1,0:T(8,128)(2,1)S(1)}) custom-call(s32[8]{0:T(128)S(1)} %broadcast_xor_fusion.order_ref, f32[384,3072]{1,0:T(8,128)} %refs_0_.3), custom_call_target="tpu_custom_call" | custom-call | bytes 9437184 | tf_op jit(solution)/shard_map/split_blocks/pallas_call | solution.py:181
  17.3 2.1 %collective-permute-done.5 = f32[32,384]{1,0:T(8,128)S(1)} collective-permute-done((f32[32,384]{1,0:T(8,128)S(1)}, f32[32,384]{1,0:T(8,128)S(1)}, u32[]{:S(2)}, u32[]{:S(2)}) %collective-permute-start.5) | collective-permute-done | bytes 49184 | tf_op jit(solution)/shard_map/ppermute | solution.py:66
  19.5 3.1 %split_blocks.5 = (bf16[384,3072]{1,0:T(8,128)(2,1)S(1)}, bf16[384,3072]{1,0:T(8,128)(2,1)S(1)}) custom-call(s32[8]{0:T(128)S(1)} %broadcast_xor_fusion.order_ref, f32[2,384,3072]{2,1,0:T(8,128)} %refs_1_.1), custom_call_target="tpu_custom_call" | custom-call | bytes 9437184 | tf_op jit(solution)/shard_map/split_blocks/pallas_call | solution.py:181
  25.1 3.1 %collective-permute-done.6.v_ref = f32[32,1536]{1,0:T(8,128)S(1)} collective-permute-done((f32[32,1536]{1,0:T(8,128)S(1)}, f32[32,1536]{1,0:T(8,128)S(1)}, u32[]{:S(2)}, u32[]{:S(2)}) %collective-permute-start.6) | collective-permute-done | bytes 196640 | tf_op jit(solution)/shard_map/ppermute | solution.py:66
  29.2 2.7 %collective-permute-start.8 = (f32[32,384]{1,0:T(8,128)S(1)}, f32[32,384]{1,0:T(8,128)S(1)}, u32[]{:S(2)}, u32[]{:S(2)}) collective-permute-start(f32[32,384]{1,0:T(8,128)S(1)} %field.7), channel_id=1, source_target_pairs={{0,4},{1,5},{2,6},{3,7},{4,0},{5,1},{6,2},{7,3},{8,12},{9,13},{10,... | collective-permute-start | bytes 147464 | tf_op jit(solution)/shard_map/ppermute | solution.py:66
  34.2 3.5 %collective-permute-done.9 = f32[32,384]{1,0:T(8,128)S(1)} collective-permute-done((f32[32,384]{1,0:T(8,128)S(1)}, f32[32,384]{1,0:T(8,128)S(1)}, u32[]{:S(2)}, u32[]{:S(2)}) %collective-permute-start.9) | collective-permute-done | bytes 49184 | tf_op jit(solution)/shard_map/ppermute | solution.py:66
  41.4 3.1 %split_blocks.6 = (bf16[384,3072]{1,0:T(8,128)(2,1)S(1)}, bf16[384,3072]{1,0:T(8,128)(2,1)S(1)}) custom-call(s32[8]{0:T(128)S(1)} %broadcast_xor_fusion.order_ref, f32[2,384,3072]{2,1,0:T(8,128)} %refs_1_.1), custom_call_target="tpu_custom_call" | custom-call | bytes 9437184 | tf_op jit(solution)/shard_map/split_blocks/pallas_call | solution.py:181
  44.9 2.2 %collective-permute-done.13 = f32[32,1536]{1,0:T(8,128)S(1)} collective-permute-done((f32[32,1536]{1,0:T(8,128)S(1)}, f32[32,1536]{1,0:T(8,128)S(1)}, u32[]{:S(2)}, u32[]{:S(2)}) %collective-permute-start.13) | collective-permute-done | bytes 196640 | tf_op jit(solution)/shard_map/ppermute | solution.py:66
  47.1 3.1 %split_blocks.7 = (bf16[384,3072]{1,0:T(8,128)(2,1)S(1)}, bf16[384,3072]{1,0:T(8,128)(2,1)S(1)}) custom-call(s32[8]{0:T(128)S(1)} %broadcast_xor_fusion.order_ref, s32[1]{0:T(128)} %bitcast.refs_0_, f32[2,384,3072]{2,1,0:T(8,128)} %refs_1_.1, f32[2,384,3072]{2,1,0:T(8,128)} %collective-permute-done.11.refs_2_), custom_call_target="tpu_custom_call" | custom-call | bytes 9437184 | tf_op jit(solution)/shard_map/split_blocks/pallas_call | solution.py:181
  56.4 3.5 %collective-permute-done.17 = f32[128,384]{1,0:T(8,128)S(1)} collective-permute-done((f32[128,384]{1,0:T(8,128)S(1)}, f32[128,384]{1,0:T(8,128)S(1)}, u32[]{:S(2)}, u32[]{:S(2)}) %collective-permute-start.17) | collective-permute-done | bytes 196640 | tf_op jit(solution)/shard_map/ppermute | solution.py:66
  59.9 2.0 %collective-permute-start.19 = (f32[32,384]{1,0:T(8,128)S(1)}, f32[32,384]{1,0:T(8,128)S(1)}, u32[]{:S(2)}, u32[]{:S(2)}) collective-permute-start(f32[32,384]{1,0:T(8,128)S(1)} %broadcast_select_fusion.25), channel_id=1, source_target_pairs={{0,4},{1,5},{2,6},{3,7},{4,0},{5,1},{6,2},{7,3},{8,12},{9,13},{10,... | collective-permute-start | bytes 147464 | tf_op jit(solution)/shard_map/ppermute | solution.py:66
  61.9 2.3 %collective-permute-start.20 = (f32[32,384]{1,0:T(8,128)S(1)}, f32[32,384]{1,0:T(8,128)S(1)}, u32[]{:S(2)}, u32[]{:S(2)}) collective-permute-start(f32[32,384]{1,0:T(8,128)S(1)} %broadcast_select_fusion.25), channel_id=1, source_target_pairs={{0,6},{1,7},{2,4},{3,5},{4,2},{5,3},{6,0},{7,1},{8,14},{9,15},{10,... | collective-permute-start | bytes 147464 | tf_op jit(solution)/shard_map/ppermute | solution.py:66
  65.8 2.0 %collective-permute-done.20 = f32[32,384]{1,0:T(8,128)S(1)} collective-permute-done((f32[32,384]{1,0:T(8,128)S(1)}, f32[32,384]{1,0:T(8,128)S(1)}, u32[]{:S(2)}, u32[]{:S(2)}) %collective-permute-start.20) | collective-permute-done | bytes 49184 | tf_op jit(solution)/shard_map/ppermute | solution.py:66
  71.8 1.7 %field.9.base_ref = f32[128,384]{1,0:T(8,128)S(1)} custom-call(bf16[384,3072]{1,0:T(8,128)(2,1)S(1)} %get-tuple-element.106.high_ref.h1_ref, bf16[384,3072]{1,0:T(8,128)(2,1)S(1)} %get-tuple-element.107.low_ref.l1_ref, f32[128,3072]{1,0:T(8,128)S(1)} %maximum_maximum_fusion.v_ref, f32[128,384]{1,0:T(8,128)S(1)} %select_select_fusion.2.base_ref), custom_call_target="tpu_custom_call" | custom-call | flops 905969664 | bytes 4718592 | tf_op jit(solution)/shard_map/field/pallas_call | solution.py:217
  77.0 2.3 %collective-permute-start.25 = (f32[32,384]{1,0:T(8,128)S(1)}, f32[32,384]{1,0:T(8,128)S(1)}, u32[]{:S(2)}, u32[]{:S(2)}) collective-permute-start(f32[32,384]{1,0:T(8,128)S(1)} %field.10), channel_id=1, source_target_pairs={{0,4},{1,5},{2,6},{3,7},{4,0},{5,1},{6,2},{7,3},{8,12},{9,13},{10,... | collective-permute-start | bytes 147464 | tf_op jit(solution)/shard_map/ppermute | solution.py:66
  82.0 3.2 %collective-permute-done.26 = f32[32,384]{1,0:T(8,128)S(1)} collective-permute-done((f32[32,384]{1,0:T(8,128)S(1)}, f32[32,384]{1,0:T(8,128)S(1)}, u32[]{:S(2)}, u32[]{:S(2)}) %collective-permute-start.26) | collective-permute-done | bytes 49184 | tf_op jit(solution)/shard_map/ppermute | solution.py:66
  88.8 2.8 %collective-permute-done.29 = f32[32,1536]{1,0:T(8,128)S(1)} collective-permute-done((f32[32,1536]{1,0:T(8,128)S(1)}, f32[32,1536]{1,0:T(8,128)S(1)}, u32[]{:S(2)}, u32[]{:S(2)}) %collective-permute-start.29) | collective-permute-done | bytes 196640 | tf_op jit(solution)/shard_map/ppermute | solution.py:66
  92.5 2.1 %collective-permute-done.28 = f32[32,1536]{1,0:T(8,128)S(1)} collective-permute-done((f32[32,1536]{1,0:T(8,128)S(1)}, f32[32,1536]{1,0:T(8,128)S(1)}, u32[]{:S(2)}, u32[]{:S(2)}) %collective-permute-start.28) | collective-permute-done | bytes 196640 | tf_op jit(solution)/shard_map/ppermute | solution.py:66
  99.9 3.5 %collective-permute-done.33 = f32[128,384]{1,0:T(8,128)S(1)} collective-permute-done((f32[128,384]{1,0:T(8,128)S(1)}, f32[128,384]{1,0:T(8,128)S(1)}, u32[]{:S(2)}, u32[]{:S(2)}) %collective-permute-start.33) | collective-permute-done | bytes 196640 | tf_op jit(solution)/shard_map/ppermute | solution.py:66
  103.4 1.9 %collective-permute-start.35 = (f32[32,384]{1,0:T(8,128)S(1)}, f32[32,384]{1,0:T(8,128)S(1)}, u32[]{:S(2)}, u32[]{:S(2)}) collective-permute-start(f32[32,384]{1,0:T(8,128)S(1)} %broadcast_select_fusion.24), channel_id=1, source_target_pairs={{0,4},{1,5},{2,6},{3,7},{4,0},{5,1},{6,2},{7,3},{8,12},{9,13},{10,... | collective-permute-start | bytes 147464 | tf_op jit(solution)/shard_map/ppermute | solution.py:66
  105.4 2.5 %collective-permute-start.36 = (f32[32,384]{1,0:T(8,128)S(1)}, f32[32,384]{1,0:T(8,128)S(1)}, u32[]{:S(2)}, u32[]{:S(2)}) collective-permute-start(f32[32,384]{1,0:T(8,128)S(1)} %broadcast_select_fusion.24), channel_id=1, source_target_pairs={{0,6},{1,7},{2,4},{3,5},{4,2},{5,3},{6,0},{7,1},{8,14},{9,15},{10,... | collective-permute-start | bytes 147464 | tf_op jit(solution)/shard_map/ppermute | solution.py:66
  109.3 2.0 %collective-permute-done.36 = f32[32,384]{1,0:T(8,128)S(1)} collective-permute-done((f32[32,384]{1,0:T(8,128)S(1)}, f32[32,384]{1,0:T(8,128)S(1)}, u32[]{:S(2)}, u32[]{:S(2)}) %collective-permute-start.36) | collective-permute-done | bytes 49184 | tf_op jit(solution)/shard_map/ppermute | solution.py:66
  117.2 1.8 %collective-permute-done.39.v_ref = f32[32,1536]{1,0:T(8,128)S(1)} collective-permute-done((f32[32,1536]{1,0:T(8,128)S(1)}, f32[32,1536]{1,0:T(8,128)S(1)}, u32[]{:S(2)}, u32[]{:S(2)}) %collective-permute-start.39) | collective-permute-done | bytes 196640 | tf_op jit(solution)/shard_map/ppermute | solution.py:66
  120.5 2.3 %collective-permute-start.41 = (f32[32,384]{1,0:T(8,128)S(1)}, f32[32,384]{1,0:T(8,128)S(1)}, u32[]{:S(2)}, u32[]{:S(2)}) collective-permute-start(f32[32,384]{1,0:T(8,128)S(1)} %field.13), channel_id=1, source_target_pairs={{0,4},{1,5},{2,6},{3,7},{4,0},{5,1},{6,2},{7,3},{8,12},{9,13},{10,... | collective-permute-start | bytes 147464 | tf_op jit(solution)/shard_map/ppermute | solution.py:66
  125.5 3.2 %collective-permute-done.42 = f32[32,384]{1,0:T(8,128)S(1)} collective-permute-done((f32[32,384]{1,0:T(8,128)S(1)}, f32[32,384]{1,0:T(8,128)S(1)}, u32[]{:S(2)}, u32[]{:S(2)}) %collective-permute-start.42) | collective-permute-done | bytes 49184 | tf_op jit(solution)/shard_map/ppermute | solution.py:66
  133.1 3.4 %collective-permute-done.43 = f32[32,1536]{1,0:T(8,128)S(1)} collective-permute-done((f32[32,1536]{1,0:T(8,128)S(1)}, f32[32,1536]{1,0:T(8,128)S(1)}, u32[]{:S(2)}, u32[]{:S(2)}) %collective-permute-start.43) | collective-permute-done | bytes 196640 | tf_op jit(solution)/shard_map/ppermute | solution.py:66
  138.7 3.5 %collective-permute-done.48 = f32[32,1536]{1,0:T(8,128)S(1)} collective-permute-done((f32[32,1536]{1,0:T(8,128)S(1)}, f32[32,1536]{1,0:T(8,128)S(1)}, u32[]{:S(2)}, u32[]{:S(2)}) %collective-permute-start.48) | collective-permute-done | bytes 196640 | tf_op jit(solution)/shard_map/ppermute | solution.py:66
  143.0 2.0 %last_near.1 = (f32[384,128]{1,0:T(8,128)}, f32[2,384,128]{2,1,0:T(8,128)S(1)}) custom-call(bf16[384,3072]{1,0:T(8,128)(2,1)S(1)} %get-tuple-element.104.high_ref.h0_ref, bf16[384,3072]{1,0:T(8,128)(2,1)S(1)} %get-tuple-element.105.low_ref.l0_ref, bf16[384,3072]{1,0:T(8,128)(2,1)S(1)} %get-tuple-element.106.high_ref.h1_ref, ...), custom_call_target="tpu_custom_call" | custom-call | flops 905969664 | bytes 4718592 | tf_op jit(solution)/shard_map/last_near/pallas_call | solution.py:271
  145.2 2.2 %last_far.1 = f32[2,384,128]{2,1,0:T(8,128)} custom-call(bf16[384,3072]{1,0:T(8,128)(2,1)S(1)} %get-tuple-element.104.high_ref.h0_ref, bf16[384,3072]{1,0:T(8,128)(2,1)S(1)} %get-tuple-element.105.low_ref.l0_ref, bf16[384,3072]{1,0:T(8,128)(2,1)S(1)} %get-tuple-element.106.high_ref.h1_ref, bf16[384,3072]{1,0:T(8,128)(2,1)S(1)} %get-tuple-element.107.low_ref.l1_ref, ...), custom_call_target="tpu_custom_call" | custom-call | flops 905969664 | bytes 4718592 | tf_op jit(solution)/shard_map/last_far/pallas_call | solution.py:287
  (141 shorter events, 62.7 us)
Async XLA Ops:
  8.8 38.3 %collective-permute-start.11 = (f32[2,384,3072]{2,1,0:T(8,128)}, f32[2,384,3072]{2,1,0:T(8,128)}, u32[]{:S(2)}, u32[]{:S(2)}) collective-permute-start(f32[2,384,3072]{2,1,0:T(8,128)} %refs_1_.1), channel_id=1, source_target_pairs={{0,8},{1,9},{2,10},{3,11},{4,12},{5,13},{6,14},{7,15},{8,0},{9,1},... | collective-permute-start | bytes 28311560 | tf_op jit(solution)/shard_map/ppermute | solution.py:66
  9.3 8.0 %collective-permute-start.3 = (f32[32,384]{1,0:T(8,128)S(1)}, f32[32,384]{1,0:T(8,128)S(1)}, u32[]{:S(2)}, u32[]{:S(2)}) collective-permute-start(f32[32,384]{1,0:T(8,128)S(1)} %select_select_fusion.3), channel_id=1, source_target_pairs={{0,2},{1,3},{2,0},{3,1},{4,6},{5,7},{6,4},{7,5},{8,10},{9,11},{10,... | collective-permute-start | bytes 147464 | tf_op jit(solution)/shard_map/ppermute | solution.py:66
  11.0 6.3 %collective-permute-start.4 = (f32[32,384]{1,0:T(8,128)S(1)}, f32[32,384]{1,0:T(8,128)S(1)}, u32[]{:S(2)}, u32[]{:S(2)}) collective-permute-start(f32[32,384]{1,0:T(8,128)S(1)} %select_select_fusion.3), channel_id=1, source_target_pairs={{0,4},{1,5},{2,6},{3,7},{4,0},{5,1},{6,2},{7,3},{8,12},{9,13},{10,... | collective-permute-start | bytes 147464 | tf_op jit(solution)/shard_map/ppermute | solution.py:66
  13.5 5.9 %collective-permute-start.5 = (f32[32,384]{1,0:T(8,128)S(1)}, f32[32,384]{1,0:T(8,128)S(1)}, u32[]{:S(2)}, u32[]{:S(2)}) collective-permute-start(f32[32,384]{1,0:T(8,128)S(1)} %select_select_fusion.3), channel_id=1, source_target_pairs={{0,6},{1,7},{2,4},{3,5},{4,2},{5,3},{6,0},{7,1},{8,14},{9,15},{10,... | collective-permute-start | bytes 147464 | tf_op jit(solution)/shard_map/ppermute | solution.py:66
  31.9 5.9 %collective-permute-start.9 = (f32[32,384]{1,0:T(8,128)S(1)}, f32[32,384]{1,0:T(8,128)S(1)}, u32[]{:S(2)}, u32[]{:S(2)}) collective-permute-start(f32[32,384]{1,0:T(8,128)S(1)} %field.7), channel_id=1, source_target_pairs={{0,6},{1,7},{2,4},{3,5},{4,2},{5,3},{6,0},{7,1},{8,14},{9,15},{10,... | collective-permute-start | bytes 147464 | tf_op jit(solution)/shard_map/ppermute | solution.py:66
  33.6 10.8 %collective-permute-start.14 = (f32[64,384]{1,0:T(8,128)S(1)}, f32[64,384]{1,0:T(8,128)S(1)}, u32[]{:S(2)}, u32[]{:S(2)}) collective-permute-start(f32[64,384]{1,0:T(8,128)S(1)} %pad_maximum_fusion.14), channel_id=1, source_target_pairs={{0,8},{1,9},{2,10},{3,11},{4,12},{5,13},{6,14},{7,15},{8,0},{9,1},... | collective-permute-start | bytes 294920 | tf_op jit(solution)/shard_map/ppermute | solution.py:66
  37.8 7.1 %collective-permute-start.10 = (f32[32,1536]{1,0:T(8,128)S(1)}, f32[32,1536]{1,0:T(8,128)S(1)}, u32[]{:S(2)}, u32[]{:S(2)}) collective-permute-start(f32[32,1536]{1,0:T(8,128)S(1)} %pad_maximum_fusion.9), channel_id=1, source_target_pairs={{0,16},{1,17},{2,18},{3,19},{4,20},{5,21},{6,22},{7,23},{8,24},{9,... | collective-permute-start | bytes 589832 | tf_op jit(solution)/shard_map/ppermute | solution.py:66
  38.8 6.2 %collective-permute-start.12 = (f32[32,1536]{1,0:T(8,128)S(1)}, f32[32,1536]{1,0:T(8,128)S(1)}, u32[]{:S(2)}, u32[]{:S(2)}) collective-permute-start(f32[32,1536]{1,0:T(8,128)S(1)} %pad_maximum_fusion.9), channel_id=1, source_target_pairs={{0,1},{1,0},{2,3},{3,2},{4,5},{5,4},{6,7},{7,6},{8,9},{9,8},{10,11... | collective-permute-start | bytes 589832 | tf_op jit(solution)/shard_map/ppermute | solution.py:66
  40.2 6.9 %collective-permute-start.13 = (f32[32,1536]{1,0:T(8,128)S(1)}, f32[32,1536]{1,0:T(8,128)S(1)}, u32[]{:S(2)}, u32[]{:S(2)}) collective-permute-start(f32[32,1536]{1,0:T(8,128)S(1)} %pad_maximum_fusion.9), channel_id=1, source_target_pairs={{0,17},{1,16},{2,19},{3,18},{4,21},{5,20},{6,23},{7,22},{8,25},{9,... | collective-permute-start | bytes 589832 | tf_op jit(solution)/shard_map/ppermute | solution.py:66
  53.0 6.9 %collective-permute-start.17 = (f32[128,384]{1,0:T(8,128)S(1)}, f32[128,384]{1,0:T(8,128)S(1)}, u32[]{:S(2)}, u32[]{:S(2)}) collective-permute-start(f32[128,384]{1,0:T(8,128)S(1)} %get-tuple-element.121), channel_id=1, source_target_pairs={{0,24},{1,25},{2,26},{3,27},{4,28},{5,29},{6,30},{7,31},{8,16},{9,... | collective-permute-start | bytes 589832 | tf_op jit(solution)/shard_map/ppermute | solution.py:66
  54.2 13.6 %collective-permute-start.21 = (f32[64,1536]{1,0:T(8,128)S(1)}, f32[64,1536]{1,0:T(8,128)S(1)}, u32[]{:S(2)}, u32[]{:S(2)}) collective-permute-start(f32[64,1536]{1,0:T(8,128)S(1)} %pad_maximum_fusion.2.v_ref), channel_id=1, source_target_pairs={{0,8},{1,9},{2,10},{3,11},{4,12},{5,13},{6,14},{7,15},{8,0},{9,1},... | collective-permute-start | bytes 1179656 | tf_op jit(solution)/shard_map/ppermute | solution.py:66
  54.2 13.7 %collective-permute-start.22 = (f32[64,1536]{1,0:T(8,128)S(1)}, f32[64,1536]{1,0:T(8,128)S(1)}, u32[]{:S(2)}, u32[]{:S(2)}) collective-permute-start(f32[64,1536]{1,0:T(8,128)S(1)} %pad_maximum_fusion.3.v_ref), channel_id=1, source_target_pairs={{0,8},{1,9},{2,10},{3,11},{4,12},{5,13},{6,14},{7,15},{8,0},{9,1},... | collective-permute-start | bytes 1179656 | tf_op jit(solution)/shard_map/ppermute | solution.py:66
  59.9 5.9 %collective-permute-start.19 = (f32[32,384]{1,0:T(8,128)S(1)}, f32[32,384]{1,0:T(8,128)S(1)}, u32[]{:S(2)}, u32[]{:S(2)}) collective-permute-start(f32[32,384]{1,0:T(8,128)S(1)} %broadcast_select_fusion.25), channel_id=1, source_target_pairs={{0,4},{1,5},{2,6},{3,7},{4,0},{5,1},{6,2},{7,3},{8,12},{9,13},{10,... | collective-permute-start | bytes 147464 | tf_op jit(solution)/shard_map/ppermute | solution.py:66
  61.9 5.9 %collective-permute-start.20 = (f32[32,384]{1,0:T(8,128)S(1)}, f32[32,384]{1,0:T(8,128)S(1)}, u32[]{:S(2)}, u32[]{:S(2)}) collective-permute-start(f32[32,384]{1,0:T(8,128)S(1)} %broadcast_select_fusion.25), channel_id=1, source_target_pairs={{0,6},{1,7},{2,4},{3,5},{4,2},{5,3},{6,0},{7,1},{8,14},{9,15},{10,... | collective-permute-start | bytes 147464 | tf_op jit(solution)/shard_map/ppermute | solution.py:66
  79.3 5.9 %collective-permute-start.26 = (f32[32,384]{1,0:T(8,128)S(1)}, f32[32,384]{1,0:T(8,128)S(1)}, u32[]{:S(2)}, u32[]{:S(2)}) collective-permute-start(f32[32,384]{1,0:T(8,128)S(1)} %field.10), channel_id=1, source_target_pairs={{0,6},{1,7},{2,4},{3,5},{4,2},{5,3},{6,0},{7,1},{8,14},{9,15},{10,... | collective-permute-start | bytes 147464 | tf_op jit(solution)/shard_map/ppermute | solution.py:66
  80.8 7.9 %collective-permute-start.30 = (f32[64,384]{1,0:T(8,128)S(1)}, f32[64,384]{1,0:T(8,128)S(1)}, u32[]{:S(2)}, u32[]{:S(2)}) collective-permute-start(f32[64,384]{1,0:T(8,128)S(1)} %pad_maximum_fusion.15), channel_id=1, source_target_pairs={{0,8},{1,9},{2,10},{3,11},{4,12},{5,13},{6,14},{7,15},{8,0},{9,1},... | collective-permute-start | bytes 294920 | tf_op jit(solution)/shard_map/ppermute | solution.py:66
  85.2 6.4 %collective-permute-start.29 = (f32[32,1536]{1,0:T(8,128)S(1)}, f32[32,1536]{1,0:T(8,128)S(1)}, u32[]{:S(2)}, u32[]{:S(2)}) collective-permute-start(f32[32,1536]{1,0:T(8,128)S(1)} %pad_maximum_fusion.11), channel_id=1, source_target_pairs={{0,16},{1,17},{2,18},{3,19},{4,20},{5,21},{6,22},{7,23},{8,24},{9,... | collective-permute-start | bytes 589832 | tf_op jit(solution)/shard_map/ppermute | solution.py:66
  86.0 6.5 %collective-permute-start.27 = (f32[32,1536]{1,0:T(8,128)S(1)}, f32[32,1536]{1,0:T(8,128)S(1)}, u32[]{:S(2)}, u32[]{:S(2)}) collective-permute-start(f32[32,1536]{1,0:T(8,128)S(1)} %pad_maximum_fusion.11), channel_id=1, source_target_pairs={{0,1},{1,0},{2,3},{3,2},{4,5},{5,4},{6,7},{7,6},{8,9},{9,8},{10,11... | collective-permute-start | bytes 589832 | tf_op jit(solution)/shard_map/ppermute | solution.py:66
  87.5 7.1 %collective-permute-start.28 = (f32[32,1536]{1,0:T(8,128)S(1)}, f32[32,1536]{1,0:T(8,128)S(1)}, u32[]{:S(2)}, u32[]{:S(2)}) collective-permute-start(f32[32,1536]{1,0:T(8,128)S(1)} %pad_maximum_fusion.11), channel_id=1, source_target_pairs={{0,17},{1,16},{2,19},{3,18},{4,21},{5,20},{6,23},{7,22},{8,25},{9,... | collective-permute-start | bytes 589832 | tf_op jit(solution)/shard_map/ppermute | solution.py:66
  96.4 7.0 %collective-permute-start.33 = (f32[128,384]{1,0:T(8,128)S(1)}, f32[128,384]{1,0:T(8,128)S(1)}, u32[]{:S(2)}, u32[]{:S(2)}) collective-permute-start(f32[128,384]{1,0:T(8,128)S(1)} %field.8), channel_id=1, source_target_pairs={{0,24},{1,25},{2,26},{3,27},{4,28},{5,29},{6,30},{7,31},{8,16},{9,... | collective-permute-start | bytes 589832 | tf_op jit(solution)/shard_map/ppermute | solution.py:66
  97.7 13.6 %collective-permute-start.37 = (f32[64,1536]{1,0:T(8,128)S(1)}, f32[64,1536]{1,0:T(8,128)S(1)}, u32[]{:S(2)}, u32[]{:S(2)}) collective-permute-start(f32[64,1536]{1,0:T(8,128)S(1)} %pad_maximum_fusion.5.v_ref), channel_id=1, source_target_pairs={{0,8},{1,9},{2,10},{3,11},{4,12},{5,13},{6,14},{7,15},{8,0},{9,1},... | collective-permute-start | bytes 1179656 | tf_op jit(solution)/shard_map/ppermute | solution.py:66
  97.7 13.7 %collective-permute-start.38 = (f32[64,1536]{1,0:T(8,128)S(1)}, f32[64,1536]{1,0:T(8,128)S(1)}, u32[]{:S(2)}, u32[]{:S(2)}) collective-permute-start(f32[64,1536]{1,0:T(8,128)S(1)} %pad_maximum_fusion.4.v_ref), channel_id=1, source_target_pairs={{0,8},{1,9},{2,10},{3,11},{4,12},{5,13},{6,14},{7,15},{8,0},{9,1},... | collective-permute-start | bytes 1179656 | tf_op jit(solution)/shard_map/ppermute | solution.py:66
  103.4 5.9 %collective-permute-start.35 = (f32[32,384]{1,0:T(8,128)S(1)}, f32[32,384]{1,0:T(8,128)S(1)}, u32[]{:S(2)}, u32[]{:S(2)}) collective-permute-start(f32[32,384]{1,0:T(8,128)S(1)} %broadcast_select_fusion.24), channel_id=1, source_target_pairs={{0,4},{1,5},{2,6},{3,7},{4,0},{5,1},{6,2},{7,3},{8,12},{9,13},{10,... | collective-permute-start | bytes 147464 | tf_op jit(solution)/shard_map/ppermute | solution.py:66
  105.4 5.9 %collective-permute-start.36 = (f32[32,384]{1,0:T(8,128)S(1)}, f32[32,384]{1,0:T(8,128)S(1)}, u32[]{:S(2)}, u32[]{:S(2)}) collective-permute-start(f32[32,384]{1,0:T(8,128)S(1)} %broadcast_select_fusion.24), channel_id=1, source_target_pairs={{0,6},{1,7},{2,4},{3,5},{4,2},{5,3},{6,0},{7,1},{8,14},{9,15},{10,... | collective-permute-start | bytes 147464 | tf_op jit(solution)/shard_map/ppermute | solution.py:66
  113.1 5.8 %collective-permute-start.39 = (f32[32,1536]{1,0:T(8,128)S(1)}, f32[32,1536]{1,0:T(8,128)S(1)}, u32[]{:S(2)}, u32[]{:S(2)}) collective-permute-start(f32[32,1536]{1,0:T(8,128)S(1)} %pad_maximum_fusion.12), channel_id=1, source_target_pairs={{0,1},{1,0},{2,3},{3,2},{4,5},{5,4},{6,7},{7,6},{8,9},{9,8},{10,11... | collective-permute-start | bytes 589832 | tf_op jit(solution)/shard_map/ppermute | solution.py:66
  122.8 5.9 %collective-permute-start.42 = (f32[32,384]{1,0:T(8,128)S(1)}, f32[32,384]{1,0:T(8,128)S(1)}, u32[]{:S(2)}, u32[]{:S(2)}) collective-permute-start(f32[32,384]{1,0:T(8,128)S(1)} %field.13), channel_id=1, source_target_pairs={{0,6},{1,7},{2,4},{3,5},{4,2},{5,3},{6,0},{7,1},{8,14},{9,15},{10,... | collective-permute-start | bytes 147464 | tf_op jit(solution)/shard_map/ppermute | solution.py:66
  128.7 7.7 %collective-permute-start.43 = (f32[32,1536]{1,0:T(8,128)S(1)}, f32[32,1536]{1,0:T(8,128)S(1)}, u32[]{:S(2)}, u32[]{:S(2)}) collective-permute-start(f32[32,1536]{1,0:T(8,128)S(1)} %pad_maximum_fusion.13), channel_id=1, source_target_pairs={{0,16},{1,17},{2,18},{3,19},{4,20},{5,21},{6,22},{7,23},{8,24},{9,... | collective-permute-start | bytes 589832 | tf_op jit(solution)/shard_map/ppermute | solution.py:66
  129.5 7.1 %collective-permute-start.45 = (f32[128,384]{1,0:T(8,128)S(1)}, f32[128,384]{1,0:T(8,128)S(1)}, u32[]{:S(2)}, u32[]{:S(2)}) collective-permute-start(f32[128,384]{1,0:T(8,128)S(1)} %field.11), channel_id=1, source_target_pairs={{0,8},{1,9},{2,10},{3,11},{4,12},{5,13},{6,14},{7,15},{8,0},{9,1},... | collective-permute-start | bytes 589832 | tf_op jit(solution)/shard_map/ppermute | solution.py:66
  129.5 8.4 %collective-permute-start.46 = (f32[128,384]{1,0:T(8,128)S(1)}, f32[128,384]{1,0:T(8,128)S(1)}, u32[]{:S(2)}, u32[]{:S(2)}) collective-permute-start(f32[128,384]{1,0:T(8,128)S(1)} %field.11), channel_id=1, source_target_pairs={{0,24},{1,25},{2,26},{3,27},{4,28},{5,29},{6,30},{7,31},{8,16},{9,... | collective-permute-start | bytes 589832 | tf_op jit(solution)/shard_map/ppermute | solution.py:66
  130.9 7.8 %collective-permute-start.47 = (f32[32,1536]{1,0:T(8,128)S(1)}, f32[32,1536]{1,0:T(8,128)S(1)}, u32[]{:S(2)}, u32[]{:S(2)}) collective-permute-start(f32[32,1536]{1,0:T(8,128)S(1)} %pad_maximum_fusion.13), channel_id=1, source_target_pairs={{0,1},{1,0},{2,3},{3,2},{4,5},{5,4},{6,7},{7,6},{8,9},{9,8},{10,11... | collective-permute-start | bytes 589832 | tf_op jit(solution)/shard_map/ppermute | solution.py:66
  132.5 9.7 %collective-permute-start.48 = (f32[32,1536]{1,0:T(8,128)S(1)}, f32[32,1536]{1,0:T(8,128)S(1)}, u32[]{:S(2)}, u32[]{:S(2)}) collective-permute-start(f32[32,1536]{1,0:T(8,128)S(1)} %pad_maximum_fusion.13), channel_id=1, source_target_pairs={{0,17},{1,16},{2,19},{3,18},{4,21},{5,20},{6,23},{7,22},{8,25},{9,... | collective-permute-start | bytes 589832 | tf_op jit(solution)/shard_map/ppermute | solution.py:66
  136.5 6.4 %collective-permute-start.44 = (f32[64,1536]{1,0:T(8,128)S(1)}, f32[64,1536]{1,0:T(8,128)S(1)}, u32[]{:S(2)}, u32[]{:S(2)}) collective-permute-start(f32[64,1536]{1,0:T(8,128)S(1)} %pad_maximum_fusion.6), channel_id=1, source_target_pairs={{0,8},{1,9},{2,10},{3,11},{4,12},{5,13},{6,14},{7,15},{8,0},{9,1},... | collective-permute-start | bytes 1179656 | tf_op jit(solution)/shard_map/ppermute | solution.py:66
  (21 other events, 105.4 us)
